TPU v7x, 32 devices: a whole 2x2x4 slice. The times are simulated.
32 devices in a mesh: dp: 4 (over x, core), expert: 8 (over z, y).
Axes of the slice: x: 2, y: 2, z: 4, core: 2. Of those that a mesh axis runs over, the one named last changes fastest.
Arguments:
- tokens: bfloat16 [32768, 768], P(('dp', 'expert')), may hold values from -6 to 6
- routing: int32 [32768, 1], P(('dp', 'expert')), may hold values from 0 to 7; in each aligned block of 1024 rows (0 to 1023, 1024 to 2047, ...) at most 256 rows name the same one
- query_weight: bfloat16 [768, 768], replicated, may hold values from -0.3125 to 0.3125
- key_weight: bfloat16 [768, 768], replicated, may hold values from -0.3125 to 0.3125
- value_weight: bfloat16 [768, 768], replicated, may hold values from -0.21875 to 0.21875
- output_weight: bfloat16 [768, 768], replicated, may hold values from -0.625 to 0.625
- first_gain: float32 [768], replicated, may hold values from 0.25 to 1.75
- first_bias: float32 [768], replicated, may hold values from -1.2 to 1.2
- second_gain: float32 [768], replicated, may hold values from 0.25 to 1.75
- second_bias: float32 [768], replicated, may hold values from -1.2 to 1.2
- centroids: float32 [8, 768], replicated, may hold values from -0.18 to 0.18
- expert_up: bfloat16 [8, 768, 3072], P('expert'), may hold values from -0.21875 to 0.21875
- expert_down: bfloat16 [8, 3072, 768], P('expert'), may hold values from -0.3125 to 0.3125
- cotangent: bfloat16 [32768, 768], P(('dp', 'expert')), may hold values from -6 to 6
Outputs:
- layer_out: bfloat16 [32768, 768], P(('dp', 'expert'))
- grad_tokens: float32 [32768, 768], P(('dp', 'expert'))
- grad_query: float32 [768, 768], replicated
- grad_key: float32 [768, 768], replicated
- grad_value: float32 [768, 768], replicated
- grad_output: float32 [768, 768], replicated
- grad_first_gain: float32 [768], replicated
- grad_first_bias: float32 [768], replicated
- grad_second_gain: float32 [768], replicated
- grad_second_bias: float32 [768], replicated
- grad_up: float32 [8, 768, 3072], P('expert', None, 'dp')
- grad_down: float32 [8, 3072, 768], P('expert', 'dp')
Inputs may be any that keep to these rules, and one draw needn't show every extreme that they name: `routing`: each token names one expert. Among the 1024 tokens of one device no expert is named more than 256 times, and in some device's tokens one expert is named exactly 256 times.
All inputs are finite; a program needn't handle non-finite values.
Results may differ from a plain program's by a relative error of at most 0.014.
The roundings to bfloat16 on the way count: a program that leaves them out, or rounds other values in their place, can miss the bound.
Values may be sent and summed in bfloat16 or wider, within the bound.
No kernel may reach another device: no remote copies, remote signals or barrier semaphores. Data moves between devices by JAX's collectives and lax.ppermute only.
A program may use at most 256 MiB of HBM per device.

v0:
```python
import functools
import math

import jax
import jax.numpy as jnp
from jax import lax
from jax.experimental import pallas as pl
from jax.experimental.pallas import tpu as pltpu
from jax.sharding import PartitionSpec as P

HEADS = 12
HEAD = 64
LANES = 128
EPS = 1e-05
F32 = jnp.float32
BF16 = jnp.bfloat16
ROWS = 256

LIGHT = pl.CostEstimate(flops=1000000, bytes_accessed=100000, transcendentals=0)


def contract(left, right, left_dim, right_dim):
    return lax.dot_general(
        left, right, (((left_dim,), (right_dim,)), ((), ())), preferred_element_type=F32
    )


def normalize(values, gain, bias):
    centered = values - jnp.mean(values, axis=-1, keepdims=True)
    variance = jnp.mean(centered * centered, axis=-1, keepdims=True)
    scale = lax.rsqrt(variance + EPS)
    xhat = centered * scale
    return xhat * gain + bias, xhat, scale


def normalize_back(grad, xhat, scale, gain):
    scaled = grad * gain
    first = jnp.mean(scaled, axis=-1, keepdims=True)
    cross = jnp.mean(scaled * xhat, axis=-1, keepdims=True)
    return scale * (scaled - first - xhat * cross)


def head_mask(parity, value):
    lane = lax.broadcasted_iota(jnp.int32, (1, LANES), 1)
    return jnp.where(lane // HEAD == parity, value, 0.0).astype(BF16)


def causal_bias(bias_ref, keys_dim):
    @pl.when((pl.program_id(0) == 0) & (pl.program_id(1) == 0))
    def _():
        key = lax.broadcasted_iota(jnp.int32, bias_ref.shape, keys_dim)
        query = lax.broadcasted_iota(jnp.int32, bias_ref.shape, 1 - keys_dim)
        bias_ref[...] = jnp.where(key <= query, 0.0, -1e30)


def attention_kernel(q_ref, k_ref, v_ref, o_ref, lse_ref, bias_ref, *, block):
    causal_bias(bias_ref, 1)
    parity = pl.program_id(1)
    length = q_ref.shape[0]
    queries = q_ref[...] * head_mask(parity, HEAD**-0.5)
    values = v_ref[...] * head_mask(parity, 1.0)
    outs = []
    for index in range(length // block):
        first, finish = index * block, (index + 1) * block
        scores = contract(queries[first:finish], k_ref[:finish, :], 1, 1)
        diagonal = scores[:, first:] + bias_ref[...]
        if index:
            scores = jnp.concatenate([scores[:, :first], diagonal], axis=1)
        else:
            scores = diagonal
        top = jnp.max(scores, axis=1, keepdims=True)
        shifted = jnp.exp(scores - top)
        total = jnp.sum(shifted, axis=1, keepdims=True)
        probs = (shifted * (1.0 / total)).astype(BF16)
        outs.append(contract(probs, values[:finish], 1, 0).astype(BF16))
        lse = jnp.broadcast_to(top + jnp.log(total), (block, LANES))
        lse_ref[0, :, first:finish] = jnp.transpose(lse)[0:1, :]
    mixed = jnp.concatenate(outs, axis=0)

    @pl.when(parity == 0)
    def _():
        o_ref[...] = mixed

    @pl.when(parity == 1)
    def _():
        o_ref[...] = o_ref[...] + mixed


def attention(queries, keys, values):
    length, width = queries.shape
    pairs = width // LANES
    block = min(256, length)
    spec = pl.BlockSpec((length, LANES), lambda pair, parity: (0, pair))
    return pl.pallas_call(
        functools.partial(attention_kernel, block=block),
        grid=(pairs, 2),
        in_specs=[spec, spec, spec],
        out_specs=[
            spec,
            pl.BlockSpec((1, 1, length), lambda pair, parity: (pair * 2 + parity, 0, 0)),
        ],
        out_shape=[
            jax.ShapeDtypeStruct((length, width), BF16),
            jax.ShapeDtypeStruct((2 * pairs, 1, length), F32),
        ],
        scratch_shapes=[pltpu.VMEM((block, block), F32)],
        cost_estimate=LIGHT,
        name="attention",
    )(queries, keys, values)


def attention_back_kernel(
    q_ref, k_ref, v_ref, g_ref, lse_ref, grads_ref, dk_sum, dv_sum, bias_ref, *, block
):
    causal_bias(bias_ref, 0)
    parity = pl.program_id(1)
    length = q_ref.shape[0]
    scale_mask = head_mask(parity, HEAD**-0.5)
    queries = q_ref[...] * scale_mask
    grads = g_ref[...] * head_mask(parity, 1.0)
    keys_scaled = k_ref[...] * scale_mask
    dk_sum[...] = jnp.zeros_like(dk_sum)
    dv_sum[...] = jnp.zeros_like(dv_sum)
    dq_parts = []
    for index in range(length // block):
        first, finish = index * block, (index + 1) * block
        scores = contract(k_ref[:finish, :], queries[first:finish], 1, 1)
        diagonal = scores[first:] + bias_ref[...]
        if index:
            scores = jnp.concatenate([scores[:first], diagonal], axis=0)
        else:
            scores = diagonal
        probs = jnp.exp(scores - lse_ref[0, :, first:finish])
        dv_sum[:finish, :] += contract(probs.astype(BF16), grads[first:finish], 1, 0)
        grad_probs = contract(v_ref[:finish, :], grads[first:finish], 1, 1)
        delta = jnp.sum(probs * grad_probs, axis=0, keepdims=True)
        grad_scores = (probs * (grad_probs - delta)).astype(BF16)
        dk_sum[:finish, :] += contract(grad_scores, queries[first:finish], 1, 0)
        dq_parts.append(contract(grad_scores, keys_scaled[:finish], 0, 0).astype(BF16))
    parts = (
        jnp.concatenate(dq_parts, axis=0),
        dk_sum[...].astype(BF16),
        dv_sum[...].astype(BF16),
    )

    @pl.when(parity == 0)
    def _():
        for index, part in enumerate(parts):
            grads_ref[index] = part

    @pl.when(parity == 1)
    def _():
        for index, part in enumerate(parts):
            grads_ref[index] = grads_ref[index] + part


def attention_back(queries, keys, values, grads, lse, start, pairs):
    length = queries.shape[0]
    block = min(256, length)
    spec = pl.BlockSpec((length, LANES), lambda pair, parity: (0, start + pair))
    return pl.pallas_call(
        functools.partial(attention_back_kernel, block=block),
        grid=(pairs, 2),
        in_specs=[
            spec,
            spec,
            spec,
            spec,
            pl.BlockSpec(
                (1, 1, length), lambda pair, parity: ((start + pair) * 2 + parity, 0, 0)
            ),
        ],
        out_specs=pl.BlockSpec((3, length, LANES), lambda pair, parity: (0, 0, pair)),
        out_shape=jax.ShapeDtypeStruct((3, length, pairs * LANES), BF16),
        scratch_shapes=[pltpu.VMEM((length, LANES), F32)] * 2 + [pltpu.VMEM((block, block), F32)],
        cost_estimate=LIGHT,
        name="attention_back",
    )(queries, keys, values, grads, lse)


def gelu_parts(value):
    cdf = 0.5 + 0.5 * lax.erf(value * 0.5**0.5)
    density = jnp.exp2(value * value * (-0.5 / math.log(2.0)))
    return cdf, value * (density * (1.0 / math.sqrt(2.0 * math.pi)))


def expert_kernel(
    x_ref, c_ref, cen_ref, up_ref, down_ref,
    y_ref, gs_ref, dy_ref, h_ref, dp_ref,
    y_sum, dx_sum, gate_ref,
):
    step = pl.program_id(0)

    @pl.when(step == 0)
    def _():
        logit = jnp.sum(x_ref[...].astype(F32) * cen_ref[...], axis=1, keepdims=True)
        gate = jax.nn.sigmoid(logit)
        gate_ref[...] = jnp.broadcast_to(gate, gate_ref.shape)
        dy_ref[...] = (c_ref[...].astype(F32) * gate).astype(BF16)
        y_sum[...] = jnp.zeros_like(y_sum)
        dx_sum[...] = jnp.zeros_like(dx_sum)

    pre = contract(x_ref[...], up_ref[0], 1, 0)
    cdf, weighted = gelu_parts(pre)
    hidden = (pre * cdf).astype(BF16)
    slope = cdf + weighted
    h_ref[...] = hidden
    y_sum[...] += contract(hidden, down_ref[0], 1, 0)
    grad_hidden = contract(dy_ref[...], down_ref[0], 1, 1)
    grad_pre = (grad_hidden * slope).astype(BF16)
    dp_ref[...] = grad_pre
    dx_sum[...] += contract(grad_pre, up_ref[0], 1, 1)

    @pl.when(step == pl.num_programs(0) - 1)
    def _():
        produced = y_sum[...].astype(BF16)
        y_ref[...] = produced
        gate = gate_ref[:, 0:1]
        dot = jnp.sum(c_ref[...].astype(F32) * produced.astype(F32), axis=1, keepdims=True)
        grad_logit = dot * gate * (1.0 - gate)
        back = dx_sum[...].astype(BF16).astype(F32) + grad_logit * cen_ref[...]
        gs_ref[...] = back.astype(BF16)


def expert(rows, cots, centroid, up, down):
    count, width = rows.shape
    hidden = up.shape[2]
    tile = min(512, hidden)
    whole = pl.BlockSpec((count, width), lambda f: (0, 0))
    wide = jax.ShapeDtypeStruct((count, width), BF16)
    deep = jax.ShapeDtypeStruct((count, hidden), BF16)
    return pl.pallas_call(
        expert_kernel,
        grid=(hidden // tile,),
        in_specs=[
            whole,
            whole,
            pl.BlockSpec((1, width), lambda f: (0, 0)),
            pl.BlockSpec((1, width, tile), lambda f: (0, 0, f)),
            pl.BlockSpec((1, tile, width), lambda f: (0, f, 0)),
        ],
        out_specs=[whole, whole, whole]
        + [pl.BlockSpec((count, tile), lambda f: (0, f))] * 2,
        out_shape=[wide, wide, wide, deep, deep],
        scratch_shapes=[
            pltpu.VMEM((count, width), F32),
            pltpu.VMEM((count, width), F32),
            pltpu.VMEM((count, LANES), F32),
        ],
        cost_estimate=LIGHT,
        name="expert",
    )(rows, cots, centroid, up, down)


def expert_weights_kernel(
    core_ref, x_ref, dy_ref, h_ref, dp_ref,
    up_send_ref, down_send_ref, up_keep_ref, down_keep_ref, xt_ref,
):
    @pl.when(pl.program_id(0) == 0)
    def _():
        xt_ref[...] = jnp.transpose(x_ref[...])

    up = contract(xt_ref[...], dp_ref[...], 1, 0).astype(BF16)
    down = contract(h_ref[...], dy_ref[...], 0, 0).astype(BF16)
    sending = pl.program_id(0) < pl.num_programs(0) // 2

    @pl.when(sending)
    def _():
        up_send_ref[0] = up
        down_send_ref[0] = down

    @pl.when(jnp.logical_not(sending))
    def _():
        up_keep_ref[0] = up
        down_keep_ref[0] = down


def expert_weights(rows, grads, hidden_rows, grad_pre, parts, core):
    count, width = rows.shape
    hidden = hidden_rows.shape[1]
    share = hidden // parts
    tile = min(384, share)
    each = share // tile
    half = hidden // tile // 2

    def column(f, core):
        step = f % half
        other = jnp.where(f < half, 1 - core[0], core[0])
        return ((step // each) * 2 + other) * each + step % each

    def send(f):
        return jnp.minimum(f, half - 1)

    def keep(f):
        return jnp.maximum(f - half, 0)

    whole = pl.BlockSpec((count, width), lambda f, core: (0, 0))
    deep = pl.BlockSpec((count, tile), lambda f, core: (0, column(f, core)))
    up = [
        pl.BlockSpec((1, width, tile), lambda f, core, at=at: (at(f) // each, 0, at(f) % each))
        for at in (send, keep)
    ]
    down = [
        pl.BlockSpec((1, tile, width), lambda f, core, at=at: (at(f) // each, at(f) % each, 0))
        for at in (send, keep)
    ]
    up_shape = jax.ShapeDtypeStruct((parts // 2, width, share), BF16)
    down_shape = jax.ShapeDtypeStruct((parts // 2, share, width), BF16)
    return pl.pallas_call(
        expert_weights_kernel,
        grid_spec=pltpu.PrefetchScalarGridSpec(
            num_scalar_prefetch=1,
            grid=(2 * half,),
            in_specs=[whole, whole, deep, deep],
            out_specs=[up[0], down[0], up[1], down[1]],
            scratch_shapes=[pltpu.VMEM((width, count), BF16)],
        ),
        out_shape=[up_shape, down_shape, up_shape, down_shape],
        cost_estimate=LIGHT,
        name="expert_weights",
    )(core, rows, grads, hidden_rows, grad_pre)


def one_hot(condition):
    return jnp.where(condition, 1.0, 0.0).astype(BF16)


def block_rows(step, count, length, dim):
    return step * count + lax.broadcasted_iota(jnp.int32, (count, length), dim)


def const(*shape):
    return pl.BlockSpec(shape, lambda *step: (0,) * len(shape))


def route_kernel(routing_ref, cot_ref, send_ref, slot_ref, wide_ref, *, experts, capacity):
    length = routing_ref.shape[1]
    step = pl.program_id(0)

    @pl.when(step == 0)
    def _():
        chosen = routing_ref[...]
        named = lax.broadcasted_iota(jnp.int32, (experts, length), 0) == chosen
        named = jnp.where(named, 1.0, 0.0)
        lane = lax.broadcasted_iota(jnp.int32, (experts, length), 1)
        count = named
        shift = 1
        while shift < length:
            count = count + jnp.where(lane >= shift, pltpu.roll(count, shift, 1), 0.0)
            shift *= 2
        position = jnp.sum(named * (count - named), axis=0, keepdims=True)
        slot = chosen.astype(F32) * capacity + position
        slot = jnp.where(position < capacity, slot, -1.0)
        slot_ref[...] = slot.astype(jnp.int32)
        wide_ref[...] = jnp.transpose(jnp.broadcast_to(slot, (LANES, length))).astype(jnp.int32)

    place = one_hot(block_rows(step, send_ref.shape[0], length, 0) == slot_ref[...])
    send_ref[...] = contract(place, cot_ref[...], 1, 0).astype(BF16)


def route(routing, cotangent, experts, capacity):
    length, width = cotangent.shape
    slots = experts * capacity
    return pl.pallas_call(
        functools.partial(route_kernel, experts=experts, capacity=capacity),
        grid=(slots // ROWS,),
        in_specs=[const(1, length), const(length, width)],
        out_specs=[
            pl.BlockSpec((ROWS, width), lambda i: (i, 0)),
            const(1, length),
            const(length, LANES),
        ],
        out_shape=[
            jax.ShapeDtypeStruct((slots, width), BF16),
            jax.ShapeDtypeStruct((1, length), jnp.int32),
            jax.ShapeDtypeStruct((length, LANES), jnp.int32),
        ],
        cost_estimate=LIGHT,
        name="route",
    )(routing, cotangent)


def project_kernel(
    tokens_ref, gain_ref, bias_ref, wq_ref, wk_ref, wv_ref, turned_ref, q_ref, k_ref, v_ref
):
    normed, _, _ = normalize(tokens_ref[...].astype(F32), gain_ref[...], bias_ref[...])
    normed = normed.astype(BF16)
    turned_ref[...] = jnp.transpose(normed)
    for weight, out in ((wq_ref, q_ref), (wk_ref, k_ref), (wv_ref, v_ref)):
        out[...] = contract(normed, weight[...], 1, 0).astype(BF16)


def project(tokens, gain, bias, weights):
    length, width = tokens.shape
    rows = pl.BlockSpec((ROWS, width), lambda i: (i, 0))
    out = jax.ShapeDtypeStruct((length, width), BF16)
    return pl.pallas_call(
        project_kernel,
        grid=(length // ROWS,),
        in_specs=[rows, const(1, width), const(1, width)] + [const(width, width)] * 3,
        out_specs=[pl.BlockSpec((width, ROWS), lambda i: (0, i))] + [rows] * 3,
        out_shape=[jax.ShapeDtypeStruct((width, length), BF16)] + [out] * 3,
        cost_estimate=LIGHT,
        name="project",
    )(tokens, gain, bias, *weights)


def branch_kernel(
    mixed_ref, tokens_ref, weight_ref, gain_ref, bias_ref, cen_ref, chosen_ref, slot_ref,
    resid_ref, gate_ref, turned_ref, send_ref, low_ref, *, blocks,
):
    step = pl.program_id(0)

    @pl.when(step < blocks)
    def _():
        mixed = mixed_ref[...]
        turned_ref[...] = jnp.transpose(mixed)
        resid = tokens_ref[...].astype(F32) + contract(mixed, weight_ref[...], 1, 0)
        second, _, _ = normalize(resid, gain_ref[...], bias_ref[...])
        resid_ref[...] = resid
        low_ref[pl.ds(pl.multiple_of(step * ROWS, ROWS), ROWS), :] = second.astype(BF16)
        centroid = jnp.zeros_like(second)
        for index in range(cen_ref.shape[0]):
            centroid = jnp.where(chosen_ref[...] == index, cen_ref[index : index + 1, :], centroid)
        gate_ref[...] = jax.nn.sigmoid(jnp.sum(second * centroid, axis=1, keepdims=True))

    @pl.when(step >= blocks)
    def _():
        place = one_hot(block_rows(step - blocks, ROWS, slot_ref.shape[1], 0) == slot_ref[...])
        send_ref[...] = contract(place, low_ref[...], 1, 0).astype(BF16)


def branch(mixed, tokens, weight, gain, bias, centroids, routing, slot, slots):
    length, width = mixed.shape
    blocks = length // ROWS

    def at(i):
        return jnp.minimum(i, blocks - 1)

    rows = pl.BlockSpec((ROWS, width), lambda i: (at(i), 0))
    thin = pl.BlockSpec((ROWS, 1), lambda i: (at(i), 0))
    return pl.pallas_call(
        functools.partial(branch_kernel, blocks=blocks),
        grid=(blocks + slots // ROWS,),
        in_specs=[
            rows,
            rows,
            const(width, width),
            const(1, width),
            const(1, width),
            const(*centroids.shape),
            thin,
            const(1, length),
        ],
        out_specs=[
            rows,
            thin,
            pl.BlockSpec((width, ROWS), lambda i: (0, at(i))),
            pl.BlockSpec((ROWS, width), lambda i: (jnp.maximum(i - blocks, 0), 0)),
        ],
        out_shape=[
            jax.ShapeDtypeStruct((length, width), F32),
            jax.ShapeDtypeStruct((length, 1), F32),
            jax.ShapeDtypeStruct((width, length), BF16),
            jax.ShapeDtypeStruct((slots, width), BF16),
        ],
        scratch_shapes=[pltpu.VMEM((length, width), BF16)],
        cost_estimate=LIGHT,
        name="branch",
    )(mixed, tokens, weight, gain, bias, centroids, routing, slot)


def gathered(wide_ref, rows_ref):
    slots = rows_ref.shape[0]
    count = wide_ref.shape[0]
    wide = jnp.concatenate([wide_ref[...]] * (slots // LANES), axis=1)
    place = one_hot(lax.broadcasted_iota(jnp.int32, (count, slots), 1) == wide)
    return contract(place, rows_ref[...], 1, 0)


def second_back_kernel(
    wide_ref, back_ref, resid_ref, cot_ref, gain_ref, weight_ref,
    grad_ref, low_ref, mixed_ref, sums_ref,
):
    grad = gathered(wide_ref, back_ref)
    _, xhat, scale = normalize(resid_ref[...], gain_ref[...], gain_ref[...])
    sums = jnp.concatenate(
        [jnp.sum(grad * xhat, axis=0, keepdims=True), jnp.sum(grad, axis=0, keepdims=True)], axis=0
    )

    @pl.when(pl.program_id(0) == 0)
    def _():
        sums_ref[...] = sums

    @pl.when(pl.program_id(0) > 0)
    def _():
        sums_ref[...] = sums_ref[...] + sums

    grad = cot_ref[...].astype(F32) + normalize_back(grad, xhat, scale, gain_ref[...])
    grad_ref[...] = grad
    low = grad.astype(BF16)
    low_ref[...] = low
    mixed_ref[...] = contract(low, weight_ref[...], 1, 1).astype(BF16)


def second_back(wide, back, resid, cotangent, gain, weight):
    length, width = resid.shape
    rows = pl.BlockSpec((ROWS, width), lambda i: (i, 0))
    low = jax.ShapeDtypeStruct((length, width), BF16)
    return pl.pallas_call(
        second_back_kernel,
        grid=(length // ROWS,),
        in_specs=[
            pl.BlockSpec((ROWS, LANES), lambda i: (i, 0)),
            const(*back.shape),
            rows,
            rows,
            const(1, width),
            const(width, width),
        ],
        out_specs=[rows, rows, rows, const(2, width)],
        out_shape=[
            jax.ShapeDtypeStruct((length, width), F32),
            low,
            low,
            jax.ShapeDtypeStruct((2, width), F32),
        ],
        cost_estimate=LIGHT,
        name="second_back",
    )(wide, back, resid, cotangent, gain, weight)


def first_back_kernel(
    left_ref, right_ref, tokens_ref, resid_ref, gain_ref, wq_ref, wk_ref, wv_ref,
    grad_ref, sums_ref,
):
    side = left_ref.shape[2]
    grad = 0.0
    for index, weight in enumerate((wq_ref, wk_ref, wv_ref)):
        grad = grad + contract(left_ref[index], weight[:, :side], 1, 1)
        grad = grad + contract(right_ref[index], weight[:, side:], 1, 1)
    gain = gain_ref[...]
    _, xhat, scale = normalize(tokens_ref[...].astype(F32), gain, gain)
    sums = jnp.concatenate(
        [jnp.sum(grad * xhat, axis=0, keepdims=True), jnp.sum(grad, axis=0, keepdims=True)], axis=0
    )

    @pl.when(pl.program_id(0) == 0)
    def _():
        sums_ref[...] = sums

    @pl.when(pl.program_id(0) > 0)
    def _():
        sums_ref[...] = sums_ref[...] + sums

    grad_ref[...] = resid_ref[...] + normalize_back(grad, xhat, scale, gain)


def first_back(left, right, tokens, resid, gain, weights):
    length, width = tokens.shape
    rows = pl.BlockSpec((ROWS, width), lambda i: (i, 0))
    return pl.pallas_call(
        first_back_kernel,
        grid=(length // ROWS,),
        in_specs=[
            pl.BlockSpec((3, ROWS, part.shape[2]), lambda i: (0, i, 0)) for part in (left, right)
        ]
        + [rows, rows, const(1, width)]
        + [const(width, width)] * 3,
        out_specs=[rows, const(2, width)],
        out_shape=[
            jax.ShapeDtypeStruct((length, width), F32),
            jax.ShapeDtypeStruct((2, width), F32),
        ],
        cost_estimate=LIGHT,
        name="first_back",
    )(left, right, tokens, resid, gain, *weights)


def layer_out_kernel(wide_ref, rows_ref, resid_ref, gate_ref, out_ref):
    out_ref[...] = (resid_ref[...] + gate_ref[...] * gathered(wide_ref, rows_ref)).astype(BF16)


def layer_output(wide, produced, resid, gate):
    length, width = resid.shape
    rows = pl.BlockSpec((ROWS, width), lambda i: (i, 0))
    return pl.pallas_call(
        layer_out_kernel,
        grid=(length // ROWS,),
        in_specs=[
            pl.BlockSpec((ROWS, LANES), lambda i: (i, 0)),
            const(*produced.shape),
            rows,
            pl.BlockSpec((ROWS, 1), lambda i: (i, 0)),
        ],
        out_specs=rows,
        out_shape=jax.ShapeDtypeStruct((length, width), BF16),
        cost_estimate=LIGHT,
        name="layer_output",
    )(wide, produced, resid, gate)


def weight_grads_kernel(core_ref, *refs, sources):
    lefts, rights, send_ref, keep_ref = refs[:-2:2], refs[1:-2:2], refs[-2], refs[-1]
    matrix = pl.program_id(0)
    rows = send_ref.shape[1]
    first = 0
    for left, right, count in zip(lefts, rights, sources):
        @pl.when((matrix >= first) & (matrix < first + count))
        def _(left=left, right=right):
            grad = right[0] if len(right.shape) == 3 else right[...]
            for half, out in ((1 - core_ref[0], send_ref), (core_ref[0], keep_ref)):
                turned = left[pl.ds(pl.multiple_of(half * rows, rows), rows), :]
                out[0] = contract(turned, grad, 1, 0).astype(BF16)

        first += count


def weight_grads(core, side, *sources):
    width, length = sources[0][0].shape
    counts, specs, args = [], [], []
    for turned, grads in sources:
        counts.append(3 if grads.ndim == 3 else grads.shape[1] // side)
    total = sum(counts)
    first = 0
    for (turned, grads), count in zip(sources, counts):
        def which(step, first=first, count=count):
            return jnp.clip(step - first, 0, count - 1)

        specs.append(pl.BlockSpec((width, length), lambda i, core: (0, 0)))
        if grads.ndim == 3:
            specs.append(
                pl.BlockSpec((1, length, side), lambda i, core, which=which: (which(i), 0, 0))
            )
        else:
            specs.append(pl.BlockSpec((length, side), lambda i, core, which=which: (0, which(i))))
        args += [turned, grads]
        first += count
    shape = jax.ShapeDtypeStruct((total, width // 2, side), BF16)
    send, keep = pl.pallas_call(
        functools.partial(weight_grads_kernel, sources=tuple(counts)),
        grid_spec=pltpu.PrefetchScalarGridSpec(
            num_scalar_prefetch=1,
            grid=(total,),
            in_specs=specs,
            out_specs=[pl.BlockSpec((1, width // 2, side), lambda i, core: (i, 0, 0))] * 2,
        ),
        out_shape=[shape, shape],
        cost_estimate=LIGHT,
        name="weight_grads",
    )(core, *args)
    return send.reshape(-1, side), keep.reshape(-1, side)


def assemble_kernel(core_ref, early_mine, early_other, late_mine, late_other, *outs):
    mine = pl.program_id(0) == core_ref[0]
    side = early_mine.shape[2]

    def write(early, late):
        outs[0][:, :side] = early[0].astype(F32)
        outs[0][:, side:] = early[1].astype(F32)
        for index in range(3):
            outs[1 + index][:, :side] = early[2 + index].astype(F32)
            outs[1 + index][:, side:] = late[index].astype(F32)

    @pl.when(mine)
    def _():
        write(early_mine, late_mine)

    @pl.when(jnp.logical_not(mine))
    def _():
        write(early_other, late_other)


def assemble(core, early_mine, early_other, late_mine, late_other, width):
    side = early_mine.shape[1]
    args = [
        part.reshape(-1, width // 2, side)
        for part in (early_mine, early_other, late_mine, late_other)
    ]
    out = jax.ShapeDtypeStruct((width, width), F32)
    return pl.pallas_call(
        assemble_kernel,
        grid_spec=pltpu.PrefetchScalarGridSpec(
            num_scalar_prefetch=1,
            grid=(2,),
            in_specs=[const(*part.shape) for part in args],
            out_specs=[pl.BlockSpec((width // 2, width), lambda i, core: (i, 0))] * 4,
        ),
        out_shape=[out] * 4,
        cost_estimate=LIGHT,
        name="assemble",
    )(core, *args)


def swap(value, axis, bit):
    size = lax.axis_size(axis)
    return lax.ppermute(value, axis, [(i, i ^ bit) for i in range(size)])


def stages(axis, low, high):
    found = []
    bit = low
    while bit < min(high, lax.axis_size(axis)):
        found.append((axis, bit))
        bit *= 2
    return found


def bit_of(axis, bit):
    return (lax.axis_index(axis) // bit) % 2


def add_low(left, right):
    return (left.astype(F32) + right.astype(F32)).astype(BF16)


def add(left, right):
    return left + right


def halves(rows, stage):
    axis, bit = stage
    half = rows.shape[0] // 2
    mine = bit_of(axis, bit)
    return (
        lax.dynamic_slice_in_dim(rows, (1 - mine) * half, half, 0),
        lax.dynamic_slice_in_dim(rows, mine * half, half, 0),
    )


def joined(rows, other, stage):
    first = bit_of(*stage) == 0
    return jnp.concatenate([jnp.where(first, rows, other), jnp.where(first, other, rows)], axis=0)


def add_split_kernel(mine_ref, left_ref, right_ref, send_ref, keep_ref):
    value = add_low(left_ref[...], right_ref[...])

    @pl.when(pl.program_id(0) == 0)
    def _():
        send_ref[...] = value

    @pl.when(pl.program_id(0) == 1)
    def _():
        keep_ref[...] = value


def add_split(left, right, stage):
    half, width = left.shape[0] // 2, left.shape[1]
    if half % 8:
        return halves(add_low(left, right), stage)
    mine = bit_of(*stage).astype(jnp.int32)[None]
    block = pl.BlockSpec((half, width), lambda i, mine: (jnp.where(i == 0, 1 - mine[0], mine[0]), 0))
    out = pl.BlockSpec((half, width), lambda i, mine: (0, 0))
    shape = jax.ShapeDtypeStruct((half, width), BF16)
    return pl.pallas_call(
        add_split_kernel,
        grid_spec=pltpu.PrefetchScalarGridSpec(
            num_scalar_prefetch=1,
            grid=(2,),
            in_specs=[block, block],
            out_specs=[out, out],
        ),
        out_shape=[shape, shape],
        cost_estimate=LIGHT,
        name="add_split",
    )(mine, left, right)


def halves_sum(left, right, stage):
    width = left.shape[2]
    parts = add_split(left.reshape(-1, width), right.reshape(-1, width), stage)
    return [part.reshape(-1, *left.shape[1:]) for part in parts]


class Sum:
    def __init__(self, keep, send, stages, plus=add_low, split=True):
        self.keep, self.send, self.plus = keep, send, plus
        if split:
            self.steps = [("whole", stages[0])]
            self.steps += [("halve", stage) for stage in stages[1:-1]]
            self.steps += [("whole", stages[-1])]
            self.steps += [("join", stage) for stage in stages[-2:0:-1]]
        else:
            self.steps = [("whole", stage) for stage in stages]

    def start(self):
        return swap(self.send, *self.steps[0][1])

    def finish(self, got):
        kind, stage = self.steps.pop(0)
        if self.steps and self.steps[0][0] == "halve":
            self.send, self.keep = add_split(self.keep, got, self.steps[0][1])
        else:
            join = functools.partial(joined, stage=stage)
            self.keep = self.send = (join if kind == "join" else self.plus)(self.keep, got)


def advance(sums, *others):
    sums = [each for each in sums if each.steps]
    tied = tie((*(each.start() for each in sums), *others))
    for each, got in zip(sums, tied):
        each.finish(got)
    rest = tied[len(sums) :]
    return rest[0] if len(rest) == 1 else rest


def chip_stages(total):
    return [("dp", 2 << index) for index in range((total.shape[0]).bit_length() - 1)][::-1]


tie = lax.optimization_barrier


def exchange(rows):
    return lax.all_to_all(rows, "expert", split_axis=0, concat_axis=0, tiled=True)


def local(
    tokens,
    routing,
    query_weight,
    key_weight,
    value_weight,
    output_weight,
    first_gain,
    first_bias,
    second_gain,
    second_bias,
    centroids,
    expert_up,
    expert_down,
    cotangent,
):
    length, width = tokens.shape
    experts = centroids.shape[0]
    capacity = length // experts
    peers = lax.axis_size("expert")
    parts = lax.axis_size("dp")
    slots = experts * capacity
    core = (lax.axis_index("dp") % 2).astype(jnp.int32)[None]
    vectors = tie(jnp.stack([first_gain, first_bias, second_gain, second_bias]))
    first_gain, first_bias, second_gain, second_bias = (vectors[i : i + 1] for i in range(4))
    weights = (query_weight, key_weight, value_weight)

    cots, slot, wide = route(routing.reshape(1, length), cotangent, experts, capacity)
    cots, tokens = tie((cots, tokens))
    cots = exchange(cots.reshape(peers, -1, width)).reshape(slots, width)

    normed_turned, queries, keys, values = project(tokens, first_gain, first_bias, weights)
    mixed, lse = attention(queries, keys, values)
    mixed, cots = tie((mixed, cots))
    resid, gate, mixed_turned, rows = branch(
        mixed, tokens, output_weight, second_gain, second_bias, centroids, routing, slot, slots
    )

    rows = exchange(rows.reshape(peers, -1, width)).reshape(slots, width)
    own = centroids[lax.axis_index("expert")][None, :]
    produced, returned, grad_rows, hidden, grad_pre = expert(
        rows, cots, own, expert_up, expert_down
    )
    returned = exchange(returned.reshape(peers, -1, width))
    up_send, down_send, up_keep, down_keep = expert_weights(
        rows, grad_rows, hidden, grad_pre, parts, core
    )
    chips = chip_stages(up_send)
    up_send, up_keep = halves_sum(up_keep, swap(up_send, "dp", 1), chips[0])
    down_send, down_keep = halves_sum(down_keep, swap(down_send, "dp", 1), chips[0])
    returned, produced, up_send, up_keep, down_send, down_keep = tie(
        (returned, produced, up_send, up_keep, down_send, down_keep)
    )
    returned = returned.reshape(slots, width)
    up_got = swap(up_send, *chips[0])
    down_got = swap(down_send, *chips[0])
    produced = exchange(produced.reshape(peers, -1, width))

    grad_resid, grad_branch, grad_mixed, second_sums = second_back(
        wide, returned, resid, cotangent, second_gain, output_weight
    )

    pairs = width // LANES
    split = pairs // 2
    side = split * LANES
    cross = stages("expert", 1, 1 << 20)
    apart = stages("dp", 2, 1 << 20)
    left = attention_back(queries, keys, values, grad_mixed, lse, 0, split)
    left, up_got = tie((left, up_got))
    send, keep = weight_grads(core, side, (mixed_turned, grad_branch), (normed_turned, left))
    early = Sum(keep, send, [("dp", 1)] + cross + apart)
    advance([early])
    early.send, lse = tie((early.send, lse))
    right = attention_back(queries, keys, values, grad_mixed, lse, split, pairs - split)
    right, produced = advance([early], right, produced)
    produced = produced.reshape(slots, width)
    send, keep = weight_grads(core, side, (normed_turned, right))
    send, keep = tie((send, keep))
    grad_tokens, first_sums = first_back(left, right, tokens, grad_resid, first_gain, weights)
    late = Sum(keep, send, [("dp", 1)] + apart + cross)
    grad_tokens, first_sums, down_got = advance([early, late], grad_tokens, first_sums, down_got)
    grad_up = up_keep.astype(F32) + up_got.astype(F32)
    grad_down = down_keep.astype(F32) + down_got.astype(F32)
    for stage in chips[1:]:
        grad_up, grad_down = (
            keep.astype(F32) + swap(send, *stage).astype(F32)
            for send, keep in (halves(value.astype(BF16), stage) for value in (grad_up, grad_down))
        )
    grad_up, grad_down = (value.reshape(value.shape[1:])[None] for value in (grad_up, grad_down))
    small = jnp.concatenate([first_sums, second_sums], axis=0)
    small = Sum(small, small, stages("dp", 1, 1 << 20) + cross, plus=add, split=False)
    layer_out = layer_output(wide, produced, resid, gate)
    layer_out = advance([early, late, small], layer_out)
    while early.steps or late.steps or small.steps:
        advance([early, late, small])
    early, late, small = early.keep, late.keep, small.keep
    grad_output, grad_query, grad_key, grad_value = assemble(
        core, early, swap(early, "dp", 1), late, swap(late, "dp", 1), width
    )
    return (
        layer_out,
        grad_tokens,
        grad_query,
        grad_key,
        grad_value,
        grad_output,
        small[0],
        small[1],
        small[2],
        small[3],
        grad_up,
        grad_down,
    )


def solution(mesh):
    rows = P(("dp", "expert"), None)
    return jax.shard_map(
        local,
        mesh=mesh,
        in_specs=(rows, rows)
        + (P(),) * 9
        + (P("expert", None, None), P("expert", None, None), rows),
        out_specs=(rows, rows) + (P(),) * 8 + (P("expert", None, "dp"), P("expert", "dp", None)),
        check_vma=False,
    )
```

profile of v0, /device:TPU:0, one launch (start us, length us, event | category | flops | bytes accessed | tf_op | source)
XLA Modules:
  0.0 372.1 jit_solution(10468218632340767893)
XLA Ops:
  0.6 5.4 %route.1 = (bf16[1024,768]{1,0:T(8,128)(2,1)}, s32[1,1024]{1,0:T(1,128)}, s32[1024,128]{1,0:T(8,128)}) custom-call(s32[1,1024]{1,0:T(1,128)} %bitcast.49, bf16[1024,768]{1,0:T(8,128)(2,1)} %cot_ref.3), custom_call_target="tpu_custom_call" | custom-call | flops 1000000 | bytes 100000 | tf_op jit(solution)/shard_map/route/pallas_call | solution.py:364
  6.1 7.5 %all-to-all-start = ((bf16[8,128,768]{2,1,0:T(8,128)(2,1)}), bf16[8,128,768]{2,1,0:T(8,128)(2,1)S(1)}, u32[]{:S(2)}, u32[]{:S(2)}) async-start(bf16[8,128,768]{2,1,0:T(8,128)(2,1)} %bitcast.41), calls=%async_computation | async-start | bytes 3145728 | tf_op jit(solution)/shard_map/all_to_all | solution.py:817
  15.3 8.2 %project.1 = (bf16[768,1024]{1,0:T(8,128)(2,1)}, bf16[1024,768]{1,0:T(8,128)(2,1)}, bf16[1024,768]{1,0:T(8,128)(2,1)}, bf16[1024,768]{1,0:T(8,128)(2,1)}) custom-call(bf16[1024,768]{1,0:T(8,128)(2,1)} %tokens_ref.2, f32[1,768]{1,0:T(1,128)} %get-tuple-element.215.gain_ref, f32[1,768]{1,0:T(1,128)} %get-tuple-element.214.bias_ref, bf16[768,768]{1,0:T(8,128)(2,1)} %wq_ref.3, ...), custom_call_target="tpu_custom_call" | custom-call | flops 1000000 | bytes 100000 | tf_op jit(solution)/shard_map/project/pallas_call | solution.py:397
  23.5 29.3 %attention.1 = (bf16[1024,768]{1,0:T(8,128)(2,1)}, f32[12,1,1024]{2,1,0:T(1,128)}) custom-call(bf16[1024,768]{1,0:T(8,128)(2,1)} %get-tuple-element.106.q_ref, bf16[1024,768]{1,0:T(8,128)(2,1)} %get-tuple-element.107.k_ref, bf16[1024,768]{1,0:T(8,128)(2,1)} %get-tuple-element.108.v_ref), custom_call_target="tpu_custom_call" | custom-call | flops 1000000 | bytes 100000 | tf_op jit(solution)/shard_map/attention/pallas_call | solution.py:94
  52.8 11.2 %branch.1 = (f32[1024,768]{1,0:T(8,128)}, f32[1024,1]{1,0:T(8,128)}, bf16[768,1024]{1,0:T(8,128)(2,1)}, bf16[1024,768]{1,0:T(8,128)(2,1)}) custom-call(bf16[1024,768]{1,0:T(8,128)(2,1)} %get-tuple-element.111.mixed_ref, bf16[1024,768]{1,0:T(8,128)(2,1)} %tokens_ref.2, bf16[768,768]{1,0:T(8,128)(2,1)} %weight_ref.3, f32[1,768]{1,0:T(1,128)} %get-tuple-element.213.gain_ref, ...), custom_call_target="tpu_custom_call" | custom-call | flops 1000000 | bytes 100000 | tf_op jit(solution)/shard_map/branch/pallas_call | solution.py:442
  63.9 6.0 %all-to-all-start.1 = ((bf16[8,128,768]{2,1,0:T(8,128)(2,1)}), bf16[8,128,768]{2,1,0:T(8,128)(2,1)S(1)}, u32[]{:S(2)}, u32[]{:S(2)}) async-start(bf16[8,128,768]{2,1,0:T(8,128)(2,1)} %bitcast.42), calls=%async_computation.1 | async-start | bytes 3145728 | tf_op jit(solution)/shard_map/all_to_all | solution.py:817
  71.3 35.1 %all-to-all-done.1 = bf16[8,128,768]{2,1,0:T(8,128)(2,1)S(1)} async-done(((bf16[8,128,768]{2,1,0:T(8,128)(2,1)}), bf16[8,128,768]{2,1,0:T(8,128)(2,1)S(1)}, u32[]{:S(2)}, u32[]{:S(2)}) %all-to-all-start.1) | async-done | bytes 1572896 | tf_op jit(solution)/shard_map/all_to_all | solution.py:817
  107.5 29.3 %expert.1 = (bf16[1024,768]{1,0:T(8,128)(2,1)}, bf16[1024,768]{1,0:T(8,128)(2,1)}, bf16[1024,768]{1,0:T(8,128)(2,1)}, bf16[1024,3072]{1,0:T(8,128)(2,1)}, bf16[1024,3072]{1,0:T(8,128)(2,1)}) custom-call(bf16[1024,768]{1,0:T(8,128)(2,1)} %bitcast.30, bf16[1024,768]{1,0:T(8,128)(2,1)} %bitcast.34, f32[1,768]{1,0:T(1,128)} %constant_dynamic-slice_fusion.cen_ref, ...), custom_call_target="tpu_custom_call" | custom-call | flops 1000000 | bytes 100000 | tf_op jit(solution)/shard_map/expert/pallas_call | solution.py:232
  140.6 18.9 %expert_weights.1 = (bf16[2,768,768]{2,1,0:T(8,128)(2,1)}, bf16[2,768,768]{2,1,0:T(8,128)(2,1)}, bf16[2,768,768]{2,1,0:T(8,128)(2,1)}, bf16[2,768,768]{2,1,0:T(8,128)(2,1)}) custom-call(s32[1]{0:T(128)} %bitcast.3.core_ref, bf16[1024,768]{1,0:T(8,128)(2,1)} %bitcast.31, bf16[1024,768]{1,0:T(8,128)(2,1)} %get-tuple-element.119.dy_ref, ...), custom_call_target="tpu_custom_call" | custom-call | flops 1000000 | bytes 100000 | tf_op jit(solution)/shard_map/expert_weights/pallas_call | solution.py:309
  164.3 4.4 %add_split.8 = (bf16[768,768]{1,0:T(8,128)(2,1)}, bf16[768,768]{1,0:T(8,128)(2,1)}) custom-call(s32[1]{0:T(128)} %bitcast.10.mine_ref, bf16[1536,768]{1,0:T(8,128)(2,1)} %bitcast.38, bf16[1536,768]{1,0:T(8,128)(2,1)} %bitcast.12.right_ref), custom_call_target="tpu_custom_call" | custom-call | flops 1000000 | bytes 100000 | tf_op jit(solution)/shard_map/add_split/pallas_call | solution.py:757
  168.7 4.4 %add_split.9 = (bf16[768,768]{1,0:T(8,128)(2,1)}, bf16[768,768]{1,0:T(8,128)(2,1)}) custom-call(s32[1]{0:T(128)} %bitcast.10.mine_ref, bf16[1536,768]{1,0:T(8,128)(2,1)} %bitcast.37, bf16[1536,768]{1,0:T(8,128)(2,1)} %bitcast.16.right_ref), custom_call_target="tpu_custom_call" | custom-call | flops 1000000 | bytes 100000 | tf_op jit(solution)/shard_map/add_split/pallas_call | solution.py:757
  173.1 4.6 %all-to-all-done.2 = bf16[8,128,768]{2,1,0:T(8,128)(2,1)S(1)} async-done(((bf16[8,128,768]{2,1,0:T(8,128)(2,1)}), bf16[8,128,768]{2,1,0:T(8,128)(2,1)S(1)}, u32[]{:S(2)}, u32[]{:S(2)}) %all-to-all-start.2) | async-done | bytes 1572896 | tf_op jit(solution)/shard_map/all_to_all | solution.py:817
  182.8 9.3 %second_back.1 = (f32[1024,768]{1,0:T(8,128)}, bf16[1024,768]{1,0:T(8,128)(2,1)}, bf16[1024,768]{1,0:T(8,128)(2,1)}, f32[2,768]{1,0:T(2,128)}) custom-call(s32[1024,128]{1,0:T(8,128)} %get-tuple-element.114.wide_ref, bf16[1024,768]{1,0:T(8,128)(2,1)} %bitcast.33, f32[1024,768]{1,0:T(8,128)} %get-tuple-element.131.resid_ref, bf16[1024,768]{1,0:T(8,128)(2,1)} %cot_ref.3, ...), custom_call_target="tpu_custom_call" | custom-call | flops 1000000 | bytes 100000 | tf_op jit(solution)/shard_map/second_back/pallas_call | solution.py:510
  192.1 21.1 %attention_back.2.refs_3_.left_ref = bf16[3,1024,384]{2,1,0:T(8,128)(2,1)} custom-call(bf16[1024,768]{1,0:T(8,128)(2,1)} %get-tuple-element.106.q_ref, bf16[1024,768]{1,0:T(8,128)(2,1)} %get-tuple-element.107.k_ref, bf16[1024,768]{1,0:T(8,128)(2,1)} %get-tuple-element.108.v_ref, bf16[1024,768]{1,0:T(8,128)(2,1)} %get-tuple-element.134.g_ref, ...), custom_call_target="tpu_custom_call" | custom-call | flops 1000000 | bytes 100000 | tf_op jit(solution)/shard_map/attention_back/pallas_call | solution.py:161
  213.1 8.7 %weight_grads.2 = (bf16[5,384,384]{2,1,0:T(8,128)(2,1)}, bf16[5,384,384]{2,1,0:T(8,128)(2,1)}) custom-call(s32[1]{0:T(128)} %bitcast.3.core_ref, bf16[768,1024]{1,0:T(8,128)(2,1)} %get-tuple-element.113.refs_0_, bf16[1024,768]{1,0:T(8,128)(2,1)} %get-tuple-element.132.refs_1_, bf16[768,1024]{1,0:T(8,128)(2,1)} %get-tuple-element.133.refs_2_.refs_0_, ...), custom_call_target="tpu_custom_call" | custom-call | flops 1000000 | bytes 100000 | tf_op jit(solution)/shard_map/weight_grads/pallas_call | solution.py:640
  232.8 21.1 %attention_back.3.refs_1_.right_ref = bf16[3,1024,384]{2,1,0:T(8,128)(2,1)} custom-call(bf16[1024,768]{1,0:T(8,128)(2,1)} %get-tuple-element.106.q_ref, bf16[1024,768]{1,0:T(8,128)(2,1)} %get-tuple-element.107.k_ref, bf16[1024,768]{1,0:T(8,128)(2,1)} %get-tuple-element.108.v_ref, bf16[1024,768]{1,0:T(8,128)(2,1)} %get-tuple-element.134.g_ref, ...), custom_call_target="tpu_custom_call" | custom-call | flops 1000000 | bytes 100000 | tf_op jit(solution)/shard_map/attention_back/pallas_call | solution.py:161
  253.9 6.4 %weight_grads.3 = (bf16[3,384,384]{2,1,0:T(8,128)(2,1)}, bf16[3,384,384]{2,1,0:T(8,128)(2,1)}) custom-call(s32[1]{0:T(128)} %bitcast.3.core_ref, bf16[768,1024]{1,0:T(8,128)(2,1)} %get-tuple-element.133.refs_2_.refs_0_, bf16[3,1024,384]{2,1,0:T(8,128)(2,1)} %attention_back.3.refs_1_.right_ref), custom_call_target="tpu_custom_call" | custom-call | flops 1000000 | bytes 100000 | tf_op jit(solution)/shard_map/weight_grads/pallas_call | solution.py:640
  264.1 10.8 %first_back.1 = (f32[1024,768]{1,0:T(8,128)}, f32[2,768]{1,0:T(2,128)}) custom-call(bf16[3,1024,384]{2,1,0:T(8,128)(2,1)} %attention_back.2.refs_3_.left_ref, bf16[3,1024,384]{2,1,0:T(8,128)(2,1)} %attention_back.3.refs_1_.right_ref, bf16[1024,768]{1,0:T(8,128)(2,1)} %tokens_ref.2, f32[1024,768]{1,0:T(8,128)} %get-tuple-element.152.resid_ref, ...), custom_call_target="tpu_custom_call" | custom-call | flops 1000000 | bytes 100000 | tf_op jit(solution)/shard_map/first_back/pallas_call | solution.py:562
  283.8 6.0 %layer_output.1 = bf16[1024,768]{1,0:T(8,128)(2,1)} custom-call(s32[1024,128]{1,0:T(8,128)} %get-tuple-element.114.wide_ref, bf16[1024,768]{1,0:T(8,128)(2,1)} %bitcast.32, f32[1024,768]{1,0:T(8,128)} %get-tuple-element.131.resid_ref, f32[1024,1]{1,0:T(8,128)} %get-tuple-element.164.gate_ref), custom_call_target="tpu_custom_call" | custom-call | flops 1000000 | bytes 100000 | tf_op jit(solution)/shard_map/layer_output/pallas_call | solution.py:587
  316.0 8.4 %collective-permute-done.19 = f32[4,768]{1,0:T(4,128)S(1)} collective-permute-done((f32[4,768]{1,0:T(4,128)S(1)}, f32[4,768]{1,0:T(4,128)S(1)}, u32[]{:S(2)}, u32[]{:S(2)}) %collective-permute-start.19) | collective-permute-done | bytes 12320 | tf_op jit(solution)/shard_map/ppermute | solution.py:698
  331.5 10.1 %collective-permute-done.20 = bf16[960,384]{1,0:T(8,128)(2,1)S(1)} collective-permute-done((bf16[960,384]{1,0:T(8,128)(2,1)S(1)}, bf16[960,384]{1,0:T(8,128)(2,1)S(1)}, u32[]{:S(2)}, u32[]{:S(2)}) %collective-permute-start.20) | collective-permute-done | bytes 737312 | tf_op jit(solution)/shard_map/ppermute | solution.py:698
  342.0 5.6 %collective-permute-done.24 = bf16[288,384]{1,0:T(8,128)(2,1)S(1)} collective-permute-done((bf16[288,384]{1,0:T(8,128)(2,1)S(1)}, bf16[288,384]{1,0:T(8,128)(2,1)S(1)}, u32[]{:S(2)}, u32[]{:S(2)}) %collective-permute-start.24) | collective-permute-done | bytes 221216 | tf_op jit(solution)/shard_map/ppermute | solution.py:698
  350.1 7.2 %collective-permute-done.25 = bf16[576,384]{1,0:T(8,128)(2,1)} collective-permute-done((bf16[576,384]{1,0:T(8,128)(2,1)}, bf16[576,384]{1,0:T(8,128)(2,1)}, u32[]{:S(2)}, u32[]{:S(2)}) %collective-permute-start.25) | collective-permute-done | bytes 442400 | tf_op jit(solution)/shard_map/ppermute | solution.py:698
  365.8 6.3 %assemble.1 = (f32[768,768]{1,0:T(8,128)}, f32[768,768]{1,0:T(8,128)}, f32[768,768]{1,0:T(8,128)}, f32[768,768]{1,0:T(8,128)}) custom-call(s32[1]{0:T(128)} %bitcast.3.core_ref, bf16[5,384,384]{2,1,0:T(8,128)(2,1)} %bitcast.35, bf16[5,384,384]{2,1,0:T(8,128)(2,1)} %bitcast.43, bf16[3,384,384]{2,1,0:T(8,128)(2,1)} %bitcast.36, bf16[3,384,384]{2,1,0:T(8,128)(2,1)} %bitcast.47), custom_call_target="tpu_custom_call" | custom-call | flops 1000000 | bytes 100000 | tf_op jit(solution)/shard_map/assemble/pallas_call | solution.py:682
  (145 shorter events, 85.9 us)
Async XLA Ops:
  6.1 46.6 %all-to-all-start = ((bf16[8,128,768]{2,1,0:T(8,128)(2,1)}), bf16[8,128,768]{2,1,0:T(8,128)(2,1)S(1)}, u32[]{:S(2)}, u32[]{:S(2)}) async-start(bf16[8,128,768]{2,1,0:T(8,128)(2,1)} %bitcast.41), calls=%async_computation | async-start | bytes 3145728 | tf_op jit(solution)/shard_map/all_to_all | solution.py:817
  63.9 42.4 %all-to-all-start.1 = ((bf16[8,128,768]{2,1,0:T(8,128)(2,1)}), bf16[8,128,768]{2,1,0:T(8,128)(2,1)S(1)}, u32[]{:S(2)}, u32[]{:S(2)}) async-start(bf16[8,128,768]{2,1,0:T(8,128)(2,1)} %bitcast.42), calls=%async_computation.1 | async-start | bytes 3145728 | tf_op jit(solution)/shard_map/all_to_all | solution.py:817
  136.8 40.9 %all-to-all-start.2 = ((bf16[8,128,768]{2,1,0:T(8,128)(2,1)}), bf16[8,128,768]{2,1,0:T(8,128)(2,1)S(1)}, u32[]{:S(2)}, u32[]{:S(2)}) async-start(bf16[8,128,768]{2,1,0:T(8,128)(2,1)} %bitcast.40), calls=%async_computation.2 | async-start | bytes 3145728 | tf_op jit(solution)/shard_map/all_to_all | solution.py:817
  159.5 9.3 %collective-permute-start.1 = (bf16[2,768,768]{2,1,0:T(8,128)(2,1)}, bf16[2,768,768]{2,1,0:T(8,128)(2,1)}, u32[]{:S(2)}, u32[]{:S(2)}) collective-permute-start(bf16[2,768,768]{2,1,0:T(8,128)(2,1)} %get-tuple-element.127), channel_id=1, source_target_pairs={{0,8},{8,0},{16,24},{24,16},{1,9},{9,1},{17,25},{25,17},{2,10},{10... | collective-permute-start | bytes 7077896 | tf_op jit(solution)/shard_map/ppermute | solution.py:698
  177.7 35.5 %collective-permute-start.2 = (bf16[1,768,768]{2,1,0:T(8,128)(2,1)}, bf16[1,768,768]{2,1,0:T(8,128)(2,1)}, u32[]{:S(2)}, u32[]{:S(2)}) collective-permute-start(bf16[1,768,768]{2,1,0:T(8,128)(2,1)} %bitcast.13), channel_id=1, source_target_pairs={{0,16},{8,24},{16,0},{24,8},{1,17},{9,25},{17,1},{25,9},{2,18},{10... | collective-permute-start | bytes 3538952 | tf_op jit(solution)/shard_map/ppermute | solution.py:698
  179.2 74.8 %all-to-all-start.3 = ((bf16[8,128,768]{2,1,0:T(8,128)(2,1)}), bf16[8,128,768]{2,1,0:T(8,128)(2,1)S(1)}, u32[]{:S(2)}, u32[]{:S(2)}) async-start(bf16[8,128,768]{2,1,0:T(8,128)(2,1)} %bitcast.39), calls=%async_computation.3 | async-start | bytes 3145728 | tf_op jit(solution)/shard_map/all_to_all | solution.py:817
  229.6 24.3 %collective-permute-start.4 = (bf16[960,384]{1,0:T(8,128)(2,1)}, bf16[960,384]{1,0:T(8,128)(2,1)}, u32[]{:S(2)}, u32[]{:S(2)}) collective-permute-start(bf16[960,384]{1,0:T(8,128)(2,1)} %get-tuple-element.142), channel_id=1, source_target_pairs={{0,1},{1,0},{2,3},{3,2},{4,5},{5,4},{6,7},{7,6},{8,9},{9,8},{10,11... | collective-permute-start | bytes 2211848 | tf_op jit(solution)/shard_map/ppermute | solution.py:698
  231.6 43.3 %collective-permute-start.7 = (bf16[1,768,768]{2,1,0:T(8,128)(2,1)}, bf16[1,768,768]{2,1,0:T(8,128)(2,1)S(1)}, u32[]{:S(2)}, u32[]{:S(2)}) collective-permute-start(bf16[1,768,768]{2,1,0:T(8,128)(2,1)} %bitcast.51), channel_id=1, source_target_pairs={{0,16},{8,24},{16,0},{24,8},{1,17},{9,25},{17,1},{25,9},{2,18},{10... | collective-permute-start | bytes 3538952 | tf_op jit(solution)/shard_map/ppermute | solution.py:698
  260.3 14.7 %collective-permute-start.6 = (bf16[1152,384]{1,0:T(8,128)(2,1)}, bf16[1152,384]{1,0:T(8,128)(2,1)S(1)}, u32[]{:S(2)}, u32[]{:S(2)}) collective-permute-start(bf16[1152,384]{1,0:T(8,128)(2,1)} %bitcast.52), channel_id=1, source_target_pairs={{0,8},{8,0},{16,24},{24,16},{1,9},{9,1},{17,25},{25,17},{2,10},{10... | collective-permute-start | bytes 2654216 | tf_op jit(solution)/shard_map/ppermute | solution.py:698
  262.7 12.3 %collective-permute-start.5 = (bf16[480,384]{1,0:T(8,128)(2,1)}, bf16[480,384]{1,0:T(8,128)(2,1)S(1)}, u32[]{:S(2)}, u32[]{:S(2)}) collective-permute-start(bf16[480,384]{1,0:T(8,128)(2,1)} %get-tuple-element.147), channel_id=1, source_target_pairs={{0,2},{1,3},{2,0},{3,1},{4,6},{5,7},{6,4},{7,5},{8,10},{9,11},{10,... | collective-permute-start | bytes 1105928 | tf_op jit(solution)/shard_map/ppermute | solution.py:698
  278.4 14.4 %collective-permute-start.9 = (bf16[576,384]{1,0:T(8,128)(2,1)}, bf16[576,384]{1,0:T(8,128)(2,1)S(1)}, u32[]{:S(2)}, u32[]{:S(2)}) collective-permute-start(bf16[576,384]{1,0:T(8,128)(2,1)} %get-tuple-element.160), channel_id=1, source_target_pairs={{0,16},{8,24},{16,0},{24,8},{1,17},{9,25},{17,1},{25,9},{2,18},{10... | collective-permute-start | bytes 1327112 | tf_op jit(solution)/shard_map/ppermute | solution.py:698
  281.3 11.5 %collective-permute-start.8 = (bf16[240,384]{1,0:T(8,128)(2,1)}, bf16[240,384]{1,0:T(8,128)(2,1)S(1)}, u32[]{:S(2)}, u32[]{:S(2)}) collective-permute-start(bf16[240,384]{1,0:T(8,128)(2,1)} %get-tuple-element.157), channel_id=1, source_target_pairs={{0,4},{1,5},{2,6},{3,7},{4,0},{5,1},{6,2},{7,3},{8,12},{9,13},{10,... | collective-permute-start | bytes 552968 | tf_op jit(solution)/shard_map/ppermute | solution.py:698
  283.7 6.1 %collective-permute-start.10 = (f32[4,768]{1,0:T(4,128)S(1)}, f32[4,768]{1,0:T(4,128)S(1)}, u32[]{:S(2)}, u32[]{:S(2)}) collective-permute-start(f32[4,768]{1,0:T(4,128)S(1)} %pad_maximum_fusion.7), channel_id=1, source_target_pairs={{0,8},{8,0},{16,24},{24,16},{1,9},{9,1},{17,25},{25,17},{2,10},{10... | collective-permute-start | bytes 36872 | tf_op jit(solution)/shard_map/ppermute | solution.py:698
  292.8 7.4 %collective-permute-start.11 = (bf16[240,384]{1,0:T(8,128)(2,1)S(1)}, bf16[240,384]{1,0:T(8,128)(2,1)S(1)}, u32[]{:S(2)}, u32[]{:S(2)}) collective-permute-start(bf16[240,384]{1,0:T(8,128)(2,1)S(1)} %add_convert_fusion.1), channel_id=1, source_target_pairs={{0,16},{8,24},{16,0},{24,8},{1,17},{9,25},{17,1},{25,9},{2,18},{10... | collective-permute-start | bytes 552968 | tf_op jit(solution)/shard_map/ppermute | solution.py:698
  296.2 7.3 %collective-permute-start.12 = (bf16[288,384]{1,0:T(8,128)(2,1)}, bf16[288,384]{1,0:T(8,128)(2,1)S(1)}, u32[]{:S(2)}, u32[]{:S(2)}) collective-permute-start(bf16[288,384]{1,0:T(8,128)(2,1)} %get-tuple-element.171), channel_id=1, source_target_pairs={{0,1},{1,0},{2,3},{3,2},{4,5},{5,4},{6,7},{7,6},{8,9},{9,8},{10,11... | collective-permute-start | bytes 663560 | tf_op jit(solution)/shard_map/ppermute | solution.py:698
  303.5 9.6 %collective-permute-start.14 = (bf16[240,384]{1,0:T(8,128)(2,1)S(1)}, bf16[240,384]{1,0:T(8,128)(2,1)S(1)}, u32[]{:S(2)}, u32[]{:S(2)}) collective-permute-start(bf16[240,384]{1,0:T(8,128)(2,1)S(1)} %add_convert_fusion), channel_id=1, source_target_pairs={{0,4},{1,5},{2,6},{3,7},{4,0},{5,1},{6,2},{7,3},{8,12},{9,13},{10,... | collective-permute-start | bytes 552968 | tf_op jit(solution)/shard_map/ppermute | solution.py:698
  305.9 7.2 %collective-permute-start.15 = (bf16[144,384]{1,0:T(8,128)(2,1)}, bf16[144,384]{1,0:T(8,128)(2,1)S(1)}, u32[]{:S(2)}, u32[]{:S(2)}) collective-permute-start(bf16[144,384]{1,0:T(8,128)(2,1)} %get-tuple-element.176), channel_id=1, source_target_pairs={{0,2},{1,3},{2,0},{3,1},{4,6},{5,7},{6,4},{7,5},{8,10},{9,11},{10,... | collective-permute-start | bytes 331784 | tf_op jit(solution)/shard_map/ppermute | solution.py:698
  313.2 11.3 %collective-permute-start.17 = (bf16[480,384]{1,0:T(8,128)(2,1)S(1)}, bf16[480,384]{1,0:T(8,128)(2,1)S(1)}, u32[]{:S(2)}, u32[]{:S(2)}) collective-permute-start(bf16[480,384]{1,0:T(8,128)(2,1)S(1)} %pad_maximum_fusion.4), channel_id=1, source_target_pairs={{0,2},{1,3},{2,0},{3,1},{4,6},{5,7},{6,4},{7,5},{8,10},{9,11},{10,... | collective-permute-start | bytes 1105928 | tf_op jit(solution)/shard_map/ppermute | solution.py:698
  313.3 11.2 %collective-permute-start.18 = (bf16[144,384]{1,0:T(8,128)(2,1)S(1)}, bf16[144,384]{1,0:T(8,128)(2,1)S(1)}, u32[]{:S(2)}, u32[]{:S(2)}) collective-permute-start(bf16[144,384]{1,0:T(8,128)(2,1)S(1)} %add_convert_fusion.3), channel_id=1, source_target_pairs={{0,4},{1,5},{2,6},{3,7},{4,0},{5,1},{6,2},{7,3},{8,12},{9,13},{10,... | collective-permute-start | bytes 331784 | tf_op jit(solution)/shard_map/ppermute | solution.py:698
  316.0 8.4 %collective-permute-start.19 = (f32[4,768]{1,0:T(4,128)S(1)}, f32[4,768]{1,0:T(4,128)S(1)}, u32[]{:S(2)}, u32[]{:S(2)}) collective-permute-start(f32[4,768]{1,0:T(4,128)S(1)} %add.77), channel_id=1, source_target_pairs={{0,2},{1,3},{2,0},{3,1},{4,6},{5,7},{6,4},{7,5},{8,10},{9,11},{10,... | collective-permute-start | bytes 36872 | tf_op jit(solution)/shard_map/ppermute | solution.py:698
  324.7 16.9 %collective-permute-start.20 = (bf16[960,384]{1,0:T(8,128)(2,1)S(1)}, bf16[960,384]{1,0:T(8,128)(2,1)S(1)}, u32[]{:S(2)}, u32[]{:S(2)}) collective-permute-start(bf16[960,384]{1,0:T(8,128)(2,1)S(1)} %pad_maximum_fusion.2), channel_id=1, source_target_pairs={{0,1},{1,0},{2,3},{3,2},{4,5},{5,4},{6,7},{7,6},{8,9},{9,8},{10,11... | collective-permute-start | bytes 2211848 | tf_op jit(solution)/shard_map/ppermute | solution.py:698
  325.1 6.4 %collective-permute-start.21 = (bf16[144,384]{1,0:T(8,128)(2,1)S(1)}, bf16[144,384]{1,0:T(8,128)(2,1)S(1)}, u32[]{:S(2)}, u32[]{:S(2)}) collective-permute-start(bf16[144,384]{1,0:T(8,128)(2,1)S(1)} %add_convert_fusion.2), channel_id=1, source_target_pairs={{0,2},{1,3},{2,0},{3,1},{4,6},{5,7},{6,4},{7,5},{8,10},{9,11},{10,... | collective-permute-start | bytes 331784 | tf_op jit(solution)/shard_map/ppermute | solution.py:698
  348.5 8.8 %collective-permute-start.25 = (bf16[576,384]{1,0:T(8,128)(2,1)}, bf16[576,384]{1,0:T(8,128)(2,1)}, u32[]{:S(2)}, u32[]{:S(2)}) collective-permute-start(bf16[576,384]{1,0:T(8,128)(2,1)} %pad_maximum_fusion.3), channel_id=1, source_target_pairs={{0,16},{8,24},{16,0},{24,8},{1,17},{9,25},{17,1},{25,9},{2,18},{10... | collective-permute-start | bytes 1327112 | tf_op jit(solution)/shard_map/ppermute | solution.py:698
  350.0 14.4 %collective-permute-start.23 = (bf16[1920,384]{1,0:T(8,128)(2,1)S(1)}, bf16[1920,384]{1,0:T(8,128)(2,1)S(1)}, u32[]{:S(2)}, u32[]{:S(2)}) collective-permute-start(bf16[1920,384]{1,0:T(8,128)(2,1)S(1)} %pad_maximum_fusion), channel_id=1, source_target_pairs={{0,8},{8,0},{16,24},{24,16},{1,9},{9,1},{17,25},{25,17},{2,10},{10... | collective-permute-start | bytes 4423688 | tf_op jit(solution)/shard_map/ppermute | solution.py:698
  (33 other events, 181.1 us)
where the time goes:
time: 373 us; the launch traced here: 372 us
  Pallas kernels  215 us (58%)
  waiting for transfers between devices  95.7 us (26%)
  starting transfers between devices  43.7 us (12%)
  local copies, waits for them, and re-layouts  8.84 us (2%)
  other arithmetic  8.17 us (2%)
    ppermute x27, waiting for transfers between devices, swap(): return lax.ppermute(value, axis, [(i, i ^ bit) for i in range(size)])  56 us
    pallas_call x2, Pallas kernels, attention_back(): pl.pallas_call(functools.partial(attention_back_kernel, block=block), gri...  42.2 us
    all_to_all x4, waiting for transfers between devices, exchange(): lax.all_to_all(rows, 'expert', split_axis=0, concat_axis=0, tiled=True)  39.7 us
    pallas_call x1, Pallas kernels, expert(): pl.pallas_call(expert_kernel, grid=(hidden // tile,), in_specs=[whole, wh...  29.3 us
    pallas_call x1, Pallas kernels, attention(): pl.pallas_call(functools.partial(attention_kernel, block=block), grid=(pa...  29.3 us
    ppermute x27, starting transfers between devices, swap(): return lax.ppermute(value, axis, [(i, i ^ bit) for i in range(size)])  22.9 us
    pallas_call x8, Pallas kernels, add_split(): pl.pallas_call(add_split_kernel, grid_spec=pltpu.PrefetchScalarGridSpec(n...  22.7 us
    all_to_all x4, starting transfers between devices, exchange(): lax.all_to_all(rows, 'expert', split_axis=0, concat_axis=0, tiled=True)  20.8 us
  transfers between devices with their start and end apart: 31, of which 14 were waited for; matrix products, arithmetic and copies ran while one was open for 3% of the time, Pallas kernels for 43%

commit v1 on v0

--- a/solution.py
+++ b/solution.py
@@ -53,28 +53,26 @@
         bias_ref[...] = jnp.where(key <= query, 0.0, -1e30)
 
 
-def attention_kernel(q_ref, k_ref, v_ref, o_ref, lse_ref, bias_ref, *, block):
-    causal_bias(bias_ref, 1)
+def attention_kernel(q_ref, k_ref, v_ref, o_ref, *refs, block):
+    *probs_refs, bias_ref = refs
+    causal_bias(bias_ref, 0)
     parity = pl.program_id(1)
-    length = q_ref.shape[0]
     queries = q_ref[...] * head_mask(parity, HEAD**-0.5)
     values = v_ref[...] * head_mask(parity, 1.0)
     outs = []
-    for index in range(length // block):
+    for index, probs_ref in enumerate(probs_refs):
         first, finish = index * block, (index + 1) * block
-        scores = contract(queries[first:finish], k_ref[:finish, :], 1, 1)
-        diagonal = scores[:, first:] + bias_ref[...]
+        scores = contract(k_ref[:finish, :], queries[first:finish], 1, 1)
+        diagonal = scores[first:] + bias_ref[...]
         if index:
-            scores = jnp.concatenate([scores[:, :first], diagonal], axis=1)
+            scores = jnp.concatenate([scores[:first], diagonal], axis=0)
         else:
             scores = diagonal
-        top = jnp.max(scores, axis=1, keepdims=True)
-        shifted = jnp.exp(scores - top)
-        total = jnp.sum(shifted, axis=1, keepdims=True)
+        shifted = jnp.exp(scores - jnp.max(scores, axis=0, keepdims=True))
+        total = jnp.sum(shifted, axis=0, keepdims=True)
         probs = (shifted * (1.0 / total)).astype(BF16)
-        outs.append(contract(probs, values[:finish], 1, 0).astype(BF16))
-        lse = jnp.broadcast_to(top + jnp.log(total), (block, LANES))
-        lse_ref[0, :, first:finish] = jnp.transpose(lse)[0:1, :]
+        probs_ref[0] = probs
+        outs.append(contract(probs, values[:finish], 0, 0).astype(BF16))
     mixed = jnp.concatenate(outs, axis=0)
 
     @pl.when(parity == 0)
@@ -90,31 +88,32 @@
     length, width = queries.shape
     pairs = width // LANES
     block = min(256, length)
+    finishes = range(block, length + 1, block)
     spec = pl.BlockSpec((length, LANES), lambda pair, parity: (0, pair))
-    return pl.pallas_call(
+    mixed, *probs = pl.pallas_call(
         functools.partial(attention_kernel, block=block),
         grid=(pairs, 2),
         in_specs=[spec, spec, spec],
-        out_specs=[
-            spec,
-            pl.BlockSpec((1, 1, length), lambda pair, parity: (pair * 2 + parity, 0, 0)),
-        ],
-        out_shape=[
-            jax.ShapeDtypeStruct((length, width), BF16),
-            jax.ShapeDtypeStruct((2 * pairs, 1, length), F32),
-        ],
+        out_specs=[spec]
+        + [
+            pl.BlockSpec((1, finish, block), lambda pair, parity: (pair * 2 + parity, 0, 0))
+            for finish in finishes
+        ],
+        out_shape=[jax.ShapeDtypeStruct((length, width), BF16)]
+        + [jax.ShapeDtypeStruct((2 * pairs, finish, block), BF16) for finish in finishes],
         scratch_shapes=[pltpu.VMEM((block, block), F32)],
         cost_estimate=LIGHT,
         name="attention",
     )(queries, keys, values)
+    return mixed, probs
 
 
 def attention_back_kernel(
-    q_ref, k_ref, v_ref, g_ref, lse_ref, grads_ref, dk_sum, dv_sum, bias_ref, *, block
+    core_ref, q_ref, k_ref, v_ref, g_ref, o_ref, turned_ref, *refs, block, blocks
 ):
-    causal_bias(bias_ref, 0)
+    probs_refs = refs[:blocks]
+    grads_ref, send_ref, keep_ref, dk_sum, dv_sum = refs[-5:]
     parity = pl.program_id(1)
-    length = q_ref.shape[0]
     scale_mask = head_mask(parity, HEAD**-0.5)
     queries = q_ref[...] * scale_mask
     grads = g_ref[...] * head_mask(parity, 1.0)
@@ -122,19 +121,15 @@
     dk_sum[...] = jnp.zeros_like(dk_sum)
     dv_sum[...] = jnp.zeros_like(dv_sum)
     dq_parts = []
-    for index in range(length // block):
+    for index, probs_ref in enumerate(probs_refs):
         first, finish = index * block, (index + 1) * block
-        scores = contract(k_ref[:finish, :], queries[first:finish], 1, 1)
-        diagonal = scores[first:] + bias_ref[...]
-        if index:
-            scores = jnp.concatenate([scores[:first], diagonal], axis=0)
-        else:
-            scores = diagonal
-        probs = jnp.exp(scores - lse_ref[0, :, first:finish])
-        dv_sum[:finish, :] += contract(probs.astype(BF16), grads[first:finish], 1, 0)
-        grad_probs = contract(v_ref[:finish, :], grads[first:finish], 1, 1)
-        delta = jnp.sum(probs * grad_probs, axis=0, keepdims=True)
-        grad_scores = (probs * (grad_probs - delta)).astype(BF16)
+        probs = probs_ref[0]
+        some = grads[first:finish]
+        dv_sum[:finish, :] += contract(probs, some, 1, 0)
+        grad_probs = contract(v_ref[:finish, :], some, 1, 1)
+        shares = some.astype(F32) * o_ref[first:finish, :].astype(F32)
+        delta = jnp.sum(jnp.transpose(shares), axis=0, keepdims=True)
+        grad_scores = (probs.astype(F32) * (grad_probs - delta)).astype(BF16)
         dk_sum[:finish, :] += contract(grad_scores, queries[first:finish], 1, 0)
         dq_parts.append(contract(grad_scores, keys_scaled[:finish], 0, 0).astype(BF16))
     parts = (
@@ -150,32 +145,65 @@
 
     @pl.when(parity == 1)
     def _():
-        for index, part in enumerate(parts):
-            grads_ref[index] = grads_ref[index] + part
-
-
-def attention_back(queries, keys, values, grads, lse, start, pairs):
-    length = queries.shape[0]
-    block = min(256, length)
+        whole = [grads_ref[index] + part for index, part in enumerate(parts)]
+        for index, part in enumerate(whole):
+            grads_ref[index] = part
+        weight_parts(core_ref, turned_ref[...], jnp.concatenate(whole, axis=1), send_ref, keep_ref)
+
+
+def weight_parts(core_ref, turned, grads, send_ref, keep_ref):
+    product = contract(turned, grads, 1, 0).astype(BF16)
+    rows = send_ref.shape[1]
+
+    def write(upper, lower):
+        for index in range(grads.shape[1] // LANES):
+            columns = slice(index * LANES, (index + 1) * LANES)
+            upper[index] = product[:rows, columns]
+            lower[index] = product[rows:, columns]
+
+    @pl.when(core_ref[0] == 0)
+    def _():
+        write(keep_ref, send_ref)
+
+    @pl.when(core_ref[0] != 0)
+    def _():
+        write(send_ref, keep_ref)
+
+
+SCALAR = pl.BlockSpec(memory_space=pltpu.SMEM)
+
+
+def attention_back(core, queries, keys, values, grads, mixed, turned, probs, start, pairs, units):
+    length, width = queries.shape
+    block = probs[0].shape[2]
     spec = pl.BlockSpec((length, LANES), lambda pair, parity: (0, start + pair))
-    return pl.pallas_call(
-        functools.partial(attention_back_kernel, block=block),
+    whole = pl.BlockSpec((width, length), lambda pair, parity: (0, 0))
+    ahead = 0 if units is None else units[0].shape[0] // 3 - pairs
+    shape = jax.ShapeDtypeStruct((3 * (ahead + pairs), width // 2, LANES), BF16)
+    unit = pl.BlockSpec((3, width // 2, LANES), lambda pair, parity: (ahead + pair, 0, 0))
+    args = [core, queries, keys, values, grads, mixed, turned, *probs]
+    alias = {}
+    if units is not None:
+        alias = {len(args): 1, len(args) + 1: 2}
+        args += units
+    return pl.pallas_call(
+        functools.partial(attention_back_kernel, block=block, blocks=len(probs)),
         grid=(pairs, 2),
-        in_specs=[
-            spec,
-            spec,
-            spec,
-            spec,
+        in_specs=[SCALAR, spec, spec, spec, spec, spec, whole]
+        + [
             pl.BlockSpec(
-                (1, 1, length), lambda pair, parity: ((start + pair) * 2 + parity, 0, 0)
-            ),
-        ],
-        out_specs=pl.BlockSpec((3, length, LANES), lambda pair, parity: (0, 0, pair)),
-        out_shape=jax.ShapeDtypeStruct((3, length, pairs * LANES), BF16),
-        scratch_shapes=[pltpu.VMEM((length, LANES), F32)] * 2 + [pltpu.VMEM((block, block), F32)],
+                (1, *part.shape[1:]), lambda pair, parity: ((start + pair) * 2 + parity, 0, 0)
+            )
+            for part in probs
+        ]
+        + [pl.BlockSpec(memory_space=pl.ANY)] * len(alias),
+        out_specs=[pl.BlockSpec((3, length, LANES), lambda pair, parity: (0, 0, pair)), unit, unit],
+        out_shape=[jax.ShapeDtypeStruct((3, length, pairs * LANES), BF16), shape, shape],
+        input_output_aliases=alias,
+        scratch_shapes=[pltpu.VMEM((length, LANES), F32)] * 2,
         cost_estimate=LIGHT,
         name="attention_back",
-    )(queries, keys, values, grads, lse)
+    )(*args)
 
 
 def gelu_parts(value):
@@ -479,8 +507,8 @@
 
 
 def second_back_kernel(
-    wide_ref, back_ref, resid_ref, cot_ref, gain_ref, weight_ref,
-    grad_ref, low_ref, mixed_ref, sums_ref,
+    core_ref, wide_ref, back_ref, resid_ref, cot_ref, gain_ref, weight_ref, turned_ref,
+    grad_ref, mixed_ref, sums_ref, send_ref, keep_ref, total_ref,
 ):
     grad = gathered(wide_ref, back_ref)
     _, xhat, scale = normalize(resid_ref[...], gain_ref[...], gain_ref[...])
@@ -499,35 +527,57 @@
     grad = cot_ref[...].astype(F32) + normalize_back(grad, xhat, scale, gain_ref[...])
     grad_ref[...] = grad
     low = grad.astype(BF16)
-    low_ref[...] = low
     mixed_ref[...] = contract(low, weight_ref[...], 1, 1).astype(BF16)
-
-
-def second_back(wide, back, resid, cotangent, gain, weight):
+    product = contract(turned_ref[...], low, 1, 0)
+
+    @pl.when(pl.program_id(0) == 0)
+    def _():
+        total_ref[...] = product
+
+    @pl.when(pl.program_id(0) > 0)
+    def _():
+        total_ref[...] += product
+
+    @pl.when(pl.program_id(0) == pl.num_programs(0) - 1)
+    def _():
+        rows = send_ref.shape[1]
+        for index in range(send_ref.shape[0]):
+            columns = slice(index * LANES, (index + 1) * LANES)
+            for half, out in ((1 - core_ref[0], send_ref), (core_ref[0], keep_ref)):
+                at = pl.ds(pl.multiple_of(half * rows, rows), rows)
+                out[index] = total_ref[at, columns].astype(BF16)
+
+
+def second_back(core, wide, back, resid, cotangent, gain, weight, turned, units):
     length, width = resid.shape
     rows = pl.BlockSpec((ROWS, width), lambda i: (i, 0))
-    low = jax.ShapeDtypeStruct((length, width), BF16)
+    own = const(width // LANES, width // 2, LANES)
+    shape = jax.ShapeDtypeStruct((units, width // 2, LANES), BF16)
     return pl.pallas_call(
         second_back_kernel,
         grid=(length // ROWS,),
         in_specs=[
+            SCALAR,
             pl.BlockSpec((ROWS, LANES), lambda i: (i, 0)),
             const(*back.shape),
             rows,
             rows,
             const(1, width),
             const(width, width),
-        ],
-        out_specs=[rows, rows, rows, const(2, width)],
+            pl.BlockSpec((width, ROWS), lambda i: (0, i)),
+        ],
+        out_specs=[rows, rows, const(2, width), own, own],
         out_shape=[
             jax.ShapeDtypeStruct((length, width), F32),
-            low,
-            low,
+            jax.ShapeDtypeStruct((length, width), BF16),
             jax.ShapeDtypeStruct((2, width), F32),
-        ],
+            shape,
+            shape,
+        ],
+        scratch_shapes=[pltpu.VMEM((width, width), F32)],
         cost_estimate=LIGHT,
         name="second_back",
-    )(wide, back, resid, cotangent, gain, weight)
+    )(core, wide, back, resid, cotangent, gain, weight, turned)
 
 
 def first_back_kernel(
@@ -600,68 +650,19 @@
     )(wide, produced, resid, gate)
 
 
-def weight_grads_kernel(core_ref, *refs, sources):
-    lefts, rights, send_ref, keep_ref = refs[:-2:2], refs[1:-2:2], refs[-2], refs[-1]
-    matrix = pl.program_id(0)
-    rows = send_ref.shape[1]
-    first = 0
-    for left, right, count in zip(lefts, rights, sources):
-        @pl.when((matrix >= first) & (matrix < first + count))
-        def _(left=left, right=right):
-            grad = right[0] if len(right.shape) == 3 else right[...]
-            for half, out in ((1 - core_ref[0], send_ref), (core_ref[0], keep_ref)):
-                turned = left[pl.ds(pl.multiple_of(half * rows, rows), rows), :]
-                out[0] = contract(turned, grad, 1, 0).astype(BF16)
-
-        first += count
-
-
-def weight_grads(core, side, *sources):
-    width, length = sources[0][0].shape
-    counts, specs, args = [], [], []
-    for turned, grads in sources:
-        counts.append(3 if grads.ndim == 3 else grads.shape[1] // side)
-    total = sum(counts)
-    first = 0
-    for (turned, grads), count in zip(sources, counts):
-        def which(step, first=first, count=count):
-            return jnp.clip(step - first, 0, count - 1)
-
-        specs.append(pl.BlockSpec((width, length), lambda i, core: (0, 0)))
-        if grads.ndim == 3:
-            specs.append(
-                pl.BlockSpec((1, length, side), lambda i, core, which=which: (which(i), 0, 0))
-            )
-        else:
-            specs.append(pl.BlockSpec((length, side), lambda i, core, which=which: (0, which(i))))
-        args += [turned, grads]
-        first += count
-    shape = jax.ShapeDtypeStruct((total, width // 2, side), BF16)
-    send, keep = pl.pallas_call(
-        functools.partial(weight_grads_kernel, sources=tuple(counts)),
-        grid_spec=pltpu.PrefetchScalarGridSpec(
-            num_scalar_prefetch=1,
-            grid=(total,),
-            in_specs=specs,
-            out_specs=[pl.BlockSpec((1, width // 2, side), lambda i, core: (i, 0, 0))] * 2,
-        ),
-        out_shape=[shape, shape],
-        cost_estimate=LIGHT,
-        name="weight_grads",
-    )(core, *args)
-    return send.reshape(-1, side), keep.reshape(-1, side)
-
-
 def assemble_kernel(core_ref, early_mine, early_other, late_mine, late_other, *outs):
     mine = pl.program_id(0) == core_ref[0]
-    side = early_mine.shape[2]
+    columns = outs[0].shape[1] // LANES
 
     def write(early, late):
-        outs[0][:, :side] = early[0].astype(F32)
-        outs[0][:, side:] = early[1].astype(F32)
-        for index in range(3):
-            outs[1 + index][:, :side] = early[2 + index].astype(F32)
-            outs[1 + index][:, side:] = late[index].astype(F32)
+        for index in range(columns):
+            outs[0][:, index * LANES : (index + 1) * LANES] = early[index].astype(F32)
+        for part in (early, late):
+            first = columns if part is early else 0
+            pair = 0 if part is early else (early.shape[0] - columns) // 3
+            for unit in range(first, part.shape[0]):
+                at = pair + (unit - first) // 3
+                outs[1 + (unit - first) % 3][:, at * LANES : (at + 1) * LANES] = part[unit].astype(F32)
 
     @pl.when(mine)
     def _():
@@ -673,9 +674,8 @@
 
 
 def assemble(core, early_mine, early_other, late_mine, late_other, width):
-    side = early_mine.shape[1]
     args = [
-        part.reshape(-1, width // 2, side)
+        part.reshape(-1, width // 2, LANES)
         for part in (early_mine, early_other, late_mine, late_other)
     ]
     out = jax.ShapeDtypeStruct((width, width), F32)
@@ -849,7 +849,7 @@
     cots = exchange(cots.reshape(peers, -1, width)).reshape(slots, width)
 
     normed_turned, queries, keys, values = project(tokens, first_gain, first_bias, weights)
-    mixed, lse = attention(queries, keys, values)
+    mixed, probs = attention(queries, keys, values)
     mixed, cots = tie((mixed, cots))
     resid, gate, mixed_turned, rows = branch(
         mixed, tokens, output_weight, second_gain, second_bias, centroids, routing, slot, slots
@@ -875,29 +875,31 @@
     down_got = swap(down_send, *chips[0])
     produced = exchange(produced.reshape(peers, -1, width))
 
-    grad_resid, grad_branch, grad_mixed, second_sums = second_back(
-        wide, returned, resid, cotangent, second_gain, output_weight
-    )
-
     pairs = width // LANES
     split = pairs // 2
-    side = split * LANES
+    grad_resid, grad_mixed, second_sums, *units = second_back(
+        core, wide, returned, resid, cotangent, second_gain, output_weight, mixed_turned,
+        pairs + 3 * split,
+    )
+
     cross = stages("expert", 1, 1 << 20)
     apart = stages("dp", 2, 1 << 20)
-    left = attention_back(queries, keys, values, grad_mixed, lse, 0, split)
-    left, up_got = tie((left, up_got))
-    send, keep = weight_grads(core, side, (mixed_turned, grad_branch), (normed_turned, left))
-    early = Sum(keep, send, [("dp", 1)] + cross + apart)
+    back = functools.partial(
+        attention_back, core, queries, keys, values, grad_mixed, mixed, normed_turned
+    )
+    left, send, keep = back(probs, 0, split, units)
+    left, send, keep, up_got = tie((left, send, keep, up_got))
+    early = Sum(keep.reshape(-1, LANES), send.reshape(-1, LANES), [("dp", 1)] + cross + apart)
     advance([early])
-    early.send, lse = tie((early.send, lse))
-    right = attention_back(queries, keys, values, grad_mixed, lse, split, pairs - split)
-    right, produced = advance([early], right, produced)
+    early.send, *probs = tie((early.send, *probs))
+    right, send, keep = back(probs, split, pairs - split, None)
+    right, send, keep, produced = advance([early], right, send, keep, produced)
     produced = produced.reshape(slots, width)
-    send, keep = weight_grads(core, side, (normed_turned, right))
-    send, keep = tie((send, keep))
+    late = Sum(keep.reshape(-1, LANES), send.reshape(-1, LANES), [("dp", 1)] + apart + cross)
+    layer_out = layer_output(wide, produced, resid, gate)
+    layer_out, down_got = advance([early, late], layer_out, down_got)
     grad_tokens, first_sums = first_back(left, right, tokens, grad_resid, first_gain, weights)
-    late = Sum(keep, send, [("dp", 1)] + apart + cross)
-    grad_tokens, first_sums, down_got = advance([early, late], grad_tokens, first_sums, down_got)
+    grad_tokens, first_sums = advance([early, late], grad_tokens, first_sums)
     grad_up = up_keep.astype(F32) + up_got.astype(F32)
     grad_down = down_keep.astype(F32) + down_got.astype(F32)
     for stage in chips[1:]:
@@ -908,8 +910,7 @@
     grad_up, grad_down = (value.reshape(value.shape[1:])[None] for value in (grad_up, grad_down))
     small = jnp.concatenate([first_sums, second_sums], axis=0)
     small = Sum(small, small, stages("dp", 1, 1 << 20) + cross, plus=add, split=False)
-    layer_out = layer_output(wide, produced, resid, gate)
-    layer_out = advance([early, late, small], layer_out)
+    grad_up, grad_down = advance([early, late, small], grad_up, grad_down)
     while early.steps or late.steps or small.steps:
         advance([early, late, small])
     early, late, small = early.keep, late.keep, small.keep

time: 373 us -> 350 us (0.938)
  Pallas kernels: 215 us -> 194 us
  waiting for transfers between devices: 95.7 us -> 91 us
  starting transfers between devices: 43.7 us -> 48 us
    pallas_call x5 -> x3, Pallas kernels: 66.5 us -> 49.3 us  [the longest x2 36.4 us: attention_back(): pl.pallas_call(functools.partial(attention_back_kernel, block=block, bloc...]
    ppermute x27, waiting for transfers between devices: 56 us -> 50.1 us  [swap(): return lax.ppermute(value, axis, [(i, i ^ bit) for i in range(size)])]
    ppermute x27, starting transfers between devices: 22.9 us -> 28.4 us  [swap(): return lax.ppermute(value, axis, [(i, i ^ bit) for i in range(size)])]
  transfers between devices with their start and end apart: 31 -> 31, of which waited for: 14 -> 17; matrix products, arithmetic and copies ran while one was open for 3% -> 3% of each run, Pallas kernels for 43% -> 40%
where the time goes in v1:
time: 350 us; the launch traced here: 349 us
  Pallas kernels  194 us (55%)
  waiting for transfers between devices  91 us (26%)
  starting transfers between devices  48 us (14%)
  local copies, waits for them, and re-layouts  7.78 us (2%)
  other arithmetic  6.6 us (2%)
    ppermute x27, waiting for transfers between devices, swap(): return lax.ppermute(value, axis, [(i, i ^ bit) for i in range(size)])  50.1 us
    all_to_all x4, waiting for transfers between devices, exchange(): lax.all_to_all(rows, 'expert', split_axis=0, concat_axis=0, tiled=True)  41 us
    pallas_call x2, Pallas kernels, attention_back(): pl.pallas_call(functools.partial(attention_back_kernel, block=block, bloc...  36.4 us
    pallas_call x1, Pallas kernels, expert(): pl.pallas_call(expert_kernel, grid=(hidden // tile,), in_specs=[whole, wh...  29.2 us
    ppermute x27, starting transfers between devices, swap(): return lax.ppermute(value, axis, [(i, i ^ bit) for i in range(size)])  28.4 us
    pallas_call x1, Pallas kernels, attention(): pl.pallas_call(functools.partial(attention_kernel, block=block), grid=(pa...  25.7 us
    pallas_call x8, Pallas kernels, add_split(): pl.pallas_call(add_split_kernel, grid_spec=pltpu.PrefetchScalarGridSpec(n...  23 us
    all_to_all x4, starting transfers between devices, exchange(): lax.all_to_all(rows, 'expert', split_axis=0, concat_axis=0, tiled=True)  19.5 us
  transfers between devices with their start and end apart: 31, of which 17 were waited for; matrix products, arithmetic and copies ran while one was open for 3% of the time, Pallas kernels for 40%

profile of v1, /device:TPU:0, one launch (start us, length us, event | category | flops | bytes accessed | tf_op | source)
XLA Modules:
  0.0 348.6 jit_solution(12428360590426217353)
XLA Ops:
  0.6 5.4 %route.1 = (bf16[1024,768]{1,0:T(8,128)(2,1)}, s32[1,1024]{1,0:T(1,128)}, s32[1024,128]{1,0:T(8,128)}) custom-call(s32[1,1024]{1,0:T(1,128)} %bitcast.50, bf16[1024,768]{1,0:T(8,128)(2,1)} %cot_ref.3), custom_call_target="tpu_custom_call" | custom-call | flops 1000000 | bytes 100000 | tf_op jit(solution)/shard_map/route/pallas_call | solution.py:392
  6.1 7.5 %all-to-all-start = ((bf16[8,128,768]{2,1,0:T(8,128)(2,1)}), bf16[8,128,768]{2,1,0:T(8,128)(2,1)S(1)}, u32[]{:S(2)}, u32[]{:S(2)}) async-start(bf16[8,128,768]{2,1,0:T(8,128)(2,1)} %bitcast.42), calls=%async_computation | async-start | bytes 3145728 | tf_op jit(solution)/shard_map/all_to_all | solution.py:817
  15.3 8.2 %project.1 = (bf16[768,1024]{1,0:T(8,128)(2,1)}, bf16[1024,768]{1,0:T(8,128)(2,1)}, bf16[1024,768]{1,0:T(8,128)(2,1)}, bf16[1024,768]{1,0:T(8,128)(2,1)}) custom-call(bf16[1024,768]{1,0:T(8,128)(2,1)} %tokens_ref.2, f32[1,768]{1,0:T(1,128)} %get-tuple-element.243.gain_ref, f32[1,768]{1,0:T(1,128)} %get-tuple-element.242.bias_ref, bf16[768,768]{1,0:T(8,128)(2,1)} %wq_ref.3, ...), custom_call_target="tpu_custom_call" | custom-call | flops 1000000 | bytes 100000 | tf_op jit(solution)/shard_map/project/pallas_call | solution.py:425
  23.5 25.7 %attention.1 = (bf16[1024,768]{1,0:T(8,128)(2,1)}, bf16[12,256,256]{2,1,0:T(8,128)(2,1)}, bf16[12,512,256]{2,1,0:T(8,128)(2,1)}, bf16[12,768,256]{2,1,0:T(8,128)(2,1)}, bf16[12,1024,256]{2,1,0:T(8,128)(2,1)}) custom-call(bf16[1024,768]{1,0:T(8,128)(2,1)} %get-tuple-element.120.q_ref, bf16[1024,768]{1,0:T(8,128)(2,1)} %get-tuple-element.121.k_ref, ...), custom_call_target="tpu_custom_call" | custom-call | flops 1000000 | bytes 100000 | tf_op jit(solution)/shard_map/attention/pallas_call | solution.py:93
  50.6 11.2 %branch.1 = (f32[1024,768]{1,0:T(8,128)}, f32[1024,1]{1,0:T(8,128)}, bf16[768,1024]{1,0:T(8,128)(2,1)}, bf16[1024,768]{1,0:T(8,128)(2,1)}) custom-call(bf16[1024,768]{1,0:T(8,128)(2,1)} %get-tuple-element.126.mixed_ref.o_ref, bf16[1024,768]{1,0:T(8,128)(2,1)} %tokens_ref.2, bf16[768,768]{1,0:T(8,128)(2,1)} %weight_ref.3, ...), custom_call_target="tpu_custom_call" | custom-call | flops 1000000 | bytes 100000 | tf_op jit(solution)/shard_map/branch/pallas_call | solution.py:470
  61.7 4.7 %all-to-all-start.1 = ((bf16[8,128,768]{2,1,0:T(8,128)(2,1)}), bf16[8,128,768]{2,1,0:T(8,128)(2,1)S(1)}, u32[]{:S(2)}, u32[]{:S(2)}) async-start(bf16[8,128,768]{2,1,0:T(8,128)(2,1)} %bitcast.43), calls=%async_computation.1 | async-start | bytes 3145728 | tf_op jit(solution)/shard_map/all_to_all | solution.py:817
  67.8 35.1 %all-to-all-done.1 = bf16[8,128,768]{2,1,0:T(8,128)(2,1)S(1)} async-done(((bf16[8,128,768]{2,1,0:T(8,128)(2,1)}), bf16[8,128,768]{2,1,0:T(8,128)(2,1)S(1)}, u32[]{:S(2)}, u32[]{:S(2)}) %all-to-all-start.1) | async-done | bytes 1572896 | tf_op jit(solution)/shard_map/all_to_all | solution.py:817
  104.0 29.2 %expert.1 = (bf16[1024,768]{1,0:T(8,128)(2,1)}, bf16[1024,768]{1,0:T(8,128)(2,1)}, bf16[1024,768]{1,0:T(8,128)(2,1)}, bf16[1024,3072]{1,0:T(8,128)(2,1)}, bf16[1024,3072]{1,0:T(8,128)(2,1)}) custom-call(bf16[1024,768]{1,0:T(8,128)(2,1)} %bitcast.30, bf16[1024,768]{1,0:T(8,128)(2,1)} %bitcast.34, f32[1,768]{1,0:T(1,128)} %constant_dynamic-slice_fusion.cen_ref, ...), custom_call_target="tpu_custom_call" | custom-call | flops 1000000 | bytes 100000 | tf_op jit(solution)/shard_map/expert/pallas_call | solution.py:260
  133.2 3.8 %all-to-all-start.2 = ((bf16[8,128,768]{2,1,0:T(8,128)(2,1)}), bf16[8,128,768]{2,1,0:T(8,128)(2,1)S(1)}, u32[]{:S(2)}, u32[]{:S(2)}) async-start(bf16[8,128,768]{2,1,0:T(8,128)(2,1)} %bitcast.41), calls=%async_computation.2 | async-start | bytes 3145728 | tf_op jit(solution)/shard_map/all_to_all | solution.py:817
  137.0 18.9 %expert_weights.1 = (bf16[2,768,768]{2,1,0:T(8,128)(2,1)}, bf16[2,768,768]{2,1,0:T(8,128)(2,1)}, bf16[2,768,768]{2,1,0:T(8,128)(2,1)}, bf16[2,768,768]{2,1,0:T(8,128)(2,1)}) custom-call(s32[1]{0:T(128)} %bitcast.2.core_ref, bf16[1024,768]{1,0:T(8,128)(2,1)} %bitcast.31, bf16[1024,768]{1,0:T(8,128)(2,1)} %get-tuple-element.132.dy_ref, ...), custom_call_target="tpu_custom_call" | custom-call | flops 1000000 | bytes 100000 | tf_op jit(solution)/shard_map/expert_weights/pallas_call | solution.py:337
  156.4 4.4 %collective-permute-done = bf16[2,768,768]{2,1,0:T(8,128)(2,1)} collective-permute-done((bf16[2,768,768]{2,1,0:T(8,128)(2,1)}, bf16[2,768,768]{2,1,0:T(8,128)(2,1)}, u32[]{:S(2)}, u32[]{:S(2)}) %collective-permute-start) | collective-permute-done | bytes 2359328 | tf_op jit(solution)/shard_map/ppermute | solution.py:698
  160.8 4.4 %add_split.8 = (bf16[768,768]{1,0:T(8,128)(2,1)}, bf16[768,768]{1,0:T(8,128)(2,1)}) custom-call(s32[1]{0:T(128)} %bitcast.9.mine_ref, bf16[1536,768]{1,0:T(8,128)(2,1)} %bitcast.39, bf16[1536,768]{1,0:T(8,128)(2,1)} %bitcast.11.right_ref), custom_call_target="tpu_custom_call" | custom-call | flops 1000000 | bytes 100000 | tf_op jit(solution)/shard_map/add_split/pallas_call | solution.py:757
  165.2 4.4 %add_split.9 = (bf16[768,768]{1,0:T(8,128)(2,1)}, bf16[768,768]{1,0:T(8,128)(2,1)}) custom-call(s32[1]{0:T(128)} %bitcast.9.mine_ref, bf16[1536,768]{1,0:T(8,128)(2,1)} %bitcast.38, bf16[1536,768]{1,0:T(8,128)(2,1)} %bitcast.15.right_ref), custom_call_target="tpu_custom_call" | custom-call | flops 1000000 | bytes 100000 | tf_op jit(solution)/shard_map/add_split/pallas_call | solution.py:757
  169.6 4.5 %all-to-all-done.2 = bf16[8,128,768]{2,1,0:T(8,128)(2,1)S(1)} async-done(((bf16[8,128,768]{2,1,0:T(8,128)(2,1)}), bf16[8,128,768]{2,1,0:T(8,128)(2,1)S(1)}, u32[]{:S(2)}, u32[]{:S(2)}) %all-to-all-start.2) | async-done | bytes 1572896 | tf_op jit(solution)/shard_map/all_to_all | solution.py:817
  175.6 3.6 %all-to-all-start.3 = ((bf16[8,128,768]{2,1,0:T(8,128)(2,1)}), bf16[8,128,768]{2,1,0:T(8,128)(2,1)S(1)}, u32[]{:S(2)}, u32[]{:S(2)}) async-start(bf16[8,128,768]{2,1,0:T(8,128)(2,1)} %bitcast.40), calls=%async_computation.3 | async-start | bytes 3145728 | tf_op jit(solution)/shard_map/all_to_all | solution.py:817
  179.2 12.9 %second_back.1 = (f32[1024,768]{1,0:T(8,128)}, bf16[1024,768]{1,0:T(8,128)(2,1)}, f32[2,768]{1,0:T(2,128)}, bf16[15,384,128]{2,1,0:T(8,128)(2,1)}, bf16[15,384,128]{2,1,0:T(8,128)(2,1)}) custom-call(s32[1]{0:T(128)} %bitcast.2.core_ref, s32[1024,128]{1,0:T(8,128)} %get-tuple-element.123.wide_ref, bf16[1024,768]{1,0:T(8,128)(2,1)} %bitcast.33, ...), custom_call_target="tpu_custom_call" | custom-call | flops 1000000 | bytes 100000 | tf_op jit(solution)/shard_map/second_back/pallas_call | solution.py:556
  192.1 18.2 %attention_back.2 = (bf16[3,1024,384]{2,1,0:T(8,128)(2,1)}, bf16[15,384,128]{2,1,0:T(8,128)(2,1)}, bf16[15,384,128]{2,1,0:T(8,128)(2,1)}) custom-call(s32[1]{0:T(128)} %bitcast.2.core_ref, bf16[1024,768]{1,0:T(8,128)(2,1)} %get-tuple-element.120.q_ref, bf16[1024,768]{1,0:T(8,128)(2,1)} %get-tuple-element.121.k_ref, ...), custom_call_target="tpu_custom_call", output_to_operand_aliasing={{1}: (11, {}), {2}: (12, {})} | custom-call | flops 1000000 | bytes 100000 | tf_op jit(solution)/shard_map/attention_back/pallas_call | solution.py:189
  221.4 18.2 %attention_back.3 = (bf16[3,1024,384]{2,1,0:T(8,128)(2,1)}, bf16[9,384,128]{2,1,0:T(8,128)(2,1)}, bf16[9,384,128]{2,1,0:T(8,128)(2,1)}) custom-call(s32[1]{0:T(128)} %bitcast.2.core_ref, bf16[1024,768]{1,0:T(8,128)(2,1)} %get-tuple-element.120.q_ref, bf16[1024,768]{1,0:T(8,128)(2,1)} %get-tuple-element.121.k_ref, ...), custom_call_target="tpu_custom_call" | custom-call | flops 1000000 | bytes 100000 | tf_op jit(solution)/shard_map/attention_back/pallas_call | solution.py:189
  244.4 6.0 %layer_output.1 = bf16[1024,768]{1,0:T(8,128)(2,1)} custom-call(s32[1024,128]{1,0:T(8,128)} %get-tuple-element.123.wide_ref, bf16[1024,768]{1,0:T(8,128)(2,1)} %bitcast.32, f32[1024,768]{1,0:T(8,128)} %get-tuple-element.144.resid_ref, f32[1024,1]{1,0:T(8,128)} %get-tuple-element.175.gate_ref), custom_call_target="tpu_custom_call" | custom-call | flops 1000000 | bytes 100000 | tf_op jit(solution)/shard_map/layer_output/pallas_call | solution.py:637
  264.2 10.8 %first_back.1 = (f32[1024,768]{1,0:T(8,128)}, f32[2,768]{1,0:T(2,128)}) custom-call(bf16[3,1024,384]{2,1,0:T(8,128)(2,1)} %get-tuple-element.184.left_ref, bf16[3,1024,384]{2,1,0:T(8,128)(2,1)} %get-tuple-element.185.right_ref, bf16[1024,768]{1,0:T(8,128)(2,1)} %tokens_ref.2, f32[1024,768]{1,0:T(8,128)} %get-tuple-element.186.resid_ref, ...), custom_call_target="tpu_custom_call" | custom-call | flops 1000000 | bytes 100000 | tf_op jit(solution)/shard_map/first_back/pallas_call | solution.py:612
  312.3 10.7 %collective-permute-done.19 = bf16[2880,128]{1,0:T(8,128)(2,1)S(1)} collective-permute-done((bf16[2880,128]{1,0:T(8,128)(2,1)S(1)}, bf16[2880,128]{1,0:T(8,128)(2,1)S(1)}, u32[]{:S(2)}, u32[]{:S(2)}) %collective-permute-start.19) | collective-permute-done | bytes 737312 | tf_op jit(solution)/shard_map/ppermute | solution.py:698
  325.6 3.8 %collective-permute-done.24 = f32[4,768]{1,0:T(4,128)S(1)} collective-permute-done((f32[4,768]{1,0:T(4,128)S(1)}, f32[4,768]{1,0:T(4,128)S(1)}, u32[]{:S(2)}, u32[]{:S(2)}) %collective-permute-start.24) | collective-permute-done | bytes 12320 | tf_op jit(solution)/shard_map/ppermute | solution.py:698
  330.7 7.8 %collective-permute-done.25 = bf16[1728,128]{1,0:T(8,128)(2,1)S(1)} collective-permute-done((bf16[1728,128]{1,0:T(8,128)(2,1)S(1)}, bf16[1728,128]{1,0:T(8,128)(2,1)S(1)}, u32[]{:S(2)}, u32[]{:S(2)}) %collective-permute-start.25) | collective-permute-done | bytes 442400 | tf_op jit(solution)/shard_map/ppermute | solution.py:698
  342.3 6.3 %assemble.1 = (f32[768,768]{1,0:T(8,128)}, f32[768,768]{1,0:T(8,128)}, f32[768,768]{1,0:T(8,128)}, f32[768,768]{1,0:T(8,128)}) custom-call(s32[1]{0:T(128)} %bitcast.2.core_ref, bf16[15,384,128]{2,1,0:T(8,128)(2,1)} %bitcast.35, bf16[15,384,128]{2,1,0:T(8,128)(2,1)} %bitcast.44, bf16[9,384,128]{2,1,0:T(8,128)(2,1)} %bitcast.37, bf16[9,384,128]{2,1,0:T(8,128)(2,1)} %bitcast.48), custom_call_target="tpu_custom_call" | custom-call | flops 1000000 | bytes 100000 | tf_op jit(solution)/shard_map/assemble/pallas_call | solution.py:682
  (139 shorter events, 81.8 us)
Async XLA Ops:
  6.1 44.5 %all-to-all-start = ((bf16[8,128,768]{2,1,0:T(8,128)(2,1)}), bf16[8,128,768]{2,1,0:T(8,128)(2,1)S(1)}, u32[]{:S(2)}, u32[]{:S(2)}) async-start(bf16[8,128,768]{2,1,0:T(8,128)(2,1)} %bitcast.42), calls=%async_computation | async-start | bytes 3145728 | tf_op jit(solution)/shard_map/all_to_all | solution.py:817
  61.7 41.1 %all-to-all-start.1 = ((bf16[8,128,768]{2,1,0:T(8,128)(2,1)}), bf16[8,128,768]{2,1,0:T(8,128)(2,1)S(1)}, u32[]{:S(2)}, u32[]{:S(2)}) async-start(bf16[8,128,768]{2,1,0:T(8,128)(2,1)} %bitcast.43), calls=%async_computation.1 | async-start | bytes 3145728 | tf_op jit(solution)/shard_map/all_to_all | solution.py:817
  133.2 40.9 %all-to-all-start.2 = ((bf16[8,128,768]{2,1,0:T(8,128)(2,1)}), bf16[8,128,768]{2,1,0:T(8,128)(2,1)S(1)}, u32[]{:S(2)}, u32[]{:S(2)}) async-start(bf16[8,128,768]{2,1,0:T(8,128)(2,1)} %bitcast.41), calls=%async_computation.2 | async-start | bytes 3145728 | tf_op jit(solution)/shard_map/all_to_all | solution.py:817
  155.9 4.9 %collective-permute-start = (bf16[2,768,768]{2,1,0:T(8,128)(2,1)}, bf16[2,768,768]{2,1,0:T(8,128)(2,1)}, u32[]{:S(2)}, u32[]{:S(2)}) collective-permute-start(bf16[2,768,768]{2,1,0:T(8,128)(2,1)} %get-tuple-element.136), channel_id=1, source_target_pairs={{0,8},{8,0},{16,24},{24,16},{1,9},{9,1},{17,25},{25,17},{2,10},{10... | collective-permute-start | bytes 7077896 | tf_op jit(solution)/shard_map/ppermute | solution.py:698
  155.9 9.3 %collective-permute-start.1 = (bf16[2,768,768]{2,1,0:T(8,128)(2,1)}, bf16[2,768,768]{2,1,0:T(8,128)(2,1)}, u32[]{:S(2)}, u32[]{:S(2)}) collective-permute-start(bf16[2,768,768]{2,1,0:T(8,128)(2,1)} %get-tuple-element.140), channel_id=1, source_target_pairs={{0,8},{8,0},{16,24},{24,16},{1,9},{9,1},{17,25},{25,17},{2,10},{10... | collective-permute-start | bytes 7077896 | tf_op jit(solution)/shard_map/ppermute | solution.py:698
  174.1 36.2 %collective-permute-start.2 = (bf16[1,768,768]{2,1,0:T(8,128)(2,1)}, bf16[1,768,768]{2,1,0:T(8,128)(2,1)}, u32[]{:S(2)}, u32[]{:S(2)}) collective-permute-start(bf16[1,768,768]{2,1,0:T(8,128)(2,1)} %bitcast.12), channel_id=1, source_target_pairs={{0,16},{8,24},{16,0},{24,8},{1,17},{9,25},{17,1},{25,9},{2,18},{10... | collective-permute-start | bytes 3538952 | tf_op jit(solution)/shard_map/ppermute | solution.py:698
  175.6 64.0 %all-to-all-start.3 = ((bf16[8,128,768]{2,1,0:T(8,128)(2,1)}), bf16[8,128,768]{2,1,0:T(8,128)(2,1)S(1)}, u32[]{:S(2)}, u32[]{:S(2)}) async-start(bf16[8,128,768]{2,1,0:T(8,128)(2,1)} %bitcast.40), calls=%async_computation.3 | async-start | bytes 3145728 | tf_op jit(solution)/shard_map/all_to_all | solution.py:817
  218.3 21.3 %collective-permute-start.4 = (bf16[2880,128]{1,0:T(8,128)(2,1)}, bf16[2880,128]{1,0:T(8,128)(2,1)S(1)}, u32[]{:S(2)}, u32[]{:S(2)}) collective-permute-start(bf16[2880,128]{1,0:T(8,128)(2,1)} %get-tuple-element.162), channel_id=1, source_target_pairs={{0,1},{1,0},{2,3},{3,2},{4,5},{5,4},{6,7},{7,6},{8,9},{9,8},{10,11... | collective-permute-start | bytes 2211848 | tf_op jit(solution)/shard_map/ppermute | solution.py:698
  220.3 30.1 %collective-permute-start.7 = (bf16[1,768,768]{2,1,0:T(8,128)(2,1)}, bf16[1,768,768]{2,1,0:T(8,128)(2,1)S(1)}, u32[]{:S(2)}, u32[]{:S(2)}) collective-permute-start(bf16[1,768,768]{2,1,0:T(8,128)(2,1)} %bitcast.51), channel_id=1, source_target_pairs={{0,16},{8,24},{16,0},{24,8},{1,17},{9,25},{17,1},{25,9},{2,18},{10... | collective-permute-start | bytes 3538952 | tf_op jit(solution)/shard_map/ppermute | solution.py:698
  239.7 13.6 %collective-permute-start.6 = (bf16[3456,128]{1,0:T(8,128)(2,1)}, bf16[3456,128]{1,0:T(8,128)(2,1)}, u32[]{:S(2)}, u32[]{:S(2)}) collective-permute-start(bf16[3456,128]{1,0:T(8,128)(2,1)} %bitcast.52), channel_id=1, source_target_pairs={{0,8},{8,0},{16,24},{24,16},{1,9},{9,1},{17,25},{25,17},{2,10},{10... | collective-permute-start | bytes 2654216 | tf_op jit(solution)/shard_map/ppermute | solution.py:698
  242.9 10.4 %collective-permute-start.5 = (bf16[1440,128]{1,0:T(8,128)(2,1)}, bf16[1440,128]{1,0:T(8,128)(2,1)S(1)}, u32[]{:S(2)}, u32[]{:S(2)}) collective-permute-start(bf16[1440,128]{1,0:T(8,128)(2,1)} %get-tuple-element.172), channel_id=1, source_target_pairs={{0,2},{1,3},{2,0},{3,1},{4,6},{5,7},{6,4},{7,5},{8,10},{9,11},{10,... | collective-permute-start | bytes 1105928 | tf_op jit(solution)/shard_map/ppermute | solution.py:698
  256.0 19.0 %collective-permute-start.9 = (bf16[1728,128]{1,0:T(8,128)(2,1)}, bf16[1728,128]{1,0:T(8,128)(2,1)S(1)}, u32[]{:S(2)}, u32[]{:S(2)}) collective-permute-start(bf16[1728,128]{1,0:T(8,128)(2,1)} %get-tuple-element.183), channel_id=1, source_target_pairs={{0,16},{8,24},{16,0},{24,8},{1,17},{9,25},{17,1},{25,9},{2,18},{10... | collective-permute-start | bytes 1327112 | tf_op jit(solution)/shard_map/ppermute | solution.py:698
  258.9 16.1 %collective-permute-start.8 = (bf16[720,128]{1,0:T(8,128)(2,1)}, bf16[720,128]{1,0:T(8,128)(2,1)S(1)}, u32[]{:S(2)}, u32[]{:S(2)}) collective-permute-start(bf16[720,128]{1,0:T(8,128)(2,1)} %get-tuple-element.180), channel_id=1, source_target_pairs={{0,4},{1,5},{2,6},{3,7},{4,0},{5,1},{6,2},{7,3},{8,12},{9,13},{10,... | collective-permute-start | bytes 552968 | tf_op jit(solution)/shard_map/ppermute | solution.py:698
  275.1 6.4 %collective-permute-start.10 = (bf16[720,128]{1,0:T(8,128)(2,1)S(1)}, bf16[720,128]{1,0:T(8,128)(2,1)S(1)}, u32[]{:S(2)}, u32[]{:S(2)}) collective-permute-start(bf16[720,128]{1,0:T(8,128)(2,1)S(1)} %add_convert_fusion.1), channel_id=1, source_target_pairs={{0,16},{8,24},{16,0},{24,8},{1,17},{9,25},{17,1},{25,9},{2,18},{10... | collective-permute-start | bytes 552968 | tf_op jit(solution)/shard_map/ppermute | solution.py:698
  278.4 6.1 %collective-permute-start.11 = (bf16[864,128]{1,0:T(8,128)(2,1)}, bf16[864,128]{1,0:T(8,128)(2,1)S(1)}, u32[]{:S(2)}, u32[]{:S(2)}) collective-permute-start(bf16[864,128]{1,0:T(8,128)(2,1)} %get-tuple-element.194), channel_id=1, source_target_pairs={{0,1},{1,0},{2,3},{3,2},{4,5},{5,4},{6,7},{7,6},{8,9},{9,8},{10,11... | collective-permute-start | bytes 663560 | tf_op jit(solution)/shard_map/ppermute | solution.py:698
  284.6 8.9 %collective-permute-start.13 = (bf16[720,128]{1,0:T(8,128)(2,1)S(1)}, bf16[720,128]{1,0:T(8,128)(2,1)S(1)}, u32[]{:S(2)}, u32[]{:S(2)}) collective-permute-start(bf16[720,128]{1,0:T(8,128)(2,1)S(1)} %add_convert_fusion), channel_id=1, source_target_pairs={{0,4},{1,5},{2,6},{3,7},{4,0},{5,1},{6,2},{7,3},{8,12},{9,13},{10,... | collective-permute-start | bytes 552968 | tf_op jit(solution)/shard_map/ppermute | solution.py:698
  287.0 5.2 %collective-permute-start.14 = (bf16[432,128]{1,0:T(8,128)(2,1)}, bf16[432,128]{1,0:T(8,128)(2,1)S(1)}, u32[]{:S(2)}, u32[]{:S(2)}) collective-permute-start(bf16[432,128]{1,0:T(8,128)(2,1)} %get-tuple-element.204), channel_id=1, source_target_pairs={{0,2},{1,3},{2,0},{3,1},{4,6},{5,7},{6,4},{7,5},{8,10},{9,11},{10,... | collective-permute-start | bytes 331784 | tf_op jit(solution)/shard_map/ppermute | solution.py:698
  293.7 10.1 %collective-permute-start.16 = (bf16[1440,128]{1,0:T(8,128)(2,1)S(1)}, bf16[1440,128]{1,0:T(8,128)(2,1)S(1)}, u32[]{:S(2)}, u32[]{:S(2)}) collective-permute-start(bf16[1440,128]{1,0:T(8,128)(2,1)S(1)} %pad_maximum_fusion.4), channel_id=1, source_target_pairs={{0,2},{1,3},{2,0},{3,1},{4,6},{5,7},{6,4},{7,5},{8,10},{9,11},{10,... | collective-permute-start | bytes 1105928 | tf_op jit(solution)/shard_map/ppermute | solution.py:698
  293.8 7.8 %collective-permute-start.17 = (bf16[432,128]{1,0:T(8,128)(2,1)S(1)}, bf16[432,128]{1,0:T(8,128)(2,1)S(1)}, u32[]{:S(2)}, u32[]{:S(2)}) collective-permute-start(bf16[432,128]{1,0:T(8,128)(2,1)S(1)} %add_convert_fusion.3), channel_id=1, source_target_pairs={{0,4},{1,5},{2,6},{3,7},{4,0},{5,1},{6,2},{7,3},{8,12},{9,13},{10,... | collective-permute-start | bytes 331784 | tf_op jit(solution)/shard_map/ppermute | solution.py:698
  304.0 19.0 %collective-permute-start.19 = (bf16[2880,128]{1,0:T(8,128)(2,1)S(1)}, bf16[2880,128]{1,0:T(8,128)(2,1)S(1)}, u32[]{:S(2)}, u32[]{:S(2)}) collective-permute-start(bf16[2880,128]{1,0:T(8,128)(2,1)S(1)} %pad_maximum_fusion.2), channel_id=1, source_target_pairs={{0,1},{1,0},{2,3},{3,2},{4,5},{5,4},{6,7},{7,6},{8,9},{9,8},{10,11... | collective-permute-start | bytes 2211848 | tf_op jit(solution)/shard_map/ppermute | solution.py:698
  307.4 4.9 %collective-permute-start.20 = (bf16[432,128]{1,0:T(8,128)(2,1)S(1)}, bf16[432,128]{1,0:T(8,128)(2,1)S(1)}, u32[]{:S(2)}, u32[]{:S(2)}) collective-permute-start(bf16[432,128]{1,0:T(8,128)(2,1)S(1)} %add_convert_fusion.2), channel_id=1, source_target_pairs={{0,2},{1,3},{2,0},{3,1},{4,6},{5,7},{6,4},{7,5},{8,10},{9,11},{10,... | collective-permute-start | bytes 331784 | tf_op jit(solution)/shard_map/ppermute | solution.py:698
  323.0 6.4 %collective-permute-start.23 = (bf16[864,128]{1,0:T(8,128)(2,1)S(1)}, bf16[864,128]{1,0:T(8,128)(2,1)S(1)}, u32[]{:S(2)}, u32[]{:S(2)}) collective-permute-start(bf16[864,128]{1,0:T(8,128)(2,1)S(1)} %pad_maximum_fusion.5), channel_id=1, source_target_pairs={{0,1},{1,0},{2,3},{3,2},{4,5},{5,4},{6,7},{7,6},{8,9},{9,8},{10,11... | collective-permute-start | bytes 663560 | tf_op jit(solution)/shard_map/ppermute | solution.py:698
  329.6 9.0 %collective-permute-start.25 = (bf16[1728,128]{1,0:T(8,128)(2,1)S(1)}, bf16[1728,128]{1,0:T(8,128)(2,1)S(1)}, u32[]{:S(2)}, u32[]{:S(2)}) collective-permute-start(bf16[1728,128]{1,0:T(8,128)(2,1)S(1)} %pad_maximum_fusion.3), channel_id=1, source_target_pairs={{0,16},{8,24},{16,0},{24,8},{1,17},{9,25},{17,1},{25,9},{2,18},{10... | collective-permute-start | bytes 1327112 | tf_op jit(solution)/shard_map/ppermute | solution.py:698
  330.7 9.1 %collective-permute-start.22 = (bf16[5760,128]{1,0:T(8,128)(2,1)S(1)}, bf16[5760,128]{1,0:T(8,128)(2,1)S(1)}, u32[]{:S(2)}, u32[]{:S(2)}) collective-permute-start(bf16[5760,128]{1,0:T(8,128)(2,1)S(1)} %pad_maximum_fusion), channel_id=1, source_target_pairs={{0,8},{8,0},{16,24},{24,16},{1,9},{9,1},{17,25},{25,17},{2,10},{10... | collective-permute-start | bytes 4423688 | tf_op jit(solution)/shard_map/ppermute | solution.py:698
  (31 other events, 160.8 us)

commit v2 on v1

--- a/solution.py
+++ b/solution.py
@@ -212,8 +212,30 @@
     return cdf, value * (density * (1.0 / math.sqrt(2.0 * math.pi)))
 
 
+def expert_cots_kernel(c_ref, down_ref, out_ref):
+    out_ref[...] = contract(c_ref[...], down_ref[0], 1, 1).astype(BF16)
+
+
+def expert_cots(cots, down):
+    count, width = cots.shape
+    hidden = down.shape[1]
+    tile = min(512, hidden)
+    return pl.pallas_call(
+        expert_cots_kernel,
+        grid=(hidden // tile,),
+        in_specs=[
+            pl.BlockSpec((count, width), lambda f: (0, 0)),
+            pl.BlockSpec((1, tile, width), lambda f: (0, f, 0)),
+        ],
+        out_specs=pl.BlockSpec((count, tile), lambda f: (0, f)),
+        out_shape=jax.ShapeDtypeStruct((count, hidden), BF16),
+        cost_estimate=LIGHT,
+        name="expert_cots",
+    )(cots, down)
+
+
 def expert_kernel(
-    x_ref, c_ref, cen_ref, up_ref, down_ref,
+    x_ref, c_ref, cd_ref, cen_ref, up_ref, down_ref,
     y_ref, gs_ref, dy_ref, h_ref, dp_ref,
     y_sum, dx_sum, gate_ref,
 ):
@@ -234,7 +256,7 @@
     slope = cdf + weighted
     h_ref[...] = hidden
     y_sum[...] += contract(hidden, down_ref[0], 1, 0)
-    grad_hidden = contract(dy_ref[...], down_ref[0], 1, 1)
+    grad_hidden = cd_ref[...].astype(F32) * gate_ref[:, 0:1]
     grad_pre = (grad_hidden * slope).astype(BF16)
     dp_ref[...] = grad_pre
     dx_sum[...] += contract(grad_pre, up_ref[0], 1, 1)
@@ -250,7 +272,7 @@
         gs_ref[...] = back.astype(BF16)
 
 
-def expert(rows, cots, centroid, up, down):
+def expert(rows, cots, cots_down, centroid, up, down):
     count, width = rows.shape
     hidden = up.shape[2]
     tile = min(512, hidden)
@@ -263,6 +285,7 @@
         in_specs=[
             whole,
             whole,
+            pl.BlockSpec((count, tile), lambda f: (0, f)),
             pl.BlockSpec((1, width), lambda f: (0, 0)),
             pl.BlockSpec((1, width, tile), lambda f: (0, 0, f)),
             pl.BlockSpec((1, tile, width), lambda f: (0, f, 0)),
@@ -277,7 +300,7 @@
         ],
         cost_estimate=LIGHT,
         name="expert",
-    )(rows, cots, centroid, up, down)
+    )(rows, cots, cots_down, centroid, up, down)
 
 
 def expert_weights_kernel(
@@ -650,47 +673,50 @@
     )(wide, produced, resid, gate)
 
 
-def assemble_kernel(core_ref, early_mine, early_other, late_mine, late_other, *outs):
+def assemble_kernel(core_ref, mine_ref, other_ref, *outs, whole):
+    outs = outs[-4:] if whole else outs[-3:]
+
+    def write(parts):
+        for unit in range(whole):
+            outs[0][:, unit * LANES : (unit + 1) * LANES] = parts[unit].astype(F32)
+        for unit in range(whole, parts.shape[0]):
+            pair, matrix = divmod(unit - whole, 3)
+            out = outs[matrix - 3]
+            out[:, pair * LANES : (pair + 1) * LANES] = parts[unit].astype(F32)
+
     mine = pl.program_id(0) == core_ref[0]
-    columns = outs[0].shape[1] // LANES
-
-    def write(early, late):
-        for index in range(columns):
-            outs[0][:, index * LANES : (index + 1) * LANES] = early[index].astype(F32)
-        for part in (early, late):
-            first = columns if part is early else 0
-            pair = 0 if part is early else (early.shape[0] - columns) // 3
-            for unit in range(first, part.shape[0]):
-                at = pair + (unit - first) // 3
-                outs[1 + (unit - first) % 3][:, at * LANES : (at + 1) * LANES] = part[unit].astype(F32)
 
     @pl.when(mine)
     def _():
-        write(early_mine, late_mine)
+        write(mine_ref)
 
     @pl.when(jnp.logical_not(mine))
     def _():
-        write(early_other, late_other)
-
-
-def assemble(core, early_mine, early_other, late_mine, late_other, width):
-    args = [
-        part.reshape(-1, width // 2, LANES)
-        for part in (early_mine, early_other, late_mine, late_other)
-    ]
+        write(other_ref)
+
+
+def assemble(core, mine, other, width, outs):
+    mine, other = (part.reshape(-1, width // 2, LANES) for part in (mine, other))
+    whole = 0 if outs else width // LANES
+    columns = (mine.shape[0] - whole) // 3 * LANES
     out = jax.ShapeDtypeStruct((width, width), F32)
-    return pl.pallas_call(
-        assemble_kernel,
+    specs = [pl.BlockSpec((width // 2, columns), lambda i, core: (i, 1 if outs else 0))] * 3
+    if whole:
+        specs = [pl.BlockSpec((width // 2, width), lambda i, core: (i, 0))] + specs
+    return pl.pallas_call(
+        functools.partial(assemble_kernel, whole=whole),
         grid_spec=pltpu.PrefetchScalarGridSpec(
             num_scalar_prefetch=1,
             grid=(2,),
-            in_specs=[const(*part.shape) for part in args],
-            out_specs=[pl.BlockSpec((width // 2, width), lambda i, core: (i, 0))] * 4,
+            in_specs=[const(*mine.shape)] * 2
+            + [pl.BlockSpec(memory_space=pl.ANY)] * len(outs),
+            out_specs=specs,
         ),
-        out_shape=[out] * 4,
+        out_shape=[out] * len(specs),
+        input_output_aliases={3 + index: index for index in range(len(outs))},
         cost_estimate=LIGHT,
         name="assemble",
-    )(core, *args)
+    )(core, mine, other, *outs)
 
 
 def swap(value, axis, bit):
@@ -855,10 +881,12 @@
         mixed, tokens, output_weight, second_gain, second_bias, centroids, routing, slot, slots
     )
 
-    rows = exchange(rows.reshape(peers, -1, width)).reshape(slots, width)
+    rows = exchange(rows.reshape(peers, -1, width))
+    rows, cots_down = tie((rows, expert_cots(cots, expert_down)))
+    rows = rows.reshape(slots, width)
     own = centroids[lax.axis_index("expert")][None, :]
     produced, returned, grad_rows, hidden, grad_pre = expert(
-        rows, cots, own, expert_up, expert_down
+        rows, cots, cots_down, own, expert_up, expert_down
     )
     returned = exchange(returned.reshape(peers, -1, width))
     up_send, down_send, up_keep, down_keep = expert_weights(
@@ -895,7 +923,8 @@
     right, send, keep = back(probs, split, pairs - split, None)
     right, send, keep, produced = advance([early], right, send, keep, produced)
     produced = produced.reshape(slots, width)
-    late = Sum(keep.reshape(-1, LANES), send.reshape(-1, LANES), [("dp", 1)] + apart + cross)
+    order = [("dp", 1)] + apart + cross[1:2] + cross[:1] + cross[2:]
+    late = Sum(keep.reshape(-1, LANES), send.reshape(-1, LANES), order)
     layer_out = layer_output(wide, produced, resid, gate)
     layer_out, down_got = advance([early, late], layer_out, down_got)
     grad_tokens, first_sums = first_back(left, right, tokens, grad_resid, first_gain, weights)
@@ -910,13 +939,21 @@
     grad_up, grad_down = (value.reshape(value.shape[1:])[None] for value in (grad_up, grad_down))
     small = jnp.concatenate([first_sums, second_sums], axis=0)
     small = Sum(small, small, stages("dp", 1, 1 << 20) + cross, plus=add, split=False)
-    grad_up, grad_down = advance([early, late, small], grad_up, grad_down)
-    while early.steps or late.steps or small.steps:
+    while len(early.steps) > 1:
         advance([early, late, small])
-    early, late, small = early.keep, late.keep, small.keep
-    grad_output, grad_query, grad_key, grad_value = assemble(
-        core, early, swap(early, "dp", 1), late, swap(late, "dp", 1), width
-    )
+    got = early.start()
+    grad_up, grad_down = advance([late, small], grad_up, grad_down)
+    while len(late.steps) > 2:
+        advance([late, small])
+    early.finish(advance([late, small], got))
+    outs = assemble(core, early.keep, swap(early.keep, "dp", 1), width, [])
+    grad_output, *outs = advance([late, small], *outs)
+    while small.steps:
+        advance([small])
+    grad_query, grad_key, grad_value = assemble(
+        core, late.keep, swap(late.keep, "dp", 1), width, outs
+    )
+    small = small.keep
     return (
         layer_out,
         grad_tokens,

time: 350 us -> 344 us (0.983)
  waiting for transfers between devices: 91 us -> 79.3 us
  Pallas kernels: 194 us -> 203 us
  starting transfers between devices: 48 us -> 41 us
    pallas_call x1 -> x3, Pallas kernels: 6.28 us -> 17.9 us  [the longest x1 9.95 us: expert_cots(): pl.pallas_call(expert_cots_kernel, grid=(hidden // tile,), in_specs=[pl.B...]
    all_to_all x4, waiting for transfers between devices: 41 us -> 31 us  [exchange(): lax.all_to_all(rows, 'expert', split_axis=0, concat_axis=0, tiled=True)]
    ppermute x27, starting transfers between devices: 28.4 us -> 21.5 us  [swap(): return lax.ppermute(value, axis, [(i, i ^ bit) for i in range(size)])]
  transfers between devices with their start and end apart: 31 -> 31, of which waited for: 17 -> 21; matrix products, arithmetic and copies ran while one was open for 3% -> 3% of each run, Pallas kernels for 40% -> 44%
where the time goes in v2:
time: 344 us; the launch traced here: 343 us
  Pallas kernels  203 us (59%)
  waiting for transfers between devices  79.3 us (23%)
  starting transfers between devices  41 us (12%)
  local copies, waits for them, and re-layouts  9.68 us (3%)
  other arithmetic  8.55 us (2%)
    ppermute x27, waiting for transfers between devices, swap(): return lax.ppermute(value, axis, [(i, i ^ bit) for i in range(size)])  48.3 us
    pallas_call x2, Pallas kernels, attention_back(): pl.pallas_call(functools.partial(attention_back_kernel, block=block, bloc...  36.4 us
    all_to_all x4, waiting for transfers between devices, exchange(): lax.all_to_all(rows, 'expert', split_axis=0, concat_axis=0, tiled=True)  31 us
    pallas_call x1, Pallas kernels, expert(): pl.pallas_call(expert_kernel, grid=(hidden // tile,), in_specs=[whole, wh...  26.8 us
    pallas_call x1, Pallas kernels, attention(): pl.pallas_call(functools.partial(attention_kernel, block=block), grid=(pa...  25.7 us
    pallas_call x8, Pallas kernels, add_split(): pl.pallas_call(add_split_kernel, grid_spec=pltpu.PrefetchScalarGridSpec(n...  23 us
    ppermute x27, starting transfers between devices, swap(): return lax.ppermute(value, axis, [(i, i ^ bit) for i in range(size)])  21.5 us
    all_to_all x4, starting transfers between devices, exchange(): lax.all_to_all(rows, 'expert', split_axis=0, concat_axis=0, tiled=True)  19.5 us
  transfers between devices with their start and end apart: 31, of which 21 were waited for; matrix products, arithmetic and copies ran while one was open for 3% of the time, Pallas kernels for 44%

profile of v2, /device:TPU:0, one launch (start us, length us, event | category | flops | bytes accessed | tf_op | source)
XLA Modules:
  0.0 342.8 jit_solution(8926613369939707028)
XLA Ops:
  0.6 5.4 %route.1 = (bf16[1024,768]{1,0:T(8,128)(2,1)}, s32[1,1024]{1,0:T(1,128)}, s32[1024,128]{1,0:T(8,128)}) custom-call(s32[1,1024]{1,0:T(1,128)} %bitcast.51, bf16[1024,768]{1,0:T(8,128)(2,1)} %cot_ref.3), custom_call_target="tpu_custom_call" | custom-call | flops 1000000 | bytes 100000 | tf_op jit(solution)/shard_map/route/pallas_call | solution.py:415
  6.1 7.5 %all-to-all-start = ((bf16[8,128,768]{2,1,0:T(8,128)(2,1)}), bf16[8,128,768]{2,1,0:T(8,128)(2,1)S(1)}, u32[]{:S(2)}, u32[]{:S(2)}) async-start(bf16[8,128,768]{2,1,0:T(8,128)(2,1)} %bitcast.43), calls=%async_computation | async-start | bytes 3145728 | tf_op jit(solution)/shard_map/all_to_all | solution.py:843
  15.3 8.2 %project.1 = (bf16[768,1024]{1,0:T(8,128)(2,1)}, bf16[1024,768]{1,0:T(8,128)(2,1)}, bf16[1024,768]{1,0:T(8,128)(2,1)}, bf16[1024,768]{1,0:T(8,128)(2,1)}) custom-call(bf16[1024,768]{1,0:T(8,128)(2,1)} %tokens_ref.2, f32[1,768]{1,0:T(1,128)} %get-tuple-element.263.gain_ref, f32[1,768]{1,0:T(1,128)} %get-tuple-element.262.bias_ref, bf16[768,768]{1,0:T(8,128)(2,1)} %wq_ref.3, ...), custom_call_target="tpu_custom_call" | custom-call | flops 1000000 | bytes 100000 | tf_op jit(solution)/shard_map/project/pallas_call | solution.py:448
  23.5 25.7 %attention.1 = (bf16[1024,768]{1,0:T(8,128)(2,1)}, bf16[12,256,256]{2,1,0:T(8,128)(2,1)}, bf16[12,512,256]{2,1,0:T(8,128)(2,1)}, bf16[12,768,256]{2,1,0:T(8,128)(2,1)}, bf16[12,1024,256]{2,1,0:T(8,128)(2,1)}) custom-call(bf16[1024,768]{1,0:T(8,128)(2,1)} %get-tuple-element.130.q_ref, bf16[1024,768]{1,0:T(8,128)(2,1)} %get-tuple-element.131.k_ref, ...), custom_call_target="tpu_custom_call" | custom-call | flops 1000000 | bytes 100000 | tf_op jit(solution)/shard_map/attention/pallas_call | solution.py:93
  50.6 11.2 %branch.1 = (f32[1024,768]{1,0:T(8,128)}, f32[1024,1]{1,0:T(8,128)}, bf16[768,1024]{1,0:T(8,128)(2,1)}, bf16[1024,768]{1,0:T(8,128)(2,1)}) custom-call(bf16[1024,768]{1,0:T(8,128)(2,1)} %get-tuple-element.136.mixed_ref.o_ref, bf16[1024,768]{1,0:T(8,128)(2,1)} %tokens_ref.2, bf16[768,768]{1,0:T(8,128)(2,1)} %weight_ref.3, ...), custom_call_target="tpu_custom_call" | custom-call | flops 1000000 | bytes 100000 | tf_op jit(solution)/shard_map/branch/pallas_call | solution.py:493
  61.7 4.7 %all-to-all-start.1 = ((bf16[8,128,768]{2,1,0:T(8,128)(2,1)}), bf16[8,128,768]{2,1,0:T(8,128)(2,1)S(1)}, u32[]{:S(2)}, u32[]{:S(2)}) async-start(bf16[8,128,768]{2,1,0:T(8,128)(2,1)} %bitcast.44), calls=%async_computation.1 | async-start | bytes 3145728 | tf_op jit(solution)/shard_map/all_to_all | solution.py:843
  67.8 9.9 %expert_cots.1.cd_ref = bf16[1024,3072]{1,0:T(8,128)(2,1)} custom-call(bf16[1024,768]{1,0:T(8,128)(2,1)} %bitcast.30, bf16[1,3072,768]{2,1,0:T(8,128)(2,1)} %down_ref.3), custom_call_target="tpu_custom_call" | custom-call | flops 1000000 | bytes 100000 | tf_op jit(solution)/shard_map/expert_cots/pallas_call | solution.py:223
  77.7 25.2 %all-to-all-done.1 = bf16[8,128,768]{2,1,0:T(8,128)(2,1)S(1)} async-done(((bf16[8,128,768]{2,1,0:T(8,128)(2,1)}), bf16[8,128,768]{2,1,0:T(8,128)(2,1)S(1)}, u32[]{:S(2)}, u32[]{:S(2)}) %all-to-all-start.1) | async-done | bytes 1572896 | tf_op jit(solution)/shard_map/all_to_all | solution.py:843
  104.0 26.8 %expert.1 = (bf16[1024,768]{1,0:T(8,128)(2,1)}, bf16[1024,768]{1,0:T(8,128)(2,1)}, bf16[1024,768]{1,0:T(8,128)(2,1)}, bf16[1024,3072]{1,0:T(8,128)(2,1)}, bf16[1024,3072]{1,0:T(8,128)(2,1)}) custom-call(bf16[1024,768]{1,0:T(8,128)(2,1)} %bitcast.32, bf16[1024,768]{1,0:T(8,128)(2,1)} %bitcast.31, bf16[1024,3072]{1,0:T(8,128)(2,1)} %expert_cots.1.cd_ref, ...), custom_call_target="tpu_custom_call" | custom-call | flops 1000000 | bytes 100000 | tf_op jit(solution)/shard_map/expert/pallas_call | solution.py:282
  130.8 3.8 %all-to-all-start.2 = ((bf16[8,128,768]{2,1,0:T(8,128)(2,1)}), bf16[8,128,768]{2,1,0:T(8,128)(2,1)S(1)}, u32[]{:S(2)}, u32[]{:S(2)}) async-start(bf16[8,128,768]{2,1,0:T(8,128)(2,1)} %bitcast.42), calls=%async_computation.2 | async-start | bytes 3145728 | tf_op jit(solution)/shard_map/all_to_all | solution.py:843
  134.5 18.9 %expert_weights.1 = (bf16[2,768,768]{2,1,0:T(8,128)(2,1)}, bf16[2,768,768]{2,1,0:T(8,128)(2,1)}, bf16[2,768,768]{2,1,0:T(8,128)(2,1)}, bf16[2,768,768]{2,1,0:T(8,128)(2,1)}) custom-call(s32[1]{0:T(128)} %bitcast.2.core_ref, bf16[1024,768]{1,0:T(8,128)(2,1)} %bitcast.33, bf16[1024,768]{1,0:T(8,128)(2,1)} %get-tuple-element.144.dy_ref, ...), custom_call_target="tpu_custom_call" | custom-call | flops 1000000 | bytes 100000 | tf_op jit(solution)/shard_map/expert_weights/pallas_call | solution.py:360
  153.9 4.4 %collective-permute-done = bf16[2,768,768]{2,1,0:T(8,128)(2,1)} collective-permute-done((bf16[2,768,768]{2,1,0:T(8,128)(2,1)}, bf16[2,768,768]{2,1,0:T(8,128)(2,1)}, u32[]{:S(2)}, u32[]{:S(2)}) %collective-permute-start) | collective-permute-done | bytes 2359328 | tf_op jit(solution)/shard_map/ppermute | solution.py:724
  158.3 4.4 %add_split.8 = (bf16[768,768]{1,0:T(8,128)(2,1)}, bf16[768,768]{1,0:T(8,128)(2,1)}) custom-call(s32[1]{0:T(128)} %bitcast.9.mine_ref, bf16[1536,768]{1,0:T(8,128)(2,1)} %bitcast.40, bf16[1536,768]{1,0:T(8,128)(2,1)} %bitcast.11.right_ref), custom_call_target="tpu_custom_call" | custom-call | flops 1000000 | bytes 100000 | tf_op jit(solution)/shard_map/add_split/pallas_call | solution.py:783
  162.7 4.4 %add_split.9 = (bf16[768,768]{1,0:T(8,128)(2,1)}, bf16[768,768]{1,0:T(8,128)(2,1)}) custom-call(s32[1]{0:T(128)} %bitcast.9.mine_ref, bf16[1536,768]{1,0:T(8,128)(2,1)} %bitcast.39, bf16[1536,768]{1,0:T(8,128)(2,1)} %bitcast.15.right_ref), custom_call_target="tpu_custom_call" | custom-call | flops 1000000 | bytes 100000 | tf_op jit(solution)/shard_map/add_split/pallas_call | solution.py:783
  167.1 4.5 %all-to-all-done.2 = bf16[8,128,768]{2,1,0:T(8,128)(2,1)S(1)} async-done(((bf16[8,128,768]{2,1,0:T(8,128)(2,1)}), bf16[8,128,768]{2,1,0:T(8,128)(2,1)S(1)}, u32[]{:S(2)}, u32[]{:S(2)}) %all-to-all-start.2) | async-done | bytes 1572896 | tf_op jit(solution)/shard_map/all_to_all | solution.py:843
  176.7 12.9 %second_back.1 = (f32[1024,768]{1,0:T(8,128)}, bf16[1024,768]{1,0:T(8,128)(2,1)}, f32[2,768]{1,0:T(2,128)}, bf16[15,384,128]{2,1,0:T(8,128)(2,1)}, bf16[15,384,128]{2,1,0:T(8,128)(2,1)}) custom-call(s32[1]{0:T(128)} %bitcast.2.core_ref, s32[1024,128]{1,0:T(8,128)} %get-tuple-element.133.wide_ref, bf16[1024,768]{1,0:T(8,128)(2,1)} %bitcast.35, ...), custom_call_target="tpu_custom_call" | custom-call | flops 1000000 | bytes 100000 | tf_op jit(solution)/shard_map/second_back/pallas_call | solution.py:579
  189.6 18.2 %attention_back.2 = (bf16[3,1024,384]{2,1,0:T(8,128)(2,1)}, bf16[15,384,128]{2,1,0:T(8,128)(2,1)}, bf16[15,384,128]{2,1,0:T(8,128)(2,1)}) custom-call(s32[1]{0:T(128)} %bitcast.2.core_ref, bf16[1024,768]{1,0:T(8,128)(2,1)} %get-tuple-element.130.q_ref, bf16[1024,768]{1,0:T(8,128)(2,1)} %get-tuple-element.131.k_ref, ...), custom_call_target="tpu_custom_call", output_to_operand_aliasing={{1}: (11, {}), {2}: (12, {})} | custom-call | flops 1000000 | bytes 100000 | tf_op jit(solution)/shard_map/attention_back/pallas_call | solution.py:189
  218.9 18.2 %attention_back.3 = (bf16[3,1024,384]{2,1,0:T(8,128)(2,1)}, bf16[9,384,128]{2,1,0:T(8,128)(2,1)}, bf16[9,384,128]{2,1,0:T(8,128)(2,1)}) custom-call(s32[1]{0:T(128)} %bitcast.2.core_ref, bf16[1024,768]{1,0:T(8,128)(2,1)} %get-tuple-element.130.q_ref, bf16[1024,768]{1,0:T(8,128)(2,1)} %get-tuple-element.131.k_ref, ...), custom_call_target="tpu_custom_call" | custom-call | flops 1000000 | bytes 100000 | tf_op jit(solution)/shard_map/attention_back/pallas_call | solution.py:189
  241.9 6.0 %layer_output.1 = bf16[1024,768]{1,0:T(8,128)(2,1)} custom-call(s32[1024,128]{1,0:T(8,128)} %get-tuple-element.133.wide_ref, bf16[1024,768]{1,0:T(8,128)(2,1)} %bitcast.34, f32[1024,768]{1,0:T(8,128)} %get-tuple-element.156.resid_ref, f32[1024,1]{1,0:T(8,128)} %get-tuple-element.187.gate_ref), custom_call_target="tpu_custom_call" | custom-call | flops 1000000 | bytes 100000 | tf_op jit(solution)/shard_map/layer_output/pallas_call | solution.py:660
  258.8 10.8 %first_back.1 = (f32[1024,768]{1,0:T(8,128)}, f32[2,768]{1,0:T(2,128)}) custom-call(bf16[3,1024,384]{2,1,0:T(8,128)(2,1)} %get-tuple-element.196.left_ref, bf16[3,1024,384]{2,1,0:T(8,128)(2,1)} %get-tuple-element.197.right_ref, bf16[1024,768]{1,0:T(8,128)(2,1)} %tokens_ref.2, f32[1024,768]{1,0:T(8,128)} %get-tuple-element.198.resid_ref, ...), custom_call_target="tpu_custom_call" | custom-call | flops 1000000 | bytes 100000 | tf_op jit(solution)/shard_map/first_back/pallas_call | solution.py:635
  294.0 4.5 %collective-permute-done.17 = bf16[432,128]{1,0:T(8,128)(2,1)S(1)} collective-permute-done((bf16[432,128]{1,0:T(8,128)(2,1)S(1)}, bf16[432,128]{1,0:T(8,128)(2,1)S(1)}, u32[]{:S(2)}, u32[]{:S(2)}) %collective-permute-start.17) | collective-permute-done | bytes 110624 | tf_op jit(solution)/shard_map/ppermute | solution.py:724
  312.9 7.6 %collective-permute-done.23 = bf16[2880,128]{1,0:T(8,128)(2,1)S(1)} collective-permute-done((bf16[2880,128]{1,0:T(8,128)(2,1)S(1)}, bf16[2880,128]{1,0:T(8,128)(2,1)S(1)}, u32[]{:S(2)}, u32[]{:S(2)}) %collective-permute-start.23) | collective-permute-done | bytes 737312 | tf_op jit(solution)/shard_map/ppermute | solution.py:724
  325.4 4.6 %assemble.2 = (f32[768,768]{1,0:T(8,128)}, f32[768,768]{1,0:T(8,128)}, f32[768,768]{1,0:T(8,128)}, f32[768,768]{1,0:T(8,128)}) custom-call(s32[1]{0:T(128)} %bitcast.2.core_ref, bf16[15,384,128]{2,1,0:T(8,128)(2,1)} %bitcast.36, bf16[15,384,128]{2,1,0:T(8,128)(2,1)} %bitcast.45), custom_call_target="tpu_custom_call" | custom-call | flops 1000000 | bytes 100000 | tf_op jit(solution)/shard_map/assemble/pallas_call | solution.py:706
  330.0 4.8 %collective-permute-done.24 = bf16[1728,128]{1,0:T(8,128)(2,1)} collective-permute-done((bf16[1728,128]{1,0:T(8,128)(2,1)}, bf16[1728,128]{1,0:T(8,128)(2,1)}, u32[]{:S(2)}, u32[]{:S(2)}) %collective-permute-start.24) | collective-permute-done | bytes 442400 | tf_op jit(solution)/shard_map/ppermute | solution.py:724
  (141 shorter events, 89.2 us)
Async XLA Ops:
  6.1 44.5 %all-to-all-start = ((bf16[8,128,768]{2,1,0:T(8,128)(2,1)}), bf16[8,128,768]{2,1,0:T(8,128)(2,1)S(1)}, u32[]{:S(2)}, u32[]{:S(2)}) async-start(bf16[8,128,768]{2,1,0:T(8,128)(2,1)} %bitcast.43), calls=%async_computation | async-start | bytes 3145728 | tf_op jit(solution)/shard_map/all_to_all | solution.py:843
  61.7 41.1 %all-to-all-start.1 = ((bf16[8,128,768]{2,1,0:T(8,128)(2,1)}), bf16[8,128,768]{2,1,0:T(8,128)(2,1)S(1)}, u32[]{:S(2)}, u32[]{:S(2)}) async-start(bf16[8,128,768]{2,1,0:T(8,128)(2,1)} %bitcast.44), calls=%async_computation.1 | async-start | bytes 3145728 | tf_op jit(solution)/shard_map/all_to_all | solution.py:843
  130.8 40.9 %all-to-all-start.2 = ((bf16[8,128,768]{2,1,0:T(8,128)(2,1)}), bf16[8,128,768]{2,1,0:T(8,128)(2,1)S(1)}, u32[]{:S(2)}, u32[]{:S(2)}) async-start(bf16[8,128,768]{2,1,0:T(8,128)(2,1)} %bitcast.42), calls=%async_computation.2 | async-start | bytes 3145728 | tf_op jit(solution)/shard_map/all_to_all | solution.py:843
  153.4 4.9 %collective-permute-start = (bf16[2,768,768]{2,1,0:T(8,128)(2,1)}, bf16[2,768,768]{2,1,0:T(8,128)(2,1)}, u32[]{:S(2)}, u32[]{:S(2)}) collective-permute-start(bf16[2,768,768]{2,1,0:T(8,128)(2,1)} %get-tuple-element.148), channel_id=1, source_target_pairs={{0,8},{8,0},{16,24},{24,16},{1,9},{9,1},{17,25},{25,17},{2,10},{10... | collective-permute-start | bytes 7077896 | tf_op jit(solution)/shard_map/ppermute | solution.py:724
  153.4 9.3 %collective-permute-start.1 = (bf16[2,768,768]{2,1,0:T(8,128)(2,1)}, bf16[2,768,768]{2,1,0:T(8,128)(2,1)}, u32[]{:S(2)}, u32[]{:S(2)}) collective-permute-start(bf16[2,768,768]{2,1,0:T(8,128)(2,1)} %get-tuple-element.152), channel_id=1, source_target_pairs={{0,8},{8,0},{16,24},{24,16},{1,9},{9,1},{17,25},{25,17},{2,10},{10... | collective-permute-start | bytes 7077896 | tf_op jit(solution)/shard_map/ppermute | solution.py:724
  171.6 36.2 %collective-permute-start.2 = (bf16[1,768,768]{2,1,0:T(8,128)(2,1)}, bf16[1,768,768]{2,1,0:T(8,128)(2,1)}, u32[]{:S(2)}, u32[]{:S(2)}) collective-permute-start(bf16[1,768,768]{2,1,0:T(8,128)(2,1)} %bitcast.12), channel_id=1, source_target_pairs={{0,16},{8,24},{16,0},{24,8},{1,17},{9,25},{17,1},{25,9},{2,18},{10... | collective-permute-start | bytes 3538952 | tf_op jit(solution)/shard_map/ppermute | solution.py:724
  173.1 64.0 %all-to-all-start.3 = ((bf16[8,128,768]{2,1,0:T(8,128)(2,1)}), bf16[8,128,768]{2,1,0:T(8,128)(2,1)S(1)}, u32[]{:S(2)}, u32[]{:S(2)}) async-start(bf16[8,128,768]{2,1,0:T(8,128)(2,1)} %bitcast.41), calls=%async_computation.3 | async-start | bytes 3145728 | tf_op jit(solution)/shard_map/all_to_all | solution.py:843
  215.8 21.4 %collective-permute-start.4 = (bf16[2880,128]{1,0:T(8,128)(2,1)}, bf16[2880,128]{1,0:T(8,128)(2,1)S(1)}, u32[]{:S(2)}, u32[]{:S(2)}) collective-permute-start(bf16[2880,128]{1,0:T(8,128)(2,1)} %get-tuple-element.174), channel_id=1, source_target_pairs={{0,1},{1,0},{2,3},{3,2},{4,5},{5,4},{6,7},{7,6},{8,9},{9,8},{10,11... | collective-permute-start | bytes 2211848 | tf_op jit(solution)/shard_map/ppermute | solution.py:724
  217.8 30.1 %collective-permute-start.7 = (bf16[1,768,768]{2,1,0:T(8,128)(2,1)}, bf16[1,768,768]{2,1,0:T(8,128)(2,1)S(1)}, u32[]{:S(2)}, u32[]{:S(2)}) collective-permute-start(bf16[1,768,768]{2,1,0:T(8,128)(2,1)} %bitcast.52), channel_id=1, source_target_pairs={{0,16},{8,24},{16,0},{24,8},{1,17},{9,25},{17,1},{25,9},{2,18},{10... | collective-permute-start | bytes 3538952 | tf_op jit(solution)/shard_map/ppermute | solution.py:724
  237.2 13.6 %collective-permute-start.6 = (bf16[3456,128]{1,0:T(8,128)(2,1)}, bf16[3456,128]{1,0:T(8,128)(2,1)}, u32[]{:S(2)}, u32[]{:S(2)}) collective-permute-start(bf16[3456,128]{1,0:T(8,128)(2,1)} %bitcast.53), channel_id=1, source_target_pairs={{0,8},{8,0},{16,24},{24,16},{1,9},{9,1},{17,25},{25,17},{2,10},{10... | collective-permute-start | bytes 2654216 | tf_op jit(solution)/shard_map/ppermute | solution.py:724
  240.5 10.3 %collective-permute-start.5 = (bf16[1440,128]{1,0:T(8,128)(2,1)}, bf16[1440,128]{1,0:T(8,128)(2,1)S(1)}, u32[]{:S(2)}, u32[]{:S(2)}) collective-permute-start(bf16[1440,128]{1,0:T(8,128)(2,1)} %get-tuple-element.184), channel_id=1, source_target_pairs={{0,2},{1,3},{2,0},{3,1},{4,6},{5,7},{6,4},{7,5},{8,10},{9,11},{10,... | collective-permute-start | bytes 1105928 | tf_op jit(solution)/shard_map/ppermute | solution.py:724
  253.5 16.1 %collective-permute-start.9 = (bf16[1728,128]{1,0:T(8,128)(2,1)}, bf16[1728,128]{1,0:T(8,128)(2,1)S(1)}, u32[]{:S(2)}, u32[]{:S(2)}) collective-permute-start(bf16[1728,128]{1,0:T(8,128)(2,1)} %get-tuple-element.195), channel_id=1, source_target_pairs={{0,16},{8,24},{16,0},{24,8},{1,17},{9,25},{17,1},{25,9},{2,18},{10... | collective-permute-start | bytes 1327112 | tf_op jit(solution)/shard_map/ppermute | solution.py:724
  256.4 13.2 %collective-permute-start.8 = (bf16[720,128]{1,0:T(8,128)(2,1)}, bf16[720,128]{1,0:T(8,128)(2,1)S(1)}, u32[]{:S(2)}, u32[]{:S(2)}) collective-permute-start(bf16[720,128]{1,0:T(8,128)(2,1)} %get-tuple-element.192), channel_id=1, source_target_pairs={{0,4},{1,5},{2,6},{3,7},{4,0},{5,1},{6,2},{7,3},{8,12},{9,13},{10,... | collective-permute-start | bytes 552968 | tf_op jit(solution)/shard_map/ppermute | solution.py:724
  272.5 7.1 %collective-permute-start.11 = (bf16[864,128]{1,0:T(8,128)(2,1)}, bf16[864,128]{1,0:T(8,128)(2,1)S(1)}, u32[]{:S(2)}, u32[]{:S(2)}) collective-permute-start(bf16[864,128]{1,0:T(8,128)(2,1)} %get-tuple-element.207), channel_id=1, source_target_pairs={{0,2},{1,3},{2,0},{3,1},{4,6},{5,7},{6,4},{7,5},{8,10},{9,11},{10,... | collective-permute-start | bytes 663560 | tf_op jit(solution)/shard_map/ppermute | solution.py:724
  274.0 5.6 %collective-permute-start.10 = (bf16[720,128]{1,0:T(8,128)(2,1)S(1)}, bf16[720,128]{1,0:T(8,128)(2,1)S(1)}, u32[]{:S(2)}, u32[]{:S(2)}) collective-permute-start(bf16[720,128]{1,0:T(8,128)(2,1)S(1)} %add_convert_fusion.1), channel_id=1, source_target_pairs={{0,16},{8,24},{16,0},{24,8},{1,17},{9,25},{17,1},{25,9},{2,18},{10... | collective-permute-start | bytes 552968 | tf_op jit(solution)/shard_map/ppermute | solution.py:724
  279.7 9.2 %collective-permute-start.13 = (bf16[720,128]{1,0:T(8,128)(2,1)S(1)}, bf16[720,128]{1,0:T(8,128)(2,1)S(1)}, u32[]{:S(2)}, u32[]{:S(2)}) collective-permute-start(bf16[720,128]{1,0:T(8,128)(2,1)S(1)} %add_convert_fusion), channel_id=1, source_target_pairs={{0,4},{1,5},{2,6},{3,7},{4,0},{5,1},{6,2},{7,3},{8,12},{9,13},{10,... | collective-permute-start | bytes 552968 | tf_op jit(solution)/shard_map/ppermute | solution.py:724
  282.1 5.0 %collective-permute-start.14 = (bf16[432,128]{1,0:T(8,128)(2,1)}, bf16[432,128]{1,0:T(8,128)(2,1)S(1)}, u32[]{:S(2)}, u32[]{:S(2)}) collective-permute-start(bf16[432,128]{1,0:T(8,128)(2,1)} %get-tuple-element.213), channel_id=1, source_target_pairs={{0,1},{1,0},{2,3},{3,2},{4,5},{5,4},{6,7},{7,6},{8,9},{9,8},{10,11... | collective-permute-start | bytes 331784 | tf_op jit(solution)/shard_map/ppermute | solution.py:724
  288.9 11.8 %collective-permute-start.16 = (bf16[1440,128]{1,0:T(8,128)(2,1)S(1)}, bf16[1440,128]{1,0:T(8,128)(2,1)S(1)}, u32[]{:S(2)}, u32[]{:S(2)}) collective-permute-start(bf16[1440,128]{1,0:T(8,128)(2,1)S(1)} %pad_maximum_fusion.4), channel_id=1, source_target_pairs={{0,2},{1,3},{2,0},{3,1},{4,6},{5,7},{6,4},{7,5},{8,10},{9,11},{10,... | collective-permute-start | bytes 1105928 | tf_op jit(solution)/shard_map/ppermute | solution.py:724
  289.1 9.4 %collective-permute-start.17 = (bf16[432,128]{1,0:T(8,128)(2,1)S(1)}, bf16[432,128]{1,0:T(8,128)(2,1)S(1)}, u32[]{:S(2)}, u32[]{:S(2)}) collective-permute-start(bf16[432,128]{1,0:T(8,128)(2,1)S(1)} %add_convert_fusion.3), channel_id=1, source_target_pairs={{0,4},{1,5},{2,6},{3,7},{4,0},{5,1},{6,2},{7,3},{8,12},{9,13},{10,... | collective-permute-start | bytes 331784 | tf_op jit(solution)/shard_map/ppermute | solution.py:724
  300.7 6.0 %collective-permute-start.19 = (bf16[432,128]{1,0:T(8,128)(2,1)S(1)}, bf16[432,128]{1,0:T(8,128)(2,1)S(1)}, u32[]{:S(2)}, u32[]{:S(2)}) collective-permute-start(bf16[432,128]{1,0:T(8,128)(2,1)S(1)} %add_convert_fusion.2), channel_id=1, source_target_pairs={{0,1},{1,0},{2,3},{3,2},{4,5},{5,4},{6,7},{7,6},{8,9},{9,8},{10,11... | collective-permute-start | bytes 331784 | tf_op jit(solution)/shard_map/ppermute | solution.py:724
  301.6 18.9 %collective-permute-start.23 = (bf16[2880,128]{1,0:T(8,128)(2,1)S(1)}, bf16[2880,128]{1,0:T(8,128)(2,1)S(1)}, u32[]{:S(2)}, u32[]{:S(2)}) collective-permute-start(bf16[2880,128]{1,0:T(8,128)(2,1)S(1)} %pad_maximum_fusion.2), channel_id=1, source_target_pairs={{0,1},{1,0},{2,3},{3,2},{4,5},{5,4},{6,7},{7,6},{8,9},{9,8},{10,11... | collective-permute-start | bytes 2211848 | tf_op jit(solution)/shard_map/ppermute | solution.py:724
  306.8 6.1 %collective-permute-start.21 = (bf16[864,128]{1,0:T(8,128)(2,1)S(1)}, bf16[864,128]{1,0:T(8,128)(2,1)S(1)}, u32[]{:S(2)}, u32[]{:S(2)}) collective-permute-start(bf16[864,128]{1,0:T(8,128)(2,1)S(1)} %pad_maximum_fusion.5), channel_id=1, source_target_pairs={{0,2},{1,3},{2,0},{3,1},{4,6},{5,7},{6,4},{7,5},{8,10},{9,11},{10,... | collective-permute-start | bytes 663560 | tf_op jit(solution)/shard_map/ppermute | solution.py:724
  307.0 4.7 %collective-permute-start.22 = (f32[4,768]{1,0:T(4,128)S(1)}, f32[4,768]{1,0:T(4,128)S(1)}, u32[]{:S(2)}, u32[]{:S(2)}) collective-permute-start(f32[4,768]{1,0:T(4,128)S(1)} %add.81), channel_id=1, source_target_pairs={{0,4},{1,5},{2,6},{3,7},{4,0},{5,1},{6,2},{7,3},{8,12},{9,13},{10,... | collective-permute-start | bytes 36872 | tf_op jit(solution)/shard_map/ppermute | solution.py:724
  322.1 12.7 %collective-permute-start.24 = (bf16[1728,128]{1,0:T(8,128)(2,1)}, bf16[1728,128]{1,0:T(8,128)(2,1)}, u32[]{:S(2)}, u32[]{:S(2)}) collective-permute-start(bf16[1728,128]{1,0:T(8,128)(2,1)} %pad_maximum_fusion.3), channel_id=1, source_target_pairs={{0,16},{8,24},{16,0},{24,8},{1,17},{9,25},{17,1},{25,9},{2,18},{10... | collective-permute-start | bytes 1327112 | tf_op jit(solution)/shard_map/ppermute | solution.py:724
  (31 other events, 168.2 us)

commit v3 on v2

--- a/solution.py
+++ b/solution.py
@@ -53,10 +53,27 @@
         bias_ref[...] = jnp.where(key <= query, 0.0, -1e30)
 
 
-def attention_kernel(q_ref, k_ref, v_ref, o_ref, *refs, block):
-    *probs_refs, bias_ref = refs
+def attention_kernel(
+    tokens_ref, gain_ref, shift_ref, wq_ref, wk_ref, wv_ref, q_ref, k_ref, v_ref, o_ref, *refs, block
+):
+    *probs_refs, normed_ref, bias_ref = refs
     causal_bias(bias_ref, 0)
     parity = pl.program_id(1)
+
+    @pl.when((pl.program_id(0) == 0) & (parity == 0))
+    def _():
+        for index in range(len(probs_refs)):
+            rows = slice(index * block, (index + 1) * block)
+            normed, _, _ = normalize(tokens_ref[rows, :].astype(F32), gain_ref[...], shift_ref[...])
+            normed_ref[rows, :] = normed.astype(BF16)
+
+    @pl.when(parity == 0)
+    def _():
+        weights = jnp.concatenate([wq_ref[...], wk_ref[...], wv_ref[...]], axis=1)
+        made = contract(normed_ref[...], weights, 1, 0).astype(BF16)
+        for index, out in enumerate((q_ref, k_ref, v_ref)):
+            out[...] = made[:, index * LANES : (index + 1) * LANES]
+
     queries = q_ref[...] * head_mask(parity, HEAD**-0.5)
     values = v_ref[...] * head_mask(parity, 1.0)
     outs = []
@@ -84,28 +101,30 @@
         o_ref[...] = o_ref[...] + mixed
 
 
-def attention(queries, keys, values):
-    length, width = queries.shape
+def attention(tokens, gain, shift, weights):
+    length, width = tokens.shape
     pairs = width // LANES
     block = min(256, length)
     finishes = range(block, length + 1, block)
     spec = pl.BlockSpec((length, LANES), lambda pair, parity: (0, pair))
-    mixed, *probs = pl.pallas_call(
+    weight = pl.BlockSpec((width, LANES), lambda pair, parity: (0, pair))
+    wide = jax.ShapeDtypeStruct((length, width), BF16)
+    queries, keys, values, mixed, *probs = pl.pallas_call(
         functools.partial(attention_kernel, block=block),
         grid=(pairs, 2),
-        in_specs=[spec, spec, spec],
-        out_specs=[spec]
+        in_specs=[const(length, width), const(1, width), const(1, width)] + [weight] * 3,
+        out_specs=[spec] * 4
         + [
             pl.BlockSpec((1, finish, block), lambda pair, parity: (pair * 2 + parity, 0, 0))
             for finish in finishes
         ],
-        out_shape=[jax.ShapeDtypeStruct((length, width), BF16)]
+        out_shape=[wide] * 4
         + [jax.ShapeDtypeStruct((2 * pairs, finish, block), BF16) for finish in finishes],
-        scratch_shapes=[pltpu.VMEM((block, block), F32)],
+        scratch_shapes=[pltpu.VMEM((length, width), BF16), pltpu.VMEM((block, block), F32)],
         cost_estimate=LIGHT,
         name="attention",
-    )(queries, keys, values)
-    return mixed, probs
+    )(tokens, gain, shift, *weights)
+    return queries, keys, values, mixed, probs
 
 
 def attention_back_kernel(
@@ -431,49 +450,54 @@
     )(routing, cotangent)
 
 
-def project_kernel(
-    tokens_ref, gain_ref, bias_ref, wq_ref, wk_ref, wv_ref, turned_ref, q_ref, k_ref, v_ref
+def settle_kernel(
+    tokens_ref, first_gain_ref, first_bias_ref, mixed_ref, resid_ref, gain_ref, bias_ref,
+    cen_ref, chosen_ref,
+    normed_ref, turned_ref, xhat_ref, scale_ref, gate_ref,
 ):
-    normed, _, _ = normalize(tokens_ref[...].astype(F32), gain_ref[...], bias_ref[...])
-    normed = normed.astype(BF16)
-    turned_ref[...] = jnp.transpose(normed)
-    for weight, out in ((wq_ref, q_ref), (wk_ref, k_ref), (wv_ref, v_ref)):
-        out[...] = contract(normed, weight[...], 1, 0).astype(BF16)
-
-
-def project(tokens, gain, bias, weights):
+    normed, _, _ = normalize(tokens_ref[...].astype(F32), first_gain_ref[...], first_bias_ref[...])
+    normed_ref[...] = jnp.transpose(normed.astype(BF16))
+    turned_ref[...] = jnp.transpose(mixed_ref[...])
+    second, xhat, scale = normalize(resid_ref[...], gain_ref[...], bias_ref[...])
+    xhat_ref[...] = xhat.astype(BF16)
+    scale_ref[...] = scale
+    centroid = jnp.zeros_like(second)
+    for index in range(cen_ref.shape[0]):
+        centroid = jnp.where(chosen_ref[...] == index, cen_ref[index : index + 1, :], centroid)
+    gate_ref[...] = jax.nn.sigmoid(jnp.sum(second * centroid, axis=1, keepdims=True))
+
+
+def settle(tokens, first_gain, first_bias, mixed, resid, gain, bias, centroids, routing):
     length, width = tokens.shape
     rows = pl.BlockSpec((ROWS, width), lambda i: (i, 0))
-    out = jax.ShapeDtypeStruct((length, width), BF16)
-    return pl.pallas_call(
-        project_kernel,
+    thin = pl.BlockSpec((ROWS, 1), lambda i: (i, 0))
+    turned = pl.BlockSpec((width, ROWS), lambda i: (0, i))
+    vector = const(1, width)
+    column = jax.ShapeDtypeStruct((length, 1), F32)
+    return pl.pallas_call(
+        settle_kernel,
         grid=(length // ROWS,),
-        in_specs=[rows, const(1, width), const(1, width)] + [const(width, width)] * 3,
-        out_specs=[pl.BlockSpec((width, ROWS), lambda i: (0, i))] + [rows] * 3,
-        out_shape=[jax.ShapeDtypeStruct((width, length), BF16)] + [out] * 3,
-        cost_estimate=LIGHT,
-        name="project",
-    )(tokens, gain, bias, *weights)
+        in_specs=[rows, vector, vector, rows, rows, vector, vector, const(*centroids.shape), thin],
+        out_specs=[turned, turned, rows, thin, thin],
+        out_shape=[jax.ShapeDtypeStruct((width, length), BF16)] * 2
+        + [jax.ShapeDtypeStruct((length, width), BF16), column, column],
+        cost_estimate=LIGHT,
+        name="settle",
+    )(tokens, first_gain, first_bias, mixed, resid, gain, bias, centroids, routing)
 
 
 def branch_kernel(
-    mixed_ref, tokens_ref, weight_ref, gain_ref, bias_ref, cen_ref, chosen_ref, slot_ref,
-    resid_ref, gate_ref, turned_ref, send_ref, low_ref, *, blocks,
+    mixed_ref, tokens_ref, weight_ref, gain_ref, bias_ref, slot_ref,
+    resid_ref, send_ref, low_ref, *, blocks,
 ):
     step = pl.program_id(0)
 
     @pl.when(step < blocks)
     def _():
-        mixed = mixed_ref[...]
-        turned_ref[...] = jnp.transpose(mixed)
-        resid = tokens_ref[...].astype(F32) + contract(mixed, weight_ref[...], 1, 0)
+        resid = tokens_ref[...].astype(F32) + contract(mixed_ref[...], weight_ref[...], 1, 0)
         second, _, _ = normalize(resid, gain_ref[...], bias_ref[...])
         resid_ref[...] = resid
         low_ref[pl.ds(pl.multiple_of(step * ROWS, ROWS), ROWS), :] = second.astype(BF16)
-        centroid = jnp.zeros_like(second)
-        for index in range(cen_ref.shape[0]):
-            centroid = jnp.where(chosen_ref[...] == index, cen_ref[index : index + 1, :], centroid)
-        gate_ref[...] = jax.nn.sigmoid(jnp.sum(second * centroid, axis=1, keepdims=True))
 
     @pl.when(step >= blocks)
     def _():
@@ -481,7 +505,7 @@
         send_ref[...] = contract(place, low_ref[...], 1, 0).astype(BF16)
 
 
-def branch(mixed, tokens, weight, gain, bias, centroids, routing, slot, slots):
+def branch(mixed, tokens, weight, gain, bias, slot, slots):
     length, width = mixed.shape
     blocks = length // ROWS
 
@@ -489,7 +513,6 @@
         return jnp.minimum(i, blocks - 1)
 
     rows = pl.BlockSpec((ROWS, width), lambda i: (at(i), 0))
-    thin = pl.BlockSpec((ROWS, 1), lambda i: (at(i), 0))
     return pl.pallas_call(
         functools.partial(branch_kernel, blocks=blocks),
         grid=(blocks + slots // ROWS,),
@@ -499,26 +522,20 @@
             const(width, width),
             const(1, width),
             const(1, width),
-            const(*centroids.shape),
-            thin,
             const(1, length),
         ],
         out_specs=[
             rows,
-            thin,
-            pl.BlockSpec((width, ROWS), lambda i: (0, at(i))),
             pl.BlockSpec((ROWS, width), lambda i: (jnp.maximum(i - blocks, 0), 0)),
         ],
         out_shape=[
             jax.ShapeDtypeStruct((length, width), F32),
-            jax.ShapeDtypeStruct((length, 1), F32),
-            jax.ShapeDtypeStruct((width, length), BF16),
             jax.ShapeDtypeStruct((slots, width), BF16),
         ],
         scratch_shapes=[pltpu.VMEM((length, width), BF16)],
         cost_estimate=LIGHT,
         name="branch",
-    )(mixed, tokens, weight, gain, bias, centroids, routing, slot)
+    )(mixed, tokens, weight, gain, bias, slot)
 
 
 def gathered(wide_ref, rows_ref):
@@ -530,11 +547,11 @@
 
 
 def second_back_kernel(
-    core_ref, wide_ref, back_ref, resid_ref, cot_ref, gain_ref, weight_ref, turned_ref,
+    core_ref, wide_ref, back_ref, xhat_ref, scale_ref, cot_ref, gain_ref, weight_ref, turned_ref,
     grad_ref, mixed_ref, sums_ref, send_ref, keep_ref, total_ref,
 ):
     grad = gathered(wide_ref, back_ref)
-    _, xhat, scale = normalize(resid_ref[...], gain_ref[...], gain_ref[...])
+    xhat, scale = xhat_ref[...].astype(F32), scale_ref[...]
     sums = jnp.concatenate(
         [jnp.sum(grad * xhat, axis=0, keepdims=True), jnp.sum(grad, axis=0, keepdims=True)], axis=0
     )
@@ -548,8 +565,8 @@
         sums_ref[...] = sums_ref[...] + sums
 
     grad = cot_ref[...].astype(F32) + normalize_back(grad, xhat, scale, gain_ref[...])
-    grad_ref[...] = grad
     low = grad.astype(BF16)
+    grad_ref[...] = low
     mixed_ref[...] = contract(low, weight_ref[...], 1, 1).astype(BF16)
     product = contract(turned_ref[...], low, 1, 0)
 
@@ -571,8 +588,8 @@
                 out[index] = total_ref[at, columns].astype(BF16)
 
 
-def second_back(core, wide, back, resid, cotangent, gain, weight, turned, units):
-    length, width = resid.shape
+def second_back(core, wide, back, xhat, scale, cotangent, gain, weight, turned, units):
+    length, width = xhat.shape
     rows = pl.BlockSpec((ROWS, width), lambda i: (i, 0))
     own = const(width // LANES, width // 2, LANES)
     shape = jax.ShapeDtypeStruct((units, width // 2, LANES), BF16)
@@ -584,6 +601,7 @@
             pl.BlockSpec((ROWS, LANES), lambda i: (i, 0)),
             const(*back.shape),
             rows,
+            pl.BlockSpec((ROWS, 1), lambda i: (i, 0)),
             rows,
             const(1, width),
             const(width, width),
@@ -591,7 +609,7 @@
         ],
         out_specs=[rows, rows, const(2, width), own, own],
         out_shape=[
-            jax.ShapeDtypeStruct((length, width), F32),
+            jax.ShapeDtypeStruct((length, width), BF16),
             jax.ShapeDtypeStruct((length, width), BF16),
             jax.ShapeDtypeStruct((2, width), F32),
             shape,
@@ -600,7 +618,7 @@
         scratch_shapes=[pltpu.VMEM((width, width), F32)],
         cost_estimate=LIGHT,
         name="second_back",
-    )(core, wide, back, resid, cotangent, gain, weight, turned)
+    )(core, wide, back, xhat, scale, cotangent, gain, weight, turned)
 
 
 def first_back_kernel(
@@ -626,7 +644,7 @@
     def _():
         sums_ref[...] = sums_ref[...] + sums
 
-    grad_ref[...] = resid_ref[...] + normalize_back(grad, xhat, scale, gain)
+    grad_ref[...] = resid_ref[...].astype(F32) + normalize_back(grad, xhat, scale, gain)
 
 
 def first_back(left, right, tokens, resid, gain, weights):
@@ -807,29 +825,43 @@
             self.steps = [("whole", stages[0])]
             self.steps += [("halve", stage) for stage in stages[1:-1]]
             self.steps += [("whole", stages[-1])]
-            self.steps += [("join", stage) for stage in stages[-2:0:-1]]
+            self.steps += [("join", stage) for stage in stages[-2:2:-1]]
+            self.steps += [("both", stages[2:0:-1]), ("corner", stages[2:0:-1])]
         else:
             self.steps = [("whole", stage) for stage in stages]
 
     def start(self):
-        return swap(self.send, *self.steps[0][1])
+        kind, stage = self.steps[0]
+        if kind == "both":
+            return [swap(self.keep, *each) for each in stage]
+        if kind == "corner":
+            near, far = self.got
+            half = near.shape[0] // 2
+            return [swap(near[:half], *stage[1]), swap(far[half:], *stage[0])]
+        return [swap(self.send, *stage)]
 
     def finish(self, got):
         kind, stage = self.steps.pop(0)
-        if self.steps and self.steps[0][0] == "halve":
-            self.send, self.keep = add_split(self.keep, got, self.steps[0][1])
+        if kind == "both":
+            self.got = got
+        elif kind == "corner":
+            near, far = self.got
+            mine = joined(self.keep, near, stage[0])
+            other = joined(far, jnp.concatenate(got, axis=0), stage[0])
+            self.keep = joined(mine, other, stage[1])
+        elif self.steps and self.steps[0][0] == "halve":
+            self.send, self.keep = add_split(self.keep, got[0], self.steps[0][1])
         else:
             join = functools.partial(joined, stage=stage)
-            self.keep = self.send = (join if kind == "join" else self.plus)(self.keep, got)
+            self.keep = self.send = (join if kind == "join" else self.plus)(self.keep, got[0])
 
 
 def advance(sums, *others):
     sums = [each for each in sums if each.steps]
-    tied = tie((*(each.start() for each in sums), *others))
-    for each, got in zip(sums, tied):
-        each.finish(got)
-    rest = tied[len(sums) :]
-    return rest[0] if len(rest) == 1 else rest
+    got, others = tie(([each.start() for each in sums], others))
+    for each, arrived in zip(sums, got):
+        each.finish(arrived)
+    return others[0] if len(others) == 1 else others
 
 
 def chip_stages(total):
@@ -874,15 +906,17 @@
     cots, tokens = tie((cots, tokens))
     cots = exchange(cots.reshape(peers, -1, width)).reshape(slots, width)
 
-    normed_turned, queries, keys, values = project(tokens, first_gain, first_bias, weights)
-    mixed, probs = attention(queries, keys, values)
-    mixed, cots = tie((mixed, cots))
-    resid, gate, mixed_turned, rows = branch(
-        mixed, tokens, output_weight, second_gain, second_bias, centroids, routing, slot, slots
-    )
-
+    queries, keys, values, mixed, probs = attention(tokens, first_gain, first_bias, weights)
+    resid, rows = branch(mixed, tokens, output_weight, second_gain, second_bias, slot, slots)
+
+    rows, cots = tie((rows, cots))
     rows = exchange(rows.reshape(peers, -1, width))
-    rows, cots_down = tie((rows, expert_cots(cots, expert_down)))
+    cots_down = expert_cots(cots, expert_down)
+    settled = settle(
+        tokens, first_gain, first_bias, mixed, resid, second_gain, second_bias, centroids, routing
+    )
+    rows, cots_down, *settled = tie((rows, cots_down, *settled))
+    normed_turned, mixed_turned, xhat, scale, gate = settled
     rows = rows.reshape(slots, width)
     own = centroids[lax.axis_index("expert")][None, :]
     produced, returned, grad_rows, hidden, grad_pre = expert(
@@ -906,7 +940,7 @@
     pairs = width // LANES
     split = pairs // 2
     grad_resid, grad_mixed, second_sums, *units = second_back(
-        core, wide, returned, resid, cotangent, second_gain, output_weight, mixed_turned,
+        core, wide, returned, xhat, scale, cotangent, second_gain, output_weight, mixed_turned,
         pairs + 3 * split,
     )
 
@@ -939,14 +973,15 @@
     grad_up, grad_down = (value.reshape(value.shape[1:])[None] for value in (grad_up, grad_down))
     small = jnp.concatenate([first_sums, second_sums], axis=0)
     small = Sum(small, small, stages("dp", 1, 1 << 20) + cross, plus=add, split=False)
-    while len(early.steps) > 1:
+    while len(early.steps) > 2:
         advance([early, late, small])
-    got = early.start()
-    grad_up, grad_down = advance([late, small], grad_up, grad_down)
-    while len(late.steps) > 2:
-        advance([late, small])
-    early.finish(advance([late, small], got))
-    outs = assemble(core, early.keep, swap(early.keep, "dp", 1), width, [])
+    grad_up, grad_down = advance([early, late, small], grad_up, grad_down)
+    while early.steps:
+        advance([early, late, small])
+    core_swap = swap(early.keep, "dp", 1)
+    while len(late.steps) > 1:
+        core_swap = advance([late, small], core_swap)
+    outs = assemble(core, early.keep, core_swap, width, [])
     grad_output, *outs = advance([late, small], *outs)
     while small.steps:
         advance([small])

time: 344 us -> 337 us (0.980)
  waiting for transfers between devices: 79.3 us -> 55.5 us
  starting transfers between devices: 41 us -> 47.2 us
  Pallas kernels: 203 us -> 209 us
    ppermute x27 -> x31, waiting for transfers between devices: 48.3 us -> 34.4 us  [swap(): return lax.ppermute(value, axis, [(i, i ^ bit) for i in range(size)])]
    all_to_all x4, waiting for transfers between devices: 31 us -> 21.1 us  [exchange(): lax.all_to_all(rows, 'expert', split_axis=0, concat_axis=0, tiled=True)]
    pallas_call x1, Pallas kernels: 25.7 us -> 34 us  [attention(): pl.pallas_call(functools.partial(attention_kernel, block=block), grid=(pa...]
    ppermute x27 -> x31, starting transfers between devices: 21.5 us -> 26.3 us  [swap(): return lax.ppermute(value, axis, [(i, i ^ bit) for i in range(size)])]
    unnamed x49 -> x55, local copies, waits for them, and re-layouts: 6.95 us -> 6.99 us
  transfers between devices with their start and end apart: 31 -> 35, of which waited for: 21 -> 16; matrix products, arithmetic and copies ran while one was open for 3% -> 4% of each run, Pallas kernels for 44% -> 50%
where the time goes in v3:
time: 337 us; the launch traced here: 336 us
  Pallas kernels  209 us (62%)
  waiting for transfers between devices  55.5 us (16%)
  starting transfers between devices  47.2 us (14%)
  local copies, waits for them, and re-layouts  13 us (4%)
  other arithmetic  10 us (3%)
    pallas_call x2, Pallas kernels, attention_back(): pl.pallas_call(functools.partial(attention_back_kernel, block=block, bloc...  36.4 us
    ppermute x31, waiting for transfers between devices, swap(): return lax.ppermute(value, axis, [(i, i ^ bit) for i in range(size)])  34.4 us
    pallas_call x1, Pallas kernels, attention(): pl.pallas_call(functools.partial(attention_kernel, block=block), grid=(pa...  34 us
    pallas_call x1, Pallas kernels, expert(): pl.pallas_call(expert_kernel, grid=(hidden // tile,), in_specs=[whole, wh...  26.8 us
    ppermute x31, starting transfers between devices, swap(): return lax.ppermute(value, axis, [(i, i ^ bit) for i in range(size)])  26.3 us
    pallas_call x8, Pallas kernels, add_split(): pl.pallas_call(add_split_kernel, grid_spec=pltpu.PrefetchScalarGridSpec(n...  23 us
    all_to_all x4, waiting for transfers between devices, exchange(): lax.all_to_all(rows, 'expert', split_axis=0, concat_axis=0, tiled=True)  21.1 us
    all_to_all x4, starting transfers between devices, exchange(): lax.all_to_all(rows, 'expert', split_axis=0, concat_axis=0, tiled=True)  20.9 us
  transfers between devices with their start and end apart: 35, of which 16 were waited for; matrix products, arithmetic and copies ran while one was open for 4% of the time, Pallas kernels for 50%

profile of v3, /device:TPU:0, one launch (start us, length us, event | category | flops | bytes accessed | tf_op | source)
XLA Modules:
  0.0 335.7 jit_solution(9258190576337357160)
XLA Ops:
  0.6 5.4 %route.1 = (bf16[1024,768]{1,0:T(8,128)(2,1)}, s32[1,1024]{1,0:T(1,128)}, s32[1024,128]{1,0:T(8,128)}) custom-call(s32[1,1024]{1,0:T(1,128)} %bitcast.51, bf16[1024,768]{1,0:T(8,128)(2,1)} %cot_ref.3), custom_call_target="tpu_custom_call" | custom-call | flops 1000000 | bytes 100000 | tf_op jit(solution)/shard_map/route/pallas_call | solution.py:434
  6.1 7.5 %all-to-all-start = ((bf16[8,128,768]{2,1,0:T(8,128)(2,1)}), bf16[8,128,768]{2,1,0:T(8,128)(2,1)S(1)}, u32[]{:S(2)}, u32[]{:S(2)}) async-start(bf16[8,128,768]{2,1,0:T(8,128)(2,1)} %bitcast.43), calls=%async_computation | async-start | bytes 3145728 | tf_op jit(solution)/shard_map/all_to_all | solution.py:875
  14.3 34.0 %attention.1 = (bf16[1024,768]{1,0:T(8,128)(2,1)}, bf16[1024,768]{1,0:T(8,128)(2,1)}, bf16[1024,768]{1,0:T(8,128)(2,1)}, bf16[1024,768]{1,0:T(8,128)(2,1)}, bf16...) custom-call(bf16[1024,768]{1,0:T(8,128)(2,1)} %tokens_ref.3, ...), custom_call_target="tpu_custom_call" | custom-call | flops 1000000 | bytes 100000 | tf_op jit(solution)/shard_map/attention/pallas_call | solution.py:112
  48.3 8.9 %branch.1 = (f32[1024,768]{1,0:T(8,128)}, bf16[1024,768]{1,0:T(8,128)(2,1)}) custom-call(bf16[1024,768]{1,0:T(8,128)(2,1)} %get-tuple-element.146.mixed_ref.o_ref, bf16[1024,768]{1,0:T(8,128)(2,1)} %tokens_ref.3, bf16[768,768]{1,0:T(8,128)(2,1)} %weight_ref.3, f32[1,768]{1,0:T(1,128)} %get-tuple-element.289.gain_ref, f32[1,768]{1,0:T(1,128)} %get-tuple-element.288.bias_ref, ...), custom_call_target="tpu_custom_call" | custom-call | flops 1000000 | bytes 100000 | tf_op jit(solution)/shard_map/branch/pallas_call | solution.py:516
  58.3 6.0 %all-to-all-start.1 = ((bf16[8,128,768]{2,1,0:T(8,128)(2,1)}), bf16[8,128,768]{2,1,0:T(8,128)(2,1)S(1)}, u32[]{:S(2)}, u32[]{:S(2)}) async-start(bf16[8,128,768]{2,1,0:T(8,128)(2,1)} %bitcast.44), calls=%async_computation.1 | async-start | bytes 3145728 | tf_op jit(solution)/shard_map/all_to_all | solution.py:875
  65.3 7.7 %settle.1 = (bf16[768,1024]{1,0:T(8,128)(2,1)}, bf16[768,1024]{1,0:T(8,128)(2,1)}, bf16[1024,768]{1,0:T(8,128)(2,1)}, f32[1024,1]{1,0:T(8,128)}, f32[1024,1]{1,0:T(8,128)}) custom-call(bf16[1024,768]{1,0:T(8,128)(2,1)} %tokens_ref.3, f32[1,768]{1,0:T(1,128)} %get-tuple-element.291.gain_ref.first_gain_ref, ...), custom_call_target="tpu_custom_call" | custom-call | flops 1000000 | bytes 100000 | tf_op jit(solution)/shard_map/settle/pallas_call | solution.py:477
  74.4 10.0 %expert_cots.1.cd_ref = bf16[1024,3072]{1,0:T(8,128)(2,1)} custom-call(bf16[1024,768]{1,0:T(8,128)(2,1)} %bitcast.30, bf16[1,3072,768]{2,1,0:T(8,128)(2,1)} %down_ref.3), custom_call_target="tpu_custom_call" | custom-call | flops 1000000 | bytes 100000 | tf_op jit(solution)/shard_map/expert_cots/pallas_call | solution.py:242
  84.4 16.4 %all-to-all-done.1 = bf16[8,128,768]{2,1,0:T(8,128)(2,1)S(1)} async-done(((bf16[8,128,768]{2,1,0:T(8,128)(2,1)}), bf16[8,128,768]{2,1,0:T(8,128)(2,1)S(1)}, u32[]{:S(2)}, u32[]{:S(2)}) %all-to-all-start.1) | async-done | bytes 1572896 | tf_op jit(solution)/shard_map/all_to_all | solution.py:875
  101.9 26.8 %expert.1 = (bf16[1024,768]{1,0:T(8,128)(2,1)}, bf16[1024,768]{1,0:T(8,128)(2,1)}, bf16[1024,768]{1,0:T(8,128)(2,1)}, bf16[1024,3072]{1,0:T(8,128)(2,1)}, bf16[1024,3072]{1,0:T(8,128)(2,1)}) custom-call(bf16[1024,768]{1,0:T(8,128)(2,1)} %bitcast.32, bf16[1024,768]{1,0:T(8,128)(2,1)} %bitcast.31, bf16[1024,3072]{1,0:T(8,128)(2,1)} %expert_cots.1.cd_ref, ...), custom_call_target="tpu_custom_call" | custom-call | flops 1000000 | bytes 100000 | tf_op jit(solution)/shard_map/expert/pallas_call | solution.py:301
  128.7 3.6 %all-to-all-start.2 = ((bf16[8,128,768]{2,1,0:T(8,128)(2,1)}), bf16[8,128,768]{2,1,0:T(8,128)(2,1)S(1)}, u32[]{:S(2)}, u32[]{:S(2)}) async-start(bf16[8,128,768]{2,1,0:T(8,128)(2,1)} %bitcast.42), calls=%async_computation.2 | async-start | bytes 3145728 | tf_op jit(solution)/shard_map/all_to_all | solution.py:875
  132.3 18.9 %expert_weights.1 = (bf16[2,768,768]{2,1,0:T(8,128)(2,1)}, bf16[2,768,768]{2,1,0:T(8,128)(2,1)}, bf16[2,768,768]{2,1,0:T(8,128)(2,1)}, bf16[2,768,768]{2,1,0:T(8,128)(2,1)}) custom-call(s32[1]{0:T(128)} %bitcast.2.core_ref, bf16[1024,768]{1,0:T(8,128)(2,1)} %bitcast.33, bf16[1024,768]{1,0:T(8,128)(2,1)} %get-tuple-element.162.dy_ref, ...), custom_call_target="tpu_custom_call" | custom-call | flops 1000000 | bytes 100000 | tf_op jit(solution)/shard_map/expert_weights/pallas_call | solution.py:379
  151.7 4.4 %collective-permute-done = bf16[2,768,768]{2,1,0:T(8,128)(2,1)} collective-permute-done((bf16[2,768,768]{2,1,0:T(8,128)(2,1)}, bf16[2,768,768]{2,1,0:T(8,128)(2,1)}, u32[]{:S(2)}, u32[]{:S(2)}) %collective-permute-start) | collective-permute-done | bytes 2359328 | tf_op jit(solution)/shard_map/ppermute | solution.py:742
  156.1 4.4 %add_split.8 = (bf16[768,768]{1,0:T(8,128)(2,1)}, bf16[768,768]{1,0:T(8,128)(2,1)}) custom-call(s32[1]{0:T(128)} %bitcast.9.mine_ref, bf16[1536,768]{1,0:T(8,128)(2,1)} %bitcast.40, bf16[1536,768]{1,0:T(8,128)(2,1)} %bitcast.11.right_ref), custom_call_target="tpu_custom_call" | custom-call | flops 1000000 | bytes 100000 | tf_op jit(solution)/shard_map/add_split/pallas_call | solution.py:801
  160.5 4.4 %add_split.9 = (bf16[768,768]{1,0:T(8,128)(2,1)}, bf16[768,768]{1,0:T(8,128)(2,1)}) custom-call(s32[1]{0:T(128)} %bitcast.9.mine_ref, bf16[1536,768]{1,0:T(8,128)(2,1)} %bitcast.39, bf16[1536,768]{1,0:T(8,128)(2,1)} %bitcast.15.right_ref), custom_call_target="tpu_custom_call" | custom-call | flops 1000000 | bytes 100000 | tf_op jit(solution)/shard_map/add_split/pallas_call | solution.py:801
  164.8 4.7 %all-to-all-done.2 = bf16[8,128,768]{2,1,0:T(8,128)(2,1)S(1)} async-done(((bf16[8,128,768]{2,1,0:T(8,128)(2,1)}), bf16[8,128,768]{2,1,0:T(8,128)(2,1)S(1)}, u32[]{:S(2)}, u32[]{:S(2)}) %all-to-all-start.2) | async-done | bytes 1572896 | tf_op jit(solution)/shard_map/all_to_all | solution.py:875
  171.0 3.8 %all-to-all-start.3 = ((bf16[8,128,768]{2,1,0:T(8,128)(2,1)}), bf16[8,128,768]{2,1,0:T(8,128)(2,1)S(1)}, u32[]{:S(2)}, u32[]{:S(2)}) async-start(bf16[8,128,768]{2,1,0:T(8,128)(2,1)} %bitcast.41), calls=%async_computation.3 | async-start | bytes 3145728 | tf_op jit(solution)/shard_map/all_to_all | solution.py:875
  174.8 13.1 %second_back.1 = (bf16[1024,768]{1,0:T(8,128)(2,1)}, bf16[1024,768]{1,0:T(8,128)(2,1)}, f32[2,768]{1,0:T(2,128)}, bf16[15,384,128]{2,1,0:T(8,128)(2,1)}, bf16[15,384,128]{2,1,0:T(8,128)(2,1)}) custom-call(s32[1]{0:T(128)} %bitcast.2.core_ref, s32[1024,128]{1,0:T(8,128)} %get-tuple-element.145.wide_ref, bf16[1024,768]{1,0:T(8,128)(2,1)} %bitcast.35, ...), custom_call_target="tpu_custom_call" | custom-call | flops 1000000 | bytes 100000 | tf_op jit(solution)/shard_map/second_back/pallas_call | solution.py:596
  187.9 18.2 %attention_back.2 = (bf16[3,1024,384]{2,1,0:T(8,128)(2,1)}, bf16[15,384,128]{2,1,0:T(8,128)(2,1)}, bf16[15,384,128]{2,1,0:T(8,128)(2,1)}) custom-call(s32[1]{0:T(128)} %bitcast.2.core_ref, bf16[1024,768]{1,0:T(8,128)(2,1)} %get-tuple-element.142.q_ref, bf16[1024,768]{1,0:T(8,128)(2,1)} %get-tuple-element.143.k_ref, ...), custom_call_target="tpu_custom_call", output_to_operand_aliasing={{1}: (11, {}), {2}: (12, {})} | custom-call | flops 1000000 | bytes 100000 | tf_op jit(solution)/shard_map/attention_back/pallas_call | solution.py:208
  217.1 18.2 %attention_back.3 = (bf16[3,1024,384]{2,1,0:T(8,128)(2,1)}, bf16[9,384,128]{2,1,0:T(8,128)(2,1)}, bf16[9,384,128]{2,1,0:T(8,128)(2,1)}) custom-call(s32[1]{0:T(128)} %bitcast.2.core_ref, bf16[1024,768]{1,0:T(8,128)(2,1)} %get-tuple-element.142.q_ref, bf16[1024,768]{1,0:T(8,128)(2,1)} %get-tuple-element.143.k_ref, ...), custom_call_target="tpu_custom_call" | custom-call | flops 1000000 | bytes 100000 | tf_op jit(solution)/shard_map/attention_back/pallas_call | solution.py:208
  240.0 6.0 %layer_output.1 = bf16[1024,768]{1,0:T(8,128)(2,1)} custom-call(s32[1024,128]{1,0:T(8,128)} %get-tuple-element.145.wide_ref, bf16[1024,768]{1,0:T(8,128)(2,1)} %bitcast.34, f32[1024,768]{1,0:T(8,128)} %get-tuple-element.152.resid_ref, f32[1024,1]{1,0:T(8,128)} %get-tuple-element.206.gate_ref), custom_call_target="tpu_custom_call" | custom-call | flops 1000000 | bytes 100000 | tf_op jit(solution)/shard_map/layer_output/pallas_call | solution.py:678
  256.9 10.7 %first_back.1 = (f32[1024,768]{1,0:T(8,128)}, f32[2,768]{1,0:T(2,128)}) custom-call(bf16[3,1024,384]{2,1,0:T(8,128)(2,1)} %get-tuple-element.215.left_ref, bf16[3,1024,384]{2,1,0:T(8,128)(2,1)} %get-tuple-element.216.right_ref, bf16[1024,768]{1,0:T(8,128)(2,1)} %tokens_ref.3, bf16[1024,768]{1,0:T(8,128)(2,1)} %get-tuple-element.217.resid_ref, ...), custom_call_target="tpu_custom_call" | custom-call | flops 1000000 | bytes 100000 | tf_op jit(solution)/shard_map/first_back/pallas_call | solution.py:653
  292.0 4.7 %collective-permute-done.19 = f32[4,768]{1,0:T(4,128)S(1)} collective-permute-done((f32[4,768]{1,0:T(4,128)S(1)}, f32[4,768]{1,0:T(4,128)S(1)}, u32[]{:S(2)}, u32[]{:S(2)}) %collective-permute-start.19) | collective-permute-done | bytes 12320 | tf_op jit(solution)/shard_map/ppermute | solution.py:742
  309.9 4.0 %collective-permute-done.26 = f32[4,768]{1,0:T(4,128)S(1)} collective-permute-done((f32[4,768]{1,0:T(4,128)S(1)}, f32[4,768]{1,0:T(4,128)S(1)}, u32[]{:S(2)}, u32[]{:S(2)}) %collective-permute-start.26) | collective-permute-done | bytes 12320 | tf_op jit(solution)/shard_map/ppermute | solution.py:742
  322.1 4.7 %assemble.2 = (f32[768,768]{1,0:T(8,128)}, f32[768,768]{1,0:T(8,128)}, f32[768,768]{1,0:T(8,128)}, f32[768,768]{1,0:T(8,128)}) custom-call(s32[1]{0:T(128)} %bitcast.2.core_ref, bf16[15,384,128]{2,1,0:T(8,128)(2,1)} %bitcast.36, bf16[15,384,128]{2,1,0:T(8,128)(2,1)} %bitcast.45), custom_call_target="tpu_custom_call" | custom-call | flops 1000000 | bytes 100000 | tf_op jit(solution)/shard_map/assemble/pallas_call | solution.py:724
  (161 shorter events, 88.3 us)
Async XLA Ops:
  6.1 51.1 %all-to-all-start = ((bf16[8,128,768]{2,1,0:T(8,128)(2,1)}), bf16[8,128,768]{2,1,0:T(8,128)(2,1)S(1)}, u32[]{:S(2)}, u32[]{:S(2)}) async-start(bf16[8,128,768]{2,1,0:T(8,128)(2,1)} %bitcast.43), calls=%async_computation | async-start | bytes 3145728 | tf_op jit(solution)/shard_map/all_to_all | solution.py:875
  58.3 42.4 %all-to-all-start.1 = ((bf16[8,128,768]{2,1,0:T(8,128)(2,1)}), bf16[8,128,768]{2,1,0:T(8,128)(2,1)S(1)}, u32[]{:S(2)}, u32[]{:S(2)}) async-start(bf16[8,128,768]{2,1,0:T(8,128)(2,1)} %bitcast.44), calls=%async_computation.1 | async-start | bytes 3145728 | tf_op jit(solution)/shard_map/all_to_all | solution.py:875
  128.7 40.8 %all-to-all-start.2 = ((bf16[8,128,768]{2,1,0:T(8,128)(2,1)}), bf16[8,128,768]{2,1,0:T(8,128)(2,1)S(1)}, u32[]{:S(2)}, u32[]{:S(2)}) async-start(bf16[8,128,768]{2,1,0:T(8,128)(2,1)} %bitcast.42), calls=%async_computation.2 | async-start | bytes 3145728 | tf_op jit(solution)/shard_map/all_to_all | solution.py:875
  151.2 9.3 %collective-permute-start.1 = (bf16[2,768,768]{2,1,0:T(8,128)(2,1)}, bf16[2,768,768]{2,1,0:T(8,128)(2,1)}, u32[]{:S(2)}, u32[]{:S(2)}) collective-permute-start(bf16[2,768,768]{2,1,0:T(8,128)(2,1)} %get-tuple-element.170), channel_id=1, source_target_pairs={{0,8},{8,0},{16,24},{24,16},{1,9},{9,1},{17,25},{25,17},{2,10},{10... | collective-permute-start | bytes 7077896 | tf_op jit(solution)/shard_map/ppermute | solution.py:742
  169.5 36.6 %collective-permute-start.2 = (bf16[1,768,768]{2,1,0:T(8,128)(2,1)}, bf16[1,768,768]{2,1,0:T(8,128)(2,1)}, u32[]{:S(2)}, u32[]{:S(2)}) collective-permute-start(bf16[1,768,768]{2,1,0:T(8,128)(2,1)} %bitcast.12), channel_id=1, source_target_pairs={{0,16},{8,24},{16,0},{24,8},{1,17},{9,25},{17,1},{25,9},{2,18},{10... | collective-permute-start | bytes 3538952 | tf_op jit(solution)/shard_map/ppermute | solution.py:742
  171.0 64.3 %all-to-all-start.3 = ((bf16[8,128,768]{2,1,0:T(8,128)(2,1)}), bf16[8,128,768]{2,1,0:T(8,128)(2,1)S(1)}, u32[]{:S(2)}, u32[]{:S(2)}) async-start(bf16[8,128,768]{2,1,0:T(8,128)(2,1)} %bitcast.41), calls=%async_computation.3 | async-start | bytes 3145728 | tf_op jit(solution)/shard_map/all_to_all | solution.py:875
  214.1 21.2 %collective-permute-start.4 = (bf16[2880,128]{1,0:T(8,128)(2,1)}, bf16[2880,128]{1,0:T(8,128)(2,1)S(1)}, u32[]{:S(2)}, u32[]{:S(2)}) collective-permute-start(bf16[2880,128]{1,0:T(8,128)(2,1)} %get-tuple-element.193), channel_id=1, source_target_pairs={{0,1},{1,0},{2,3},{3,2},{4,5},{5,4},{6,7},{7,6},{8,9},{9,8},{10,11... | collective-permute-start | bytes 2211848 | tf_op jit(solution)/shard_map/ppermute | solution.py:742
  215.9 30.1 %collective-permute-start.7 = (bf16[1,768,768]{2,1,0:T(8,128)(2,1)}, bf16[1,768,768]{2,1,0:T(8,128)(2,1)S(1)}, u32[]{:S(2)}, u32[]{:S(2)}) collective-permute-start(bf16[1,768,768]{2,1,0:T(8,128)(2,1)} %bitcast.52), channel_id=1, source_target_pairs={{0,16},{8,24},{16,0},{24,8},{1,17},{9,25},{17,1},{25,9},{2,18},{10... | collective-permute-start | bytes 3538952 | tf_op jit(solution)/shard_map/ppermute | solution.py:742
  235.3 13.6 %collective-permute-start.6 = (bf16[3456,128]{1,0:T(8,128)(2,1)}, bf16[3456,128]{1,0:T(8,128)(2,1)}, u32[]{:S(2)}, u32[]{:S(2)}) collective-permute-start(bf16[3456,128]{1,0:T(8,128)(2,1)} %bitcast.53), channel_id=1, source_target_pairs={{0,8},{8,0},{16,24},{24,16},{1,9},{9,1},{17,25},{25,17},{2,10},{10... | collective-permute-start | bytes 2654216 | tf_op jit(solution)/shard_map/ppermute | solution.py:742
  238.6 10.4 %collective-permute-start.5 = (bf16[1440,128]{1,0:T(8,128)(2,1)}, bf16[1440,128]{1,0:T(8,128)(2,1)S(1)}, u32[]{:S(2)}, u32[]{:S(2)}) collective-permute-start(bf16[1440,128]{1,0:T(8,128)(2,1)} %get-tuple-element.203), channel_id=1, source_target_pairs={{0,2},{1,3},{2,0},{3,1},{4,6},{5,7},{6,4},{7,5},{8,10},{9,11},{10,... | collective-permute-start | bytes 1105928 | tf_op jit(solution)/shard_map/ppermute | solution.py:742
  251.6 15.9 %collective-permute-start.9 = (bf16[1728,128]{1,0:T(8,128)(2,1)}, bf16[1728,128]{1,0:T(8,128)(2,1)S(1)}, u32[]{:S(2)}, u32[]{:S(2)}) collective-permute-start(bf16[1728,128]{1,0:T(8,128)(2,1)} %get-tuple-element.214), channel_id=1, source_target_pairs={{0,16},{8,24},{16,0},{24,8},{1,17},{9,25},{17,1},{25,9},{2,18},{10... | collective-permute-start | bytes 1327112 | tf_op jit(solution)/shard_map/ppermute | solution.py:742
  254.5 13.0 %collective-permute-start.8 = (bf16[720,128]{1,0:T(8,128)(2,1)}, bf16[720,128]{1,0:T(8,128)(2,1)S(1)}, u32[]{:S(2)}, u32[]{:S(2)}) collective-permute-start(bf16[720,128]{1,0:T(8,128)(2,1)} %get-tuple-element.211), channel_id=1, source_target_pairs={{0,4},{1,5},{2,6},{3,7},{4,0},{5,1},{6,2},{7,3},{8,12},{9,13},{10,... | collective-permute-start | bytes 552968 | tf_op jit(solution)/shard_map/ppermute | solution.py:742
  270.5 7.1 %collective-permute-start.11 = (bf16[864,128]{1,0:T(8,128)(2,1)}, bf16[864,128]{1,0:T(8,128)(2,1)S(1)}, u32[]{:S(2)}, u32[]{:S(2)}) collective-permute-start(bf16[864,128]{1,0:T(8,128)(2,1)} %get-tuple-element.226), channel_id=1, source_target_pairs={{0,2},{1,3},{2,0},{3,1},{4,6},{5,7},{6,4},{7,5},{8,10},{9,11},{10,... | collective-permute-start | bytes 663560 | tf_op jit(solution)/shard_map/ppermute | solution.py:742
  277.7 9.2 %collective-permute-start.13 = (bf16[720,128]{1,0:T(8,128)(2,1)S(1)}, bf16[720,128]{1,0:T(8,128)(2,1)S(1)}, u32[]{:S(2)}, u32[]{:S(2)}) collective-permute-start(bf16[720,128]{1,0:T(8,128)(2,1)S(1)} %add_convert_fusion), channel_id=1, source_target_pairs={{0,4},{1,5},{2,6},{3,7},{4,0},{5,1},{6,2},{7,3},{8,12},{9,13},{10,... | collective-permute-start | bytes 552968 | tf_op jit(solution)/shard_map/ppermute | solution.py:742
  286.9 11.8 %collective-permute-start.16 = (bf16[1440,128]{1,0:T(8,128)(2,1)S(1)}, bf16[1440,128]{1,0:T(8,128)(2,1)S(1)}, u32[]{:S(2)}, u32[]{:S(2)}) collective-permute-start(bf16[1440,128]{1,0:T(8,128)(2,1)S(1)} %pad_maximum_fusion.6), channel_id=1, source_target_pairs={{0,2},{1,3},{2,0},{3,1},{4,6},{5,7},{6,4},{7,5},{8,10},{9,11},{10,... | collective-permute-start | bytes 1105928 | tf_op jit(solution)/shard_map/ppermute | solution.py:742
  287.0 11.7 %collective-permute-start.17 = (bf16[1440,128]{1,0:T(8,128)(2,1)S(1)}, bf16[1440,128]{1,0:T(8,128)(2,1)S(1)}, u32[]{:S(2)}, u32[]{:S(2)}) collective-permute-start(bf16[1440,128]{1,0:T(8,128)(2,1)S(1)} %pad_maximum_fusion.6), channel_id=1, source_target_pairs={{0,1},{1,0},{2,3},{3,2},{4,5},{5,4},{6,7},{7,6},{8,9},{9,8},{10,11... | collective-permute-start | bytes 1105928 | tf_op jit(solution)/shard_map/ppermute | solution.py:742
  287.7 9.0 %collective-permute-start.18 = (bf16[432,128]{1,0:T(8,128)(2,1)S(1)}, bf16[432,128]{1,0:T(8,128)(2,1)S(1)}, u32[]{:S(2)}, u32[]{:S(2)}) collective-permute-start(bf16[432,128]{1,0:T(8,128)(2,1)S(1)} %add_convert_fusion.3), channel_id=1, source_target_pairs={{0,4},{1,5},{2,6},{3,7},{4,0},{5,1},{6,2},{7,3},{8,12},{9,13},{10,... | collective-permute-start | bytes 331784 | tf_op jit(solution)/shard_map/ppermute | solution.py:742
  289.5 7.2 %collective-permute-start.19 = (f32[4,768]{1,0:T(4,128)S(1)}, f32[4,768]{1,0:T(4,128)S(1)}, u32[]{:S(2)}, u32[]{:S(2)}) collective-permute-start(f32[4,768]{1,0:T(4,128)S(1)} %add.78), channel_id=1, source_target_pairs={{0,1},{1,0},{2,3},{3,2},{4,5},{5,4},{6,7},{7,6},{8,9},{9,8},{10,11... | collective-permute-start | bytes 36872 | tf_op jit(solution)/shard_map/ppermute | solution.py:742
  298.8 7.7 %collective-permute-start.20 = (bf16[720,128]{1,0:T(8,128)(2,1)S(1)}, bf16[720,128]{1,0:T(8,128)(2,1)S(1)}, u32[]{:S(2)}, u32[]{:S(2)}) collective-permute-start(bf16[720,128]{1,0:T(8,128)(2,1)S(1)} %slice.40), channel_id=1, source_target_pairs={{0,1},{1,0},{2,3},{3,2},{4,5},{5,4},{6,7},{7,6},{8,9},{9,8},{10,11... | collective-permute-start | bytes 552968 | tf_op jit(solution)/shard_map/ppermute | solution.py:742
  307.0 9.2 %collective-permute-start.27 = (bf16[5760,128]{1,0:T(8,128)(2,1)S(1)}, bf16[5760,128]{1,0:T(8,128)(2,1)S(1)}, u32[]{:S(2)}, u32[]{:S(2)}) collective-permute-start(bf16[5760,128]{1,0:T(8,128)(2,1)S(1)} %pad_maximum_fusion), channel_id=1, source_target_pairs={{0,8},{8,0},{16,24},{24,16},{1,9},{9,1},{17,25},{25,17},{2,10},{10... | collective-permute-start | bytes 4423688 | tf_op jit(solution)/shard_map/ppermute | solution.py:742
  308.0 8.3 %collective-permute-start.24 = (bf16[864,128]{1,0:T(8,128)(2,1)}, bf16[864,128]{1,0:T(8,128)(2,1)}, u32[]{:S(2)}, u32[]{:S(2)}) collective-permute-start(bf16[864,128]{1,0:T(8,128)(2,1)} %pad_maximum_fusion.7), channel_id=1, source_target_pairs={{0,2},{1,3},{2,0},{3,1},{4,6},{5,7},{6,4},{7,5},{8,10},{9,11},{10,... | collective-permute-start | bytes 663560 | tf_op jit(solution)/shard_map/ppermute | solution.py:742
  308.2 8.1 %collective-permute-start.25 = (bf16[864,128]{1,0:T(8,128)(2,1)}, bf16[864,128]{1,0:T(8,128)(2,1)S(1)}, u32[]{:S(2)}, u32[]{:S(2)}) collective-permute-start(bf16[864,128]{1,0:T(8,128)(2,1)} %pad_maximum_fusion.7), channel_id=1, source_target_pairs={{0,16},{8,24},{16,0},{24,8},{1,17},{9,25},{17,1},{25,9},{2,18},{10... | collective-permute-start | bytes 663560 | tf_op jit(solution)/shard_map/ppermute | solution.py:742
  317.9 8.8 %collective-permute-start.28 = (bf16[432,128]{1,0:T(8,128)(2,1)}, bf16[432,128]{1,0:T(8,128)(2,1)S(1)}, u32[]{:S(2)}, u32[]{:S(2)}) collective-permute-start(bf16[432,128]{1,0:T(8,128)(2,1)} %slice.42), channel_id=1, source_target_pairs={{0,16},{8,24},{16,0},{24,8},{1,17},{9,25},{17,1},{25,9},{2,18},{10... | collective-permute-start | bytes 331784 | tf_op jit(solution)/shard_map/ppermute | solution.py:742
  319.1 7.7 %collective-permute-start.29 = (bf16[432,128]{1,0:T(8,128)(2,1)}, bf16[432,128]{1,0:T(8,128)(2,1)}, u32[]{:S(2)}, u32[]{:S(2)}) collective-permute-start(bf16[432,128]{1,0:T(8,128)(2,1)} %slice.43), channel_id=1, source_target_pairs={{0,2},{1,3},{2,0},{3,1},{4,6},{5,7},{6,4},{7,5},{8,10},{9,11},{10,... | collective-permute-start | bytes 331784 | tf_op jit(solution)/shard_map/ppermute | solution.py:742
  (37 other events, 207.1 us)

commit v4 on v3

--- a/solution.py
+++ b/solution.py
@@ -53,33 +53,38 @@
         bias_ref[...] = jnp.where(key <= query, 0.0, -1e30)
 
 
-def attention_kernel(
-    tokens_ref, gain_ref, shift_ref, wq_ref, wk_ref, wv_ref, q_ref, k_ref, v_ref, o_ref, *refs, block
-):
-    *probs_refs, normed_ref, bias_ref = refs
+def attention_kernel(tokens_ref, gain_ref, shift_ref, *refs, block):
+    first_weights, next_weights, (q_ref, k_ref, v_ref, o_ref) = refs[:3], refs[3:6], refs[6:10]
+    *probs_refs, normed_ref, made_ref, bias_ref = refs[10:]
     causal_bias(bias_ref, 0)
-    parity = pl.program_id(1)
-
-    @pl.when((pl.program_id(0) == 0) & (parity == 0))
-    def _():
+    pair, parity = pl.program_id(0), pl.program_id(1)
+    length = made_ref.shape[0]
+
+    @pl.when((pair == 0) & (parity == 0))
+    def _():
+        weights = jnp.concatenate([weight[...] for weight in first_weights], axis=1)
         for index in range(len(probs_refs)):
             rows = slice(index * block, (index + 1) * block)
             normed, _, _ = normalize(tokens_ref[rows, :].astype(F32), gain_ref[...], shift_ref[...])
-            normed_ref[rows, :] = normed.astype(BF16)
+            normed = normed.astype(BF16)
+            normed_ref[rows, :] = normed
+            made_ref[rows, :] = contract(normed, weights, 1, 0).astype(BF16)
 
     @pl.when(parity == 0)
     def _():
-        weights = jnp.concatenate([wq_ref[...], wk_ref[...], wv_ref[...]], axis=1)
-        made = contract(normed_ref[...], weights, 1, 0).astype(BF16)
         for index, out in enumerate((q_ref, k_ref, v_ref)):
-            out[...] = made[:, index * LANES : (index + 1) * LANES]
-
+            out[...] = made_ref[:, index * LANES : (index + 1) * LANES]
+
+    weights = jnp.concatenate([weight[...] for weight in next_weights], axis=1)
+    part = length // 2 // len(probs_refs)
     queries = q_ref[...] * head_mask(parity, HEAD**-0.5)
     values = v_ref[...] * head_mask(parity, 1.0)
     outs = []
     for index, probs_ref in enumerate(probs_refs):
         first, finish = index * block, (index + 1) * block
         scores = contract(k_ref[:finish, :], queries[first:finish], 1, 1)
+        rows = pl.ds(pl.multiple_of(parity * (length // 2) + index * part, part), part)
+        made_ref[rows, :] = contract(normed_ref[rows, :], weights, 1, 0).astype(BF16)
         diagonal = scores[first:] + bias_ref[...]
         if index:
             scores = jnp.concatenate([scores[:first], diagonal], axis=0)
@@ -107,12 +112,16 @@
     block = min(256, length)
     finishes = range(block, length + 1, block)
     spec = pl.BlockSpec((length, LANES), lambda pair, parity: (0, pair))
-    weight = pl.BlockSpec((width, LANES), lambda pair, parity: (0, pair))
+    ahead = pl.BlockSpec(
+        (width, LANES), lambda pair, parity: (0, jnp.minimum(pair + 1, pairs - 1))
+    )
     wide = jax.ShapeDtypeStruct((length, width), BF16)
     queries, keys, values, mixed, *probs = pl.pallas_call(
         functools.partial(attention_kernel, block=block),
         grid=(pairs, 2),
-        in_specs=[const(length, width), const(1, width), const(1, width)] + [weight] * 3,
+        in_specs=[const(length, width), const(1, width), const(1, width)]
+        + [const(width, LANES)] * 3
+        + [ahead] * 3,
         out_specs=[spec] * 4
         + [
             pl.BlockSpec((1, finish, block), lambda pair, parity: (pair * 2 + parity, 0, 0))
@@ -120,10 +129,14 @@
         ],
         out_shape=[wide] * 4
         + [jax.ShapeDtypeStruct((2 * pairs, finish, block), BF16) for finish in finishes],
-        scratch_shapes=[pltpu.VMEM((length, width), BF16), pltpu.VMEM((block, block), F32)],
+        scratch_shapes=[
+            pltpu.VMEM((length, width), BF16),
+            pltpu.VMEM((length, 3 * LANES), BF16),
+            pltpu.VMEM((block, block), F32),
+        ],
         cost_estimate=LIGHT,
         name="attention",
-    )(tokens, gain, shift, *weights)
+    )(tokens, gain, shift, *weights, *weights)
     return queries, keys, values, mixed, probs
 
 
@@ -819,8 +832,8 @@
 
 
 class Sum:
-    def __init__(self, keep, send, stages, plus=add_low, split=True):
-        self.keep, self.send, self.plus = keep, send, plus
+    def __init__(self, keep, send, stages, plus=add_low, split=True, shared=True):
+        self.keep, self.send, self.plus, self.shared = keep, send, plus, shared
         if split:
             self.steps = [("whole", stages[0])]
             self.steps += [("halve", stage) for stage in stages[1:-1]]
@@ -836,6 +849,8 @@
             return [swap(self.keep, *each) for each in stage]
         if kind == "corner":
             near, far = self.got
+            if not self.shared:
+                return [swap(near, *stage[1])]
             half = near.shape[0] // 2
             return [swap(near[:half], *stage[1]), swap(far[half:], *stage[0])]
         return [swap(self.send, *stage)]
@@ -847,7 +862,8 @@
         elif kind == "corner":
             near, far = self.got
             mine = joined(self.keep, near, stage[0])
-            other = joined(far, jnp.concatenate(got, axis=0), stage[0])
+            corner = jnp.concatenate(got, axis=0) if self.shared else got[0]
+            other = joined(far, corner, stage[0])
             self.keep = joined(mine, other, stage[1])
         elif self.steps and self.steps[0][0] == "halve":
             self.send, self.keep = add_split(self.keep, got[0], self.steps[0][1])
@@ -958,7 +974,7 @@
     right, send, keep, produced = advance([early], right, send, keep, produced)
     produced = produced.reshape(slots, width)
     order = [("dp", 1)] + apart + cross[1:2] + cross[:1] + cross[2:]
-    late = Sum(keep.reshape(-1, LANES), send.reshape(-1, LANES), order)
+    late = Sum(keep.reshape(-1, LANES), send.reshape(-1, LANES), order, shared=False)
     layer_out = layer_output(wide, produced, resid, gate)
     layer_out, down_got = advance([early, late], layer_out, down_got)
     grad_tokens, first_sums = first_back(left, right, tokens, grad_resid, first_gain, weights)

time: 337 us -> 333 us (0.988)
    ppermute x31 -> x30, starting transfers between devices: 26.3 us -> 25.3 us  [swap(): return lax.ppermute(value, axis, [(i, i ^ bit) for i in range(size)])]
    unnamed x55 -> x50, local copies, waits for them, and re-layouts: 6.99 us -> 7.42 us
    ppermute x31 -> x30, waiting for transfers between devices: 34.4 us -> 34.7 us  [swap(): return lax.ppermute(value, axis, [(i, i ^ bit) for i in range(size)])]
  transfers between devices with their start and end apart: 35 -> 34, of which waited for: 16 -> 17; matrix products, arithmetic and copies ran while one was open for 4% -> 3% of each run, Pallas kernels for 50% -> 51%
where the time goes in v4:
time: 333 us; the launch traced here: 331 us
  Pallas kernels  209 us (63%)
  waiting for transfers between devices  55.8 us (17%)
  starting transfers between devices  46.2 us (14%)
  local copies, waits for them, and re-layouts  10.2 us (3%)
  other arithmetic  9.32 us (3%)
    pallas_call x2, Pallas kernels, attention_back(): pl.pallas_call(functools.partial(attention_back_kernel, block=block, bloc...  36.4 us
    ppermute x30, waiting for transfers between devices, swap(): return lax.ppermute(value, axis, [(i, i ^ bit) for i in range(size)])  34.7 us
    pallas_call x1, Pallas kernels, attention(): pl.pallas_call(functools.partial(attention_kernel, block=block), grid=(pa...  34 us
    pallas_call x1, Pallas kernels, expert(): pl.pallas_call(expert_kernel, grid=(hidden // tile,), in_specs=[whole, wh...  26.8 us
    ppermute x30, starting transfers between devices, swap(): return lax.ppermute(value, axis, [(i, i ^ bit) for i in range(size)])  25.3 us
    pallas_call x8, Pallas kernels, add_split(): pl.pallas_call(add_split_kernel, grid_spec=pltpu.PrefetchScalarGridSpec(n...  23 us
    all_to_all x4, waiting for transfers between devices, exchange(): lax.all_to_all(rows, 'expert', split_axis=0, concat_axis=0, tiled=True)  21.1 us
    all_to_all x4, starting transfers between devices, exchange(): lax.all_to_all(rows, 'expert', split_axis=0, concat_axis=0, tiled=True)  20.9 us
  transfers between devices with their start and end apart: 34, of which 17 were waited for; matrix products, arithmetic and copies ran while one was open for 3% of the time, Pallas kernels for 51%

profile of v4, /device:TPU:0, one launch (start us, length us, event | category | flops | bytes accessed | tf_op | source)
XLA Modules:
  0.0 331.4 jit_solution(17280214221899398200)
XLA Ops:
  0.6 5.4 %route.1 = (bf16[1024,768]{1,0:T(8,128)(2,1)}, s32[1,1024]{1,0:T(1,128)}, s32[1024,128]{1,0:T(8,128)}) custom-call(s32[1,1024]{1,0:T(1,128)} %bitcast.51, bf16[1024,768]{1,0:T(8,128)(2,1)} %cot_ref.3), custom_call_target="tpu_custom_call" | custom-call | flops 1000000 | bytes 100000 | tf_op jit(solution)/shard_map/route/pallas_call | solution.py:447
  6.1 7.5 %all-to-all-start = ((bf16[8,128,768]{2,1,0:T(8,128)(2,1)}), bf16[8,128,768]{2,1,0:T(8,128)(2,1)S(1)}, u32[]{:S(2)}, u32[]{:S(2)}) async-start(bf16[8,128,768]{2,1,0:T(8,128)(2,1)} %bitcast.43), calls=%async_computation | async-start | bytes 3145728 | tf_op jit(solution)/shard_map/all_to_all | solution.py:891
  14.3 34.0 %attention.1 = (bf16[1024,768]{1,0:T(8,128)(2,1)}, bf16[1024,768]{1,0:T(8,128)(2,1)}, bf16[1024,768]{1,0:T(8,128)(2,1)}, bf16[1024,768]{1,0:T(8,128)(2,1)}, bf16...) custom-call(bf16[1024,768]{1,0:T(8,128)(2,1)} %tokens_ref.3, ...), custom_call_target="tpu_custom_call" | custom-call | flops 1000000 | bytes 100000 | tf_op jit(solution)/shard_map/attention/pallas_call | solution.py:119
  48.3 8.9 %branch.1 = (f32[1024,768]{1,0:T(8,128)}, bf16[1024,768]{1,0:T(8,128)(2,1)}) custom-call(bf16[1024,768]{1,0:T(8,128)(2,1)} %get-tuple-element.145.mixed_ref.o_ref, bf16[1024,768]{1,0:T(8,128)(2,1)} %tokens_ref.3, bf16[768,768]{1,0:T(8,128)(2,1)} %weight_ref.3, f32[1,768]{1,0:T(1,128)} %get-tuple-element.287.gain_ref, f32[1,768]{1,0:T(1,128)} %get-tuple-element.286.bias_ref, ...), custom_call_target="tpu_custom_call" | custom-call | flops 1000000 | bytes 100000 | tf_op jit(solution)/shard_map/branch/pallas_call | solution.py:529
  58.3 6.0 %all-to-all-start.1 = ((bf16[8,128,768]{2,1,0:T(8,128)(2,1)}), bf16[8,128,768]{2,1,0:T(8,128)(2,1)S(1)}, u32[]{:S(2)}, u32[]{:S(2)}) async-start(bf16[8,128,768]{2,1,0:T(8,128)(2,1)} %bitcast.44), calls=%async_computation.1 | async-start | bytes 3145728 | tf_op jit(solution)/shard_map/all_to_all | solution.py:891
  65.3 7.8 %settle.1 = (bf16[768,1024]{1,0:T(8,128)(2,1)}, bf16[768,1024]{1,0:T(8,128)(2,1)}, bf16[1024,768]{1,0:T(8,128)(2,1)}, f32[1024,1]{1,0:T(8,128)}, f32[1024,1]{1,0:T(8,128)}) custom-call(bf16[1024,768]{1,0:T(8,128)(2,1)} %tokens_ref.3, f32[1,768]{1,0:T(1,128)} %get-tuple-element.289.gain_ref.first_gain_ref, ...), custom_call_target="tpu_custom_call" | custom-call | flops 1000000 | bytes 100000 | tf_op jit(solution)/shard_map/settle/pallas_call | solution.py:490
  74.4 9.9 %expert_cots.1.cd_ref = bf16[1024,3072]{1,0:T(8,128)(2,1)} custom-call(bf16[1024,768]{1,0:T(8,128)(2,1)} %bitcast.30, bf16[1,3072,768]{2,1,0:T(8,128)(2,1)} %down_ref.3), custom_call_target="tpu_custom_call" | custom-call | flops 1000000 | bytes 100000 | tf_op jit(solution)/shard_map/expert_cots/pallas_call | solution.py:255
  84.3 16.4 %all-to-all-done.1 = bf16[8,128,768]{2,1,0:T(8,128)(2,1)S(1)} async-done(((bf16[8,128,768]{2,1,0:T(8,128)(2,1)}), bf16[8,128,768]{2,1,0:T(8,128)(2,1)S(1)}, u32[]{:S(2)}, u32[]{:S(2)}) %all-to-all-start.1) | async-done | bytes 1572896 | tf_op jit(solution)/shard_map/all_to_all | solution.py:891
  101.9 26.8 %expert.1 = (bf16[1024,768]{1,0:T(8,128)(2,1)}, bf16[1024,768]{1,0:T(8,128)(2,1)}, bf16[1024,768]{1,0:T(8,128)(2,1)}, bf16[1024,3072]{1,0:T(8,128)(2,1)}, bf16[1024,3072]{1,0:T(8,128)(2,1)}) custom-call(bf16[1024,768]{1,0:T(8,128)(2,1)} %bitcast.32, bf16[1024,768]{1,0:T(8,128)(2,1)} %bitcast.31, bf16[1024,3072]{1,0:T(8,128)(2,1)} %expert_cots.1.cd_ref, ...), custom_call_target="tpu_custom_call" | custom-call | flops 1000000 | bytes 100000 | tf_op jit(solution)/shard_map/expert/pallas_call | solution.py:314
  128.6 3.6 %all-to-all-start.2 = ((bf16[8,128,768]{2,1,0:T(8,128)(2,1)}), bf16[8,128,768]{2,1,0:T(8,128)(2,1)S(1)}, u32[]{:S(2)}, u32[]{:S(2)}) async-start(bf16[8,128,768]{2,1,0:T(8,128)(2,1)} %bitcast.42), calls=%async_computation.2 | async-start | bytes 3145728 | tf_op jit(solution)/shard_map/all_to_all | solution.py:891
  132.3 18.8 %expert_weights.1 = (bf16[2,768,768]{2,1,0:T(8,128)(2,1)}, bf16[2,768,768]{2,1,0:T(8,128)(2,1)}, bf16[2,768,768]{2,1,0:T(8,128)(2,1)}, bf16[2,768,768]{2,1,0:T(8,128)(2,1)}) custom-call(s32[1]{0:T(128)} %bitcast.2.core_ref, bf16[1024,768]{1,0:T(8,128)(2,1)} %bitcast.33, bf16[1024,768]{1,0:T(8,128)(2,1)} %get-tuple-element.161.dy_ref, ...), custom_call_target="tpu_custom_call" | custom-call | flops 1000000 | bytes 100000 | tf_op jit(solution)/shard_map/expert_weights/pallas_call | solution.py:392
  151.6 4.4 %collective-permute-done = bf16[2,768,768]{2,1,0:T(8,128)(2,1)} collective-permute-done((bf16[2,768,768]{2,1,0:T(8,128)(2,1)}, bf16[2,768,768]{2,1,0:T(8,128)(2,1)}, u32[]{:S(2)}, u32[]{:S(2)}) %collective-permute-start) | collective-permute-done | bytes 2359328 | tf_op jit(solution)/shard_map/ppermute | solution.py:755
  156.0 4.4 %add_split.8 = (bf16[768,768]{1,0:T(8,128)(2,1)}, bf16[768,768]{1,0:T(8,128)(2,1)}) custom-call(s32[1]{0:T(128)} %bitcast.9.mine_ref, bf16[1536,768]{1,0:T(8,128)(2,1)} %bitcast.40, bf16[1536,768]{1,0:T(8,128)(2,1)} %bitcast.11.right_ref), custom_call_target="tpu_custom_call" | custom-call | flops 1000000 | bytes 100000 | tf_op jit(solution)/shard_map/add_split/pallas_call | solution.py:814
  160.4 4.4 %add_split.9 = (bf16[768,768]{1,0:T(8,128)(2,1)}, bf16[768,768]{1,0:T(8,128)(2,1)}) custom-call(s32[1]{0:T(128)} %bitcast.9.mine_ref, bf16[1536,768]{1,0:T(8,128)(2,1)} %bitcast.39, bf16[1536,768]{1,0:T(8,128)(2,1)} %bitcast.15.right_ref), custom_call_target="tpu_custom_call" | custom-call | flops 1000000 | bytes 100000 | tf_op jit(solution)/shard_map/add_split/pallas_call | solution.py:814
  164.8 4.7 %all-to-all-done.2 = bf16[8,128,768]{2,1,0:T(8,128)(2,1)S(1)} async-done(((bf16[8,128,768]{2,1,0:T(8,128)(2,1)}), bf16[8,128,768]{2,1,0:T(8,128)(2,1)S(1)}, u32[]{:S(2)}, u32[]{:S(2)}) %all-to-all-start.2) | async-done | bytes 1572896 | tf_op jit(solution)/shard_map/all_to_all | solution.py:891
  171.0 3.8 %all-to-all-start.3 = ((bf16[8,128,768]{2,1,0:T(8,128)(2,1)}), bf16[8,128,768]{2,1,0:T(8,128)(2,1)S(1)}, u32[]{:S(2)}, u32[]{:S(2)}) async-start(bf16[8,128,768]{2,1,0:T(8,128)(2,1)} %bitcast.41), calls=%async_computation.3 | async-start | bytes 3145728 | tf_op jit(solution)/shard_map/all_to_all | solution.py:891
  174.8 13.1 %second_back.1 = (bf16[1024,768]{1,0:T(8,128)(2,1)}, bf16[1024,768]{1,0:T(8,128)(2,1)}, f32[2,768]{1,0:T(2,128)}, bf16[15,384,128]{2,1,0:T(8,128)(2,1)}, bf16[15,384,128]{2,1,0:T(8,128)(2,1)}) custom-call(s32[1]{0:T(128)} %bitcast.2.core_ref, s32[1024,128]{1,0:T(8,128)} %get-tuple-element.144.wide_ref, bf16[1024,768]{1,0:T(8,128)(2,1)} %bitcast.35, ...), custom_call_target="tpu_custom_call" | custom-call | flops 1000000 | bytes 100000 | tf_op jit(solution)/shard_map/second_back/pallas_call | solution.py:609
  187.9 18.2 %attention_back.2 = (bf16[3,1024,384]{2,1,0:T(8,128)(2,1)}, bf16[15,384,128]{2,1,0:T(8,128)(2,1)}, bf16[15,384,128]{2,1,0:T(8,128)(2,1)}) custom-call(s32[1]{0:T(128)} %bitcast.2.core_ref, bf16[1024,768]{1,0:T(8,128)(2,1)} %get-tuple-element.141.q_ref, bf16[1024,768]{1,0:T(8,128)(2,1)} %get-tuple-element.142.k_ref, ...), custom_call_target="tpu_custom_call", output_to_operand_aliasing={{1}: (11, {}), {2}: (12, {})} | custom-call | flops 1000000 | bytes 100000 | tf_op jit(solution)/shard_map/attention_back/pallas_call | solution.py:221
  217.0 18.2 %attention_back.3 = (bf16[3,1024,384]{2,1,0:T(8,128)(2,1)}, bf16[9,384,128]{2,1,0:T(8,128)(2,1)}, bf16[9,384,128]{2,1,0:T(8,128)(2,1)}) custom-call(s32[1]{0:T(128)} %bitcast.2.core_ref, bf16[1024,768]{1,0:T(8,128)(2,1)} %get-tuple-element.141.q_ref, bf16[1024,768]{1,0:T(8,128)(2,1)} %get-tuple-element.142.k_ref, ...), custom_call_target="tpu_custom_call" | custom-call | flops 1000000 | bytes 100000 | tf_op jit(solution)/shard_map/attention_back/pallas_call | solution.py:221
  240.0 6.0 %layer_output.1 = bf16[1024,768]{1,0:T(8,128)(2,1)} custom-call(s32[1024,128]{1,0:T(8,128)} %get-tuple-element.144.wide_ref, bf16[1024,768]{1,0:T(8,128)(2,1)} %bitcast.34, f32[1024,768]{1,0:T(8,128)} %get-tuple-element.151.resid_ref, f32[1024,1]{1,0:T(8,128)} %get-tuple-element.205.gate_ref), custom_call_target="tpu_custom_call" | custom-call | flops 1000000 | bytes 100000 | tf_op jit(solution)/shard_map/layer_output/pallas_call | solution.py:691
  256.9 10.7 %first_back.1 = (f32[1024,768]{1,0:T(8,128)}, f32[2,768]{1,0:T(2,128)}) custom-call(bf16[3,1024,384]{2,1,0:T(8,128)(2,1)} %get-tuple-element.214.left_ref, bf16[3,1024,384]{2,1,0:T(8,128)(2,1)} %get-tuple-element.215.right_ref, bf16[1024,768]{1,0:T(8,128)(2,1)} %tokens_ref.3, bf16[1024,768]{1,0:T(8,128)(2,1)} %get-tuple-element.216.resid_ref, ...), custom_call_target="tpu_custom_call" | custom-call | flops 1000000 | bytes 100000 | tf_op jit(solution)/shard_map/first_back/pallas_call | solution.py:666
  292.0 4.7 %collective-permute-done.19 = f32[4,768]{1,0:T(4,128)S(1)} collective-permute-done((f32[4,768]{1,0:T(4,128)S(1)}, f32[4,768]{1,0:T(4,128)S(1)}, u32[]{:S(2)}, u32[]{:S(2)}) %collective-permute-start.19) | collective-permute-done | bytes 12320 | tf_op jit(solution)/shard_map/ppermute | solution.py:755
  310.0 3.9 %collective-permute-done.26 = f32[4,768]{1,0:T(4,128)S(1)} collective-permute-done((f32[4,768]{1,0:T(4,128)S(1)}, f32[4,768]{1,0:T(4,128)S(1)}, u32[]{:S(2)}, u32[]{:S(2)}) %collective-permute-start.26) | collective-permute-done | bytes 12320 | tf_op jit(solution)/shard_map/ppermute | solution.py:755
  317.3 4.6 %assemble.2 = (f32[768,768]{1,0:T(8,128)}, f32[768,768]{1,0:T(8,128)}, f32[768,768]{1,0:T(8,128)}, f32[768,768]{1,0:T(8,128)}) custom-call(s32[1]{0:T(128)} %bitcast.2.core_ref, bf16[15,384,128]{2,1,0:T(8,128)(2,1)} %bitcast.36, bf16[15,384,128]{2,1,0:T(8,128)(2,1)} %bitcast.45), custom_call_target="tpu_custom_call" | custom-call | flops 1000000 | bytes 100000 | tf_op jit(solution)/shard_map/assemble/pallas_call | solution.py:737
  (151 shorter events, 84.2 us)
Async XLA Ops:
  6.1 51.0 %all-to-all-start = ((bf16[8,128,768]{2,1,0:T(8,128)(2,1)}), bf16[8,128,768]{2,1,0:T(8,128)(2,1)S(1)}, u32[]{:S(2)}, u32[]{:S(2)}) async-start(bf16[8,128,768]{2,1,0:T(8,128)(2,1)} %bitcast.43), calls=%async_computation | async-start | bytes 3145728 | tf_op jit(solution)/shard_map/all_to_all | solution.py:891
  58.3 42.4 %all-to-all-start.1 = ((bf16[8,128,768]{2,1,0:T(8,128)(2,1)}), bf16[8,128,768]{2,1,0:T(8,128)(2,1)S(1)}, u32[]{:S(2)}, u32[]{:S(2)}) async-start(bf16[8,128,768]{2,1,0:T(8,128)(2,1)} %bitcast.44), calls=%async_computation.1 | async-start | bytes 3145728 | tf_op jit(solution)/shard_map/all_to_all | solution.py:891
  128.6 40.8 %all-to-all-start.2 = ((bf16[8,128,768]{2,1,0:T(8,128)(2,1)}), bf16[8,128,768]{2,1,0:T(8,128)(2,1)S(1)}, u32[]{:S(2)}, u32[]{:S(2)}) async-start(bf16[8,128,768]{2,1,0:T(8,128)(2,1)} %bitcast.42), calls=%async_computation.2 | async-start | bytes 3145728 | tf_op jit(solution)/shard_map/all_to_all | solution.py:891
  151.1 9.3 %collective-permute-start.1 = (bf16[2,768,768]{2,1,0:T(8,128)(2,1)}, bf16[2,768,768]{2,1,0:T(8,128)(2,1)}, u32[]{:S(2)}, u32[]{:S(2)}) collective-permute-start(bf16[2,768,768]{2,1,0:T(8,128)(2,1)} %get-tuple-element.169), channel_id=1, source_target_pairs={{0,8},{8,0},{16,24},{24,16},{1,9},{9,1},{17,25},{25,17},{2,10},{10... | collective-permute-start | bytes 7077896 | tf_op jit(solution)/shard_map/ppermute | solution.py:755
  169.5 36.6 %collective-permute-start.2 = (bf16[1,768,768]{2,1,0:T(8,128)(2,1)}, bf16[1,768,768]{2,1,0:T(8,128)(2,1)}, u32[]{:S(2)}, u32[]{:S(2)}) collective-permute-start(bf16[1,768,768]{2,1,0:T(8,128)(2,1)} %bitcast.12), channel_id=1, source_target_pairs={{0,16},{8,24},{16,0},{24,8},{1,17},{9,25},{17,1},{25,9},{2,18},{10... | collective-permute-start | bytes 3538952 | tf_op jit(solution)/shard_map/ppermute | solution.py:755
  171.0 64.3 %all-to-all-start.3 = ((bf16[8,128,768]{2,1,0:T(8,128)(2,1)}), bf16[8,128,768]{2,1,0:T(8,128)(2,1)S(1)}, u32[]{:S(2)}, u32[]{:S(2)}) async-start(bf16[8,128,768]{2,1,0:T(8,128)(2,1)} %bitcast.41), calls=%async_computation.3 | async-start | bytes 3145728 | tf_op jit(solution)/shard_map/all_to_all | solution.py:891
  214.0 21.2 %collective-permute-start.4 = (bf16[2880,128]{1,0:T(8,128)(2,1)}, bf16[2880,128]{1,0:T(8,128)(2,1)S(1)}, u32[]{:S(2)}, u32[]{:S(2)}) collective-permute-start(bf16[2880,128]{1,0:T(8,128)(2,1)} %get-tuple-element.192), channel_id=1, source_target_pairs={{0,1},{1,0},{2,3},{3,2},{4,5},{5,4},{6,7},{7,6},{8,9},{9,8},{10,11... | collective-permute-start | bytes 2211848 | tf_op jit(solution)/shard_map/ppermute | solution.py:755
  215.9 30.1 %collective-permute-start.7 = (bf16[1,768,768]{2,1,0:T(8,128)(2,1)}, bf16[1,768,768]{2,1,0:T(8,128)(2,1)S(1)}, u32[]{:S(2)}, u32[]{:S(2)}) collective-permute-start(bf16[1,768,768]{2,1,0:T(8,128)(2,1)} %bitcast.52), channel_id=1, source_target_pairs={{0,16},{8,24},{16,0},{24,8},{1,17},{9,25},{17,1},{25,9},{2,18},{10... | collective-permute-start | bytes 3538952 | tf_op jit(solution)/shard_map/ppermute | solution.py:755
  235.3 13.6 %collective-permute-start.6 = (bf16[3456,128]{1,0:T(8,128)(2,1)}, bf16[3456,128]{1,0:T(8,128)(2,1)}, u32[]{:S(2)}, u32[]{:S(2)}) collective-permute-start(bf16[3456,128]{1,0:T(8,128)(2,1)} %bitcast.53), channel_id=1, source_target_pairs={{0,8},{8,0},{16,24},{24,16},{1,9},{9,1},{17,25},{25,17},{2,10},{10... | collective-permute-start | bytes 2654216 | tf_op jit(solution)/shard_map/ppermute | solution.py:755
  238.5 10.4 %collective-permute-start.5 = (bf16[1440,128]{1,0:T(8,128)(2,1)}, bf16[1440,128]{1,0:T(8,128)(2,1)S(1)}, u32[]{:S(2)}, u32[]{:S(2)}) collective-permute-start(bf16[1440,128]{1,0:T(8,128)(2,1)} %get-tuple-element.202), channel_id=1, source_target_pairs={{0,2},{1,3},{2,0},{3,1},{4,6},{5,7},{6,4},{7,5},{8,10},{9,11},{10,... | collective-permute-start | bytes 1105928 | tf_op jit(solution)/shard_map/ppermute | solution.py:755
  251.6 16.0 %collective-permute-start.9 = (bf16[1728,128]{1,0:T(8,128)(2,1)}, bf16[1728,128]{1,0:T(8,128)(2,1)S(1)}, u32[]{:S(2)}, u32[]{:S(2)}) collective-permute-start(bf16[1728,128]{1,0:T(8,128)(2,1)} %get-tuple-element.213), channel_id=1, source_target_pairs={{0,16},{8,24},{16,0},{24,8},{1,17},{9,25},{17,1},{25,9},{2,18},{10... | collective-permute-start | bytes 1327112 | tf_op jit(solution)/shard_map/ppermute | solution.py:755
  254.5 13.1 %collective-permute-start.8 = (bf16[720,128]{1,0:T(8,128)(2,1)}, bf16[720,128]{1,0:T(8,128)(2,1)S(1)}, u32[]{:S(2)}, u32[]{:S(2)}) collective-permute-start(bf16[720,128]{1,0:T(8,128)(2,1)} %get-tuple-element.210), channel_id=1, source_target_pairs={{0,4},{1,5},{2,6},{3,7},{4,0},{5,1},{6,2},{7,3},{8,12},{9,13},{10,... | collective-permute-start | bytes 552968 | tf_op jit(solution)/shard_map/ppermute | solution.py:755
  270.5 7.1 %collective-permute-start.11 = (bf16[864,128]{1,0:T(8,128)(2,1)}, bf16[864,128]{1,0:T(8,128)(2,1)S(1)}, u32[]{:S(2)}, u32[]{:S(2)}) collective-permute-start(bf16[864,128]{1,0:T(8,128)(2,1)} %get-tuple-element.225), channel_id=1, source_target_pairs={{0,2},{1,3},{2,0},{3,1},{4,6},{5,7},{6,4},{7,5},{8,10},{9,11},{10,... | collective-permute-start | bytes 663560 | tf_op jit(solution)/shard_map/ppermute | solution.py:755
  277.7 9.2 %collective-permute-start.13 = (bf16[720,128]{1,0:T(8,128)(2,1)S(1)}, bf16[720,128]{1,0:T(8,128)(2,1)S(1)}, u32[]{:S(2)}, u32[]{:S(2)}) collective-permute-start(bf16[720,128]{1,0:T(8,128)(2,1)S(1)} %add_convert_fusion), channel_id=1, source_target_pairs={{0,4},{1,5},{2,6},{3,7},{4,0},{5,1},{6,2},{7,3},{8,12},{9,13},{10,... | collective-permute-start | bytes 552968 | tf_op jit(solution)/shard_map/ppermute | solution.py:755
  286.9 11.8 %collective-permute-start.16 = (bf16[1440,128]{1,0:T(8,128)(2,1)S(1)}, bf16[1440,128]{1,0:T(8,128)(2,1)S(1)}, u32[]{:S(2)}, u32[]{:S(2)}) collective-permute-start(bf16[1440,128]{1,0:T(8,128)(2,1)S(1)} %pad_maximum_fusion.6), channel_id=1, source_target_pairs={{0,2},{1,3},{2,0},{3,1},{4,6},{5,7},{6,4},{7,5},{8,10},{9,11},{10,... | collective-permute-start | bytes 1105928 | tf_op jit(solution)/shard_map/ppermute | solution.py:755
  287.0 11.7 %collective-permute-start.17 = (bf16[1440,128]{1,0:T(8,128)(2,1)S(1)}, bf16[1440,128]{1,0:T(8,128)(2,1)S(1)}, u32[]{:S(2)}, u32[]{:S(2)}) collective-permute-start(bf16[1440,128]{1,0:T(8,128)(2,1)S(1)} %pad_maximum_fusion.6), channel_id=1, source_target_pairs={{0,1},{1,0},{2,3},{3,2},{4,5},{5,4},{6,7},{7,6},{8,9},{9,8},{10,11... | collective-permute-start | bytes 1105928 | tf_op jit(solution)/shard_map/ppermute | solution.py:755
  287.7 9.0 %collective-permute-start.18 = (bf16[432,128]{1,0:T(8,128)(2,1)S(1)}, bf16[432,128]{1,0:T(8,128)(2,1)S(1)}, u32[]{:S(2)}, u32[]{:S(2)}) collective-permute-start(bf16[432,128]{1,0:T(8,128)(2,1)S(1)} %add_convert_fusion.3), channel_id=1, source_target_pairs={{0,4},{1,5},{2,6},{3,7},{4,0},{5,1},{6,2},{7,3},{8,12},{9,13},{10,... | collective-permute-start | bytes 331784 | tf_op jit(solution)/shard_map/ppermute | solution.py:755
  289.4 7.2 %collective-permute-start.19 = (f32[4,768]{1,0:T(4,128)S(1)}, f32[4,768]{1,0:T(4,128)S(1)}, u32[]{:S(2)}, u32[]{:S(2)}) collective-permute-start(f32[4,768]{1,0:T(4,128)S(1)} %add.78), channel_id=1, source_target_pairs={{0,1},{1,0},{2,3},{3,2},{4,5},{5,4},{6,7},{7,6},{8,9},{9,8},{10,11... | collective-permute-start | bytes 36872 | tf_op jit(solution)/shard_map/ppermute | solution.py:755
  298.8 7.7 %collective-permute-start.20 = (bf16[720,128]{1,0:T(8,128)(2,1)S(1)}, bf16[720,128]{1,0:T(8,128)(2,1)S(1)}, u32[]{:S(2)}, u32[]{:S(2)}) collective-permute-start(bf16[720,128]{1,0:T(8,128)(2,1)S(1)} %slice.34), channel_id=1, source_target_pairs={{0,1},{1,0},{2,3},{3,2},{4,5},{5,4},{6,7},{7,6},{8,9},{9,8},{10,11... | collective-permute-start | bytes 552968 | tf_op jit(solution)/shard_map/ppermute | solution.py:755
  299.4 7.0 %collective-permute-start.21 = (bf16[720,128]{1,0:T(8,128)(2,1)S(1)}, bf16[720,128]{1,0:T(8,128)(2,1)S(1)}, u32[]{:S(2)}, u32[]{:S(2)}) collective-permute-start(bf16[720,128]{1,0:T(8,128)(2,1)S(1)} %slice.35), channel_id=1, source_target_pairs={{0,2},{1,3},{2,0},{3,1},{4,6},{5,7},{6,4},{7,5},{8,10},{9,11},{10,... | collective-permute-start | bytes 552968 | tf_op jit(solution)/shard_map/ppermute | solution.py:755
  306.9 9.2 %collective-permute-start.27 = (bf16[5760,128]{1,0:T(8,128)(2,1)S(1)}, bf16[5760,128]{1,0:T(8,128)(2,1)S(1)}, u32[]{:S(2)}, u32[]{:S(2)}) collective-permute-start(bf16[5760,128]{1,0:T(8,128)(2,1)S(1)} %pad_maximum_fusion), channel_id=1, source_target_pairs={{0,8},{8,0},{16,24},{24,16},{1,9},{9,1},{17,25},{25,17},{2,10},{10... | collective-permute-start | bytes 4423688 | tf_op jit(solution)/shard_map/ppermute | solution.py:755
  307.9 8.3 %collective-permute-start.24 = (bf16[864,128]{1,0:T(8,128)(2,1)}, bf16[864,128]{1,0:T(8,128)(2,1)}, u32[]{:S(2)}, u32[]{:S(2)}) collective-permute-start(bf16[864,128]{1,0:T(8,128)(2,1)} %pad_maximum_fusion.7), channel_id=1, source_target_pairs={{0,2},{1,3},{2,0},{3,1},{4,6},{5,7},{6,4},{7,5},{8,10},{9,11},{10,... | collective-permute-start | bytes 663560 | tf_op jit(solution)/shard_map/ppermute | solution.py:755
  308.2 8.0 %collective-permute-start.25 = (bf16[864,128]{1,0:T(8,128)(2,1)}, bf16[864,128]{1,0:T(8,128)(2,1)S(1)}, u32[]{:S(2)}, u32[]{:S(2)}) collective-permute-start(bf16[864,128]{1,0:T(8,128)(2,1)} %pad_maximum_fusion.7), channel_id=1, source_target_pairs={{0,16},{8,24},{16,0},{24,8},{1,17},{9,25},{17,1},{25,9},{2,18},{10... | collective-permute-start | bytes 663560 | tf_op jit(solution)/shard_map/ppermute | solution.py:755
  316.2 7.2 %collective-permute-start.28 = (bf16[864,128]{1,0:T(8,128)(2,1)}, bf16[864,128]{1,0:T(8,128)(2,1)}, u32[]{:S(2)}, u32[]{:S(2)}) collective-permute-start(bf16[864,128]{1,0:T(8,128)(2,1)} %collective-permute-done.24), channel_id=1, source_target_pairs={{0,16},{8,24},{16,0},{24,8},{1,17},{9,25},{17,1},{25,9},{2,18},{10... | collective-permute-start | bytes 663560 | tf_op jit(solution)/shard_map/ppermute | solution.py:755
  (34 other events, 180.5 us)

commit v5 on v4

--- a/solution.py
+++ b/solution.py
@@ -78,7 +78,7 @@
     weights = jnp.concatenate([weight[...] for weight in next_weights], axis=1)
     part = length // 2 // len(probs_refs)
     queries = q_ref[...] * head_mask(parity, HEAD**-0.5)
-    values = v_ref[...] * head_mask(parity, 1.0)
+    values = jnp.transpose(v_ref[...] * head_mask(parity, 1.0))
     outs = []
     for index, probs_ref in enumerate(probs_refs):
         first, finish = index * block, (index + 1) * block
@@ -94,7 +94,7 @@
         total = jnp.sum(shifted, axis=0, keepdims=True)
         probs = (shifted * (1.0 / total)).astype(BF16)
         probs_ref[0] = probs
-        outs.append(contract(probs, values[:finish], 0, 0).astype(BF16))
+        outs.append(jnp.transpose(contract(values[:, :finish], probs, 1, 0).astype(BF16)))
     mixed = jnp.concatenate(outs, axis=0)
 
     @pl.when(parity == 0)
@@ -149,7 +149,7 @@
     scale_mask = head_mask(parity, HEAD**-0.5)
     queries = q_ref[...] * scale_mask
     grads = g_ref[...] * head_mask(parity, 1.0)
-    keys_scaled = k_ref[...] * scale_mask
+    keys_scaled = jnp.transpose(k_ref[...] * scale_mask)
     dk_sum[...] = jnp.zeros_like(dk_sum)
     dv_sum[...] = jnp.zeros_like(dv_sum)
     dq_parts = []
@@ -163,7 +163,8 @@
         delta = jnp.sum(jnp.transpose(shares), axis=0, keepdims=True)
         grad_scores = (probs.astype(F32) * (grad_probs - delta)).astype(BF16)
         dk_sum[:finish, :] += contract(grad_scores, queries[first:finish], 1, 0)
-        dq_parts.append(contract(grad_scores, keys_scaled[:finish], 0, 0).astype(BF16))
+        part = contract(keys_scaled[:, :finish], grad_scores, 1, 0).astype(BF16)
+        dq_parts.append(jnp.transpose(part))
     parts = (
         jnp.concatenate(dq_parts, axis=0),
         dk_sum[...].astype(BF16),

time: 333 us -> 327 us (0.982)
  Pallas kernels: 209 us -> 203 us
    pallas_call x1, Pallas kernels: 34 us -> 30.1 us  [attention(): pl.pallas_call(functools.partial(attention_kernel, block=block), grid=(pa...]
  transfers between devices with their start and end apart: 34 -> 34, of which waited for: 17 -> 17; matrix products, arithmetic and copies ran while one was open for 3% -> 3% of each run, Pallas kernels for 51% -> 50%
where the time goes in v5:
time: 327 us; the launch traced here: 326 us
  Pallas kernels  203 us (62%)
  waiting for transfers between devices  55.7 us (17%)
  starting transfers between devices  46.2 us (14%)
  local copies, waits for them, and re-layouts  10.2 us (3%)
  other arithmetic  9.32 us (3%)
    pallas_call x2, Pallas kernels, attention_back(): pl.pallas_call(functools.partial(attention_back_kernel, block=block, bloc...  34.8 us
    ppermute x30, waiting for transfers between devices, swap(): return lax.ppermute(value, axis, [(i, i ^ bit) for i in range(size)])  34.7 us
    pallas_call x1, Pallas kernels, attention(): pl.pallas_call(functools.partial(attention_kernel, block=block), grid=(pa...  30.1 us
    pallas_call x1, Pallas kernels, expert(): pl.pallas_call(expert_kernel, grid=(hidden // tile,), in_specs=[whole, wh...  26.8 us
    ppermute x30, starting transfers between devices, swap(): return lax.ppermute(value, axis, [(i, i ^ bit) for i in range(size)])  25.3 us
    pallas_call x8, Pallas kernels, add_split(): pl.pallas_call(add_split_kernel, grid_spec=pltpu.PrefetchScalarGridSpec(n...  23 us
    all_to_all x4, waiting for transfers between devices, exchange(): lax.all_to_all(rows, 'expert', split_axis=0, concat_axis=0, tiled=True)  21.1 us
    all_to_all x4, starting transfers between devices, exchange(): lax.all_to_all(rows, 'expert', split_axis=0, concat_axis=0, tiled=True)  20.9 us
  transfers between devices with their start and end apart: 34, of which 17 were waited for; matrix products, arithmetic and copies ran while one was open for 3% of the time, Pallas kernels for 50%

profile of v5, /device:TPU:0, one launch (start us, length us, event | category | flops | bytes accessed | tf_op | source)
XLA Modules:
  0.0 325.8 jit_solution(3013029217612115335)
XLA Ops:
  0.6 5.4 %route.1 = (bf16[1024,768]{1,0:T(8,128)(2,1)}, s32[1,1024]{1,0:T(1,128)}, s32[1024,128]{1,0:T(8,128)}) custom-call(s32[1,1024]{1,0:T(1,128)} %bitcast.51, bf16[1024,768]{1,0:T(8,128)(2,1)} %cot_ref.3), custom_call_target="tpu_custom_call" | custom-call | flops 1000000 | bytes 100000 | tf_op jit(solution)/shard_map/route/pallas_call | solution.py:448
  6.1 7.5 %all-to-all-start = ((bf16[8,128,768]{2,1,0:T(8,128)(2,1)}), bf16[8,128,768]{2,1,0:T(8,128)(2,1)S(1)}, u32[]{:S(2)}, u32[]{:S(2)}) async-start(bf16[8,128,768]{2,1,0:T(8,128)(2,1)} %bitcast.43), calls=%async_computation | async-start | bytes 3145728 | tf_op jit(solution)/shard_map/all_to_all | solution.py:892
  14.3 30.1 %attention.1 = (bf16[1024,768]{1,0:T(8,128)(2,1)}, bf16[1024,768]{1,0:T(8,128)(2,1)}, bf16[1024,768]{1,0:T(8,128)(2,1)}, bf16[1024,768]{1,0:T(8,128)(2,1)}, bf16...) custom-call(bf16[1024,768]{1,0:T(8,128)(2,1)} %tokens_ref.3, ...), custom_call_target="tpu_custom_call" | custom-call | flops 1000000 | bytes 100000 | tf_op jit(solution)/shard_map/attention/pallas_call | solution.py:119
  44.4 8.9 %branch.1 = (f32[1024,768]{1,0:T(8,128)}, bf16[1024,768]{1,0:T(8,128)(2,1)}) custom-call(bf16[1024,768]{1,0:T(8,128)(2,1)} %get-tuple-element.145.mixed_ref.o_ref, bf16[1024,768]{1,0:T(8,128)(2,1)} %tokens_ref.3, bf16[768,768]{1,0:T(8,128)(2,1)} %weight_ref.3, f32[1,768]{1,0:T(1,128)} %get-tuple-element.287.gain_ref, f32[1,768]{1,0:T(1,128)} %get-tuple-element.286.bias_ref, ...), custom_call_target="tpu_custom_call" | custom-call | flops 1000000 | bytes 100000 | tf_op jit(solution)/shard_map/branch/pallas_call | solution.py:530
  54.4 6.0 %all-to-all-start.1 = ((bf16[8,128,768]{2,1,0:T(8,128)(2,1)}), bf16[8,128,768]{2,1,0:T(8,128)(2,1)S(1)}, u32[]{:S(2)}, u32[]{:S(2)}) async-start(bf16[8,128,768]{2,1,0:T(8,128)(2,1)} %bitcast.44), calls=%async_computation.1 | async-start | bytes 3145728 | tf_op jit(solution)/shard_map/all_to_all | solution.py:892
  61.4 7.8 %settle.1 = (bf16[768,1024]{1,0:T(8,128)(2,1)}, bf16[768,1024]{1,0:T(8,128)(2,1)}, bf16[1024,768]{1,0:T(8,128)(2,1)}, f32[1024,1]{1,0:T(8,128)}, f32[1024,1]{1,0:T(8,128)}) custom-call(bf16[1024,768]{1,0:T(8,128)(2,1)} %tokens_ref.3, f32[1,768]{1,0:T(1,128)} %get-tuple-element.289.gain_ref.first_gain_ref, ...), custom_call_target="tpu_custom_call" | custom-call | flops 1000000 | bytes 100000 | tf_op jit(solution)/shard_map/settle/pallas_call | solution.py:491
  70.5 9.9 %expert_cots.1.cd_ref = bf16[1024,3072]{1,0:T(8,128)(2,1)} custom-call(bf16[1024,768]{1,0:T(8,128)(2,1)} %bitcast.30, bf16[1,3072,768]{2,1,0:T(8,128)(2,1)} %down_ref.3), custom_call_target="tpu_custom_call" | custom-call | flops 1000000 | bytes 100000 | tf_op jit(solution)/shard_map/expert_cots/pallas_call | solution.py:256
  80.4 16.4 %all-to-all-done.1 = bf16[8,128,768]{2,1,0:T(8,128)(2,1)S(1)} async-done(((bf16[8,128,768]{2,1,0:T(8,128)(2,1)}), bf16[8,128,768]{2,1,0:T(8,128)(2,1)S(1)}, u32[]{:S(2)}, u32[]{:S(2)}) %all-to-all-start.1) | async-done | bytes 1572896 | tf_op jit(solution)/shard_map/all_to_all | solution.py:892
  98.0 26.8 %expert.1 = (bf16[1024,768]{1,0:T(8,128)(2,1)}, bf16[1024,768]{1,0:T(8,128)(2,1)}, bf16[1024,768]{1,0:T(8,128)(2,1)}, bf16[1024,3072]{1,0:T(8,128)(2,1)}, bf16[1024,3072]{1,0:T(8,128)(2,1)}) custom-call(bf16[1024,768]{1,0:T(8,128)(2,1)} %bitcast.32, bf16[1024,768]{1,0:T(8,128)(2,1)} %bitcast.31, bf16[1024,3072]{1,0:T(8,128)(2,1)} %expert_cots.1.cd_ref, ...), custom_call_target="tpu_custom_call" | custom-call | flops 1000000 | bytes 100000 | tf_op jit(solution)/shard_map/expert/pallas_call | solution.py:315
  124.8 3.6 %all-to-all-start.2 = ((bf16[8,128,768]{2,1,0:T(8,128)(2,1)}), bf16[8,128,768]{2,1,0:T(8,128)(2,1)S(1)}, u32[]{:S(2)}, u32[]{:S(2)}) async-start(bf16[8,128,768]{2,1,0:T(8,128)(2,1)} %bitcast.42), calls=%async_computation.2 | async-start | bytes 3145728 | tf_op jit(solution)/shard_map/all_to_all | solution.py:892
  128.4 18.8 %expert_weights.1 = (bf16[2,768,768]{2,1,0:T(8,128)(2,1)}, bf16[2,768,768]{2,1,0:T(8,128)(2,1)}, bf16[2,768,768]{2,1,0:T(8,128)(2,1)}, bf16[2,768,768]{2,1,0:T(8,128)(2,1)}) custom-call(s32[1]{0:T(128)} %bitcast.2.core_ref, bf16[1024,768]{1,0:T(8,128)(2,1)} %bitcast.33, bf16[1024,768]{1,0:T(8,128)(2,1)} %get-tuple-element.161.dy_ref, ...), custom_call_target="tpu_custom_call" | custom-call | flops 1000000 | bytes 100000 | tf_op jit(solution)/shard_map/expert_weights/pallas_call | solution.py:393
  147.7 4.4 %collective-permute-done = bf16[2,768,768]{2,1,0:T(8,128)(2,1)} collective-permute-done((bf16[2,768,768]{2,1,0:T(8,128)(2,1)}, bf16[2,768,768]{2,1,0:T(8,128)(2,1)}, u32[]{:S(2)}, u32[]{:S(2)}) %collective-permute-start) | collective-permute-done | bytes 2359328 | tf_op jit(solution)/shard_map/ppermute | solution.py:756
  152.1 4.4 %add_split.8 = (bf16[768,768]{1,0:T(8,128)(2,1)}, bf16[768,768]{1,0:T(8,128)(2,1)}) custom-call(s32[1]{0:T(128)} %bitcast.9.mine_ref, bf16[1536,768]{1,0:T(8,128)(2,1)} %bitcast.40, bf16[1536,768]{1,0:T(8,128)(2,1)} %bitcast.11.right_ref), custom_call_target="tpu_custom_call" | custom-call | flops 1000000 | bytes 100000 | tf_op jit(solution)/shard_map/add_split/pallas_call | solution.py:815
  156.5 4.4 %add_split.9 = (bf16[768,768]{1,0:T(8,128)(2,1)}, bf16[768,768]{1,0:T(8,128)(2,1)}) custom-call(s32[1]{0:T(128)} %bitcast.9.mine_ref, bf16[1536,768]{1,0:T(8,128)(2,1)} %bitcast.39, bf16[1536,768]{1,0:T(8,128)(2,1)} %bitcast.15.right_ref), custom_call_target="tpu_custom_call" | custom-call | flops 1000000 | bytes 100000 | tf_op jit(solution)/shard_map/add_split/pallas_call | solution.py:815
  160.9 4.7 %all-to-all-done.2 = bf16[8,128,768]{2,1,0:T(8,128)(2,1)S(1)} async-done(((bf16[8,128,768]{2,1,0:T(8,128)(2,1)}), bf16[8,128,768]{2,1,0:T(8,128)(2,1)S(1)}, u32[]{:S(2)}, u32[]{:S(2)}) %all-to-all-start.2) | async-done | bytes 1572896 | tf_op jit(solution)/shard_map/all_to_all | solution.py:892
  167.1 3.8 %all-to-all-start.3 = ((bf16[8,128,768]{2,1,0:T(8,128)(2,1)}), bf16[8,128,768]{2,1,0:T(8,128)(2,1)S(1)}, u32[]{:S(2)}, u32[]{:S(2)}) async-start(bf16[8,128,768]{2,1,0:T(8,128)(2,1)} %bitcast.41), calls=%async_computation.3 | async-start | bytes 3145728 | tf_op jit(solution)/shard_map/all_to_all | solution.py:892
  170.9 13.1 %second_back.1 = (bf16[1024,768]{1,0:T(8,128)(2,1)}, bf16[1024,768]{1,0:T(8,128)(2,1)}, f32[2,768]{1,0:T(2,128)}, bf16[15,384,128]{2,1,0:T(8,128)(2,1)}, bf16[15,384,128]{2,1,0:T(8,128)(2,1)}) custom-call(s32[1]{0:T(128)} %bitcast.2.core_ref, s32[1024,128]{1,0:T(8,128)} %get-tuple-element.144.wide_ref, bf16[1024,768]{1,0:T(8,128)(2,1)} %bitcast.35, ...), custom_call_target="tpu_custom_call" | custom-call | flops 1000000 | bytes 100000 | tf_op jit(solution)/shard_map/second_back/pallas_call | solution.py:610
  184.0 17.4 %attention_back.2 = (bf16[3,1024,384]{2,1,0:T(8,128)(2,1)}, bf16[15,384,128]{2,1,0:T(8,128)(2,1)}, bf16[15,384,128]{2,1,0:T(8,128)(2,1)}) custom-call(s32[1]{0:T(128)} %bitcast.2.core_ref, bf16[1024,768]{1,0:T(8,128)(2,1)} %get-tuple-element.141.q_ref, bf16[1024,768]{1,0:T(8,128)(2,1)} %get-tuple-element.142.k_ref, ...), custom_call_target="tpu_custom_call", output_to_operand_aliasing={{1}: (11, {}), {2}: (12, {})} | custom-call | flops 1000000 | bytes 100000 | tf_op jit(solution)/shard_map/attention_back/pallas_call | solution.py:222
  212.3 17.4 %attention_back.3 = (bf16[3,1024,384]{2,1,0:T(8,128)(2,1)}, bf16[9,384,128]{2,1,0:T(8,128)(2,1)}, bf16[9,384,128]{2,1,0:T(8,128)(2,1)}) custom-call(s32[1]{0:T(128)} %bitcast.2.core_ref, bf16[1024,768]{1,0:T(8,128)(2,1)} %get-tuple-element.141.q_ref, bf16[1024,768]{1,0:T(8,128)(2,1)} %get-tuple-element.142.k_ref, ...), custom_call_target="tpu_custom_call" | custom-call | flops 1000000 | bytes 100000 | tf_op jit(solution)/shard_map/attention_back/pallas_call | solution.py:222
  234.5 6.0 %layer_output.1 = bf16[1024,768]{1,0:T(8,128)(2,1)} custom-call(s32[1024,128]{1,0:T(8,128)} %get-tuple-element.144.wide_ref, bf16[1024,768]{1,0:T(8,128)(2,1)} %bitcast.34, f32[1024,768]{1,0:T(8,128)} %get-tuple-element.151.resid_ref, f32[1024,1]{1,0:T(8,128)} %get-tuple-element.205.gate_ref), custom_call_target="tpu_custom_call" | custom-call | flops 1000000 | bytes 100000 | tf_op jit(solution)/shard_map/layer_output/pallas_call | solution.py:692
  251.4 10.7 %first_back.1 = (f32[1024,768]{1,0:T(8,128)}, f32[2,768]{1,0:T(2,128)}) custom-call(bf16[3,1024,384]{2,1,0:T(8,128)(2,1)} %get-tuple-element.214.left_ref, bf16[3,1024,384]{2,1,0:T(8,128)(2,1)} %get-tuple-element.215.right_ref, bf16[1024,768]{1,0:T(8,128)(2,1)} %tokens_ref.3, bf16[1024,768]{1,0:T(8,128)(2,1)} %get-tuple-element.216.resid_ref, ...), custom_call_target="tpu_custom_call" | custom-call | flops 1000000 | bytes 100000 | tf_op jit(solution)/shard_map/first_back/pallas_call | solution.py:667
  286.5 4.7 %collective-permute-done.19 = f32[4,768]{1,0:T(4,128)S(1)} collective-permute-done((f32[4,768]{1,0:T(4,128)S(1)}, f32[4,768]{1,0:T(4,128)S(1)}, u32[]{:S(2)}, u32[]{:S(2)}) %collective-permute-start.19) | collective-permute-done | bytes 12320 | tf_op jit(solution)/shard_map/ppermute | solution.py:756
  304.5 3.8 %collective-permute-done.26 = f32[4,768]{1,0:T(4,128)S(1)} collective-permute-done((f32[4,768]{1,0:T(4,128)S(1)}, f32[4,768]{1,0:T(4,128)S(1)}, u32[]{:S(2)}, u32[]{:S(2)}) %collective-permute-start.26) | collective-permute-done | bytes 12320 | tf_op jit(solution)/shard_map/ppermute | solution.py:756
  311.8 4.6 %assemble.2 = (f32[768,768]{1,0:T(8,128)}, f32[768,768]{1,0:T(8,128)}, f32[768,768]{1,0:T(8,128)}, f32[768,768]{1,0:T(8,128)}) custom-call(s32[1]{0:T(128)} %bitcast.2.core_ref, bf16[15,384,128]{2,1,0:T(8,128)(2,1)} %bitcast.36, bf16[15,384,128]{2,1,0:T(8,128)(2,1)} %bitcast.45), custom_call_target="tpu_custom_call" | custom-call | flops 1000000 | bytes 100000 | tf_op jit(solution)/shard_map/assemble/pallas_call | solution.py:738
  (151 shorter events, 84.2 us)
Async XLA Ops:
  6.1 47.1 %all-to-all-start = ((bf16[8,128,768]{2,1,0:T(8,128)(2,1)}), bf16[8,128,768]{2,1,0:T(8,128)(2,1)S(1)}, u32[]{:S(2)}, u32[]{:S(2)}) async-start(bf16[8,128,768]{2,1,0:T(8,128)(2,1)} %bitcast.43), calls=%async_computation | async-start | bytes 3145728 | tf_op jit(solution)/shard_map/all_to_all | solution.py:892
  54.4 42.4 %all-to-all-start.1 = ((bf16[8,128,768]{2,1,0:T(8,128)(2,1)}), bf16[8,128,768]{2,1,0:T(8,128)(2,1)S(1)}, u32[]{:S(2)}, u32[]{:S(2)}) async-start(bf16[8,128,768]{2,1,0:T(8,128)(2,1)} %bitcast.44), calls=%async_computation.1 | async-start | bytes 3145728 | tf_op jit(solution)/shard_map/all_to_all | solution.py:892
  124.8 40.8 %all-to-all-start.2 = ((bf16[8,128,768]{2,1,0:T(8,128)(2,1)}), bf16[8,128,768]{2,1,0:T(8,128)(2,1)S(1)}, u32[]{:S(2)}, u32[]{:S(2)}) async-start(bf16[8,128,768]{2,1,0:T(8,128)(2,1)} %bitcast.42), calls=%async_computation.2 | async-start | bytes 3145728 | tf_op jit(solution)/shard_map/all_to_all | solution.py:892
  147.2 9.3 %collective-permute-start.1 = (bf16[2,768,768]{2,1,0:T(8,128)(2,1)}, bf16[2,768,768]{2,1,0:T(8,128)(2,1)}, u32[]{:S(2)}, u32[]{:S(2)}) collective-permute-start(bf16[2,768,768]{2,1,0:T(8,128)(2,1)} %get-tuple-element.169), channel_id=1, source_target_pairs={{0,8},{8,0},{16,24},{24,16},{1,9},{9,1},{17,25},{25,17},{2,10},{10... | collective-permute-start | bytes 7077896 | tf_op jit(solution)/shard_map/ppermute | solution.py:756
  165.6 35.8 %collective-permute-start.2 = (bf16[1,768,768]{2,1,0:T(8,128)(2,1)}, bf16[1,768,768]{2,1,0:T(8,128)(2,1)}, u32[]{:S(2)}, u32[]{:S(2)}) collective-permute-start(bf16[1,768,768]{2,1,0:T(8,128)(2,1)} %bitcast.12), channel_id=1, source_target_pairs={{0,16},{8,24},{16,0},{24,8},{1,17},{9,25},{17,1},{25,9},{2,18},{10... | collective-permute-start | bytes 3538952 | tf_op jit(solution)/shard_map/ppermute | solution.py:756
  167.1 62.7 %all-to-all-start.3 = ((bf16[8,128,768]{2,1,0:T(8,128)(2,1)}), bf16[8,128,768]{2,1,0:T(8,128)(2,1)S(1)}, u32[]{:S(2)}, u32[]{:S(2)}) async-start(bf16[8,128,768]{2,1,0:T(8,128)(2,1)} %bitcast.41), calls=%async_computation.3 | async-start | bytes 3145728 | tf_op jit(solution)/shard_map/all_to_all | solution.py:892
  209.4 20.4 %collective-permute-start.4 = (bf16[2880,128]{1,0:T(8,128)(2,1)}, bf16[2880,128]{1,0:T(8,128)(2,1)S(1)}, u32[]{:S(2)}, u32[]{:S(2)}) collective-permute-start(bf16[2880,128]{1,0:T(8,128)(2,1)} %get-tuple-element.192), channel_id=1, source_target_pairs={{0,1},{1,0},{2,3},{3,2},{4,5},{5,4},{6,7},{7,6},{8,9},{9,8},{10,11... | collective-permute-start | bytes 2211848 | tf_op jit(solution)/shard_map/ppermute | solution.py:756
  211.2 29.3 %collective-permute-start.7 = (bf16[1,768,768]{2,1,0:T(8,128)(2,1)}, bf16[1,768,768]{2,1,0:T(8,128)(2,1)S(1)}, u32[]{:S(2)}, u32[]{:S(2)}) collective-permute-start(bf16[1,768,768]{2,1,0:T(8,128)(2,1)} %bitcast.52), channel_id=1, source_target_pairs={{0,16},{8,24},{16,0},{24,8},{1,17},{9,25},{17,1},{25,9},{2,18},{10... | collective-permute-start | bytes 3538952 | tf_op jit(solution)/shard_map/ppermute | solution.py:756
  229.8 13.6 %collective-permute-start.6 = (bf16[3456,128]{1,0:T(8,128)(2,1)}, bf16[3456,128]{1,0:T(8,128)(2,1)}, u32[]{:S(2)}, u32[]{:S(2)}) collective-permute-start(bf16[3456,128]{1,0:T(8,128)(2,1)} %bitcast.53), channel_id=1, source_target_pairs={{0,8},{8,0},{16,24},{24,16},{1,9},{9,1},{17,25},{25,17},{2,10},{10... | collective-permute-start | bytes 2654216 | tf_op jit(solution)/shard_map/ppermute | solution.py:756
  233.1 10.4 %collective-permute-start.5 = (bf16[1440,128]{1,0:T(8,128)(2,1)}, bf16[1440,128]{1,0:T(8,128)(2,1)S(1)}, u32[]{:S(2)}, u32[]{:S(2)}) collective-permute-start(bf16[1440,128]{1,0:T(8,128)(2,1)} %get-tuple-element.202), channel_id=1, source_target_pairs={{0,2},{1,3},{2,0},{3,1},{4,6},{5,7},{6,4},{7,5},{8,10},{9,11},{10,... | collective-permute-start | bytes 1105928 | tf_op jit(solution)/shard_map/ppermute | solution.py:756
  246.1 16.0 %collective-permute-start.9 = (bf16[1728,128]{1,0:T(8,128)(2,1)}, bf16[1728,128]{1,0:T(8,128)(2,1)S(1)}, u32[]{:S(2)}, u32[]{:S(2)}) collective-permute-start(bf16[1728,128]{1,0:T(8,128)(2,1)} %get-tuple-element.213), channel_id=1, source_target_pairs={{0,16},{8,24},{16,0},{24,8},{1,17},{9,25},{17,1},{25,9},{2,18},{10... | collective-permute-start | bytes 1327112 | tf_op jit(solution)/shard_map/ppermute | solution.py:756
  249.0 13.0 %collective-permute-start.8 = (bf16[720,128]{1,0:T(8,128)(2,1)}, bf16[720,128]{1,0:T(8,128)(2,1)S(1)}, u32[]{:S(2)}, u32[]{:S(2)}) collective-permute-start(bf16[720,128]{1,0:T(8,128)(2,1)} %get-tuple-element.210), channel_id=1, source_target_pairs={{0,4},{1,5},{2,6},{3,7},{4,0},{5,1},{6,2},{7,3},{8,12},{9,13},{10,... | collective-permute-start | bytes 552968 | tf_op jit(solution)/shard_map/ppermute | solution.py:756
  265.0 7.1 %collective-permute-start.11 = (bf16[864,128]{1,0:T(8,128)(2,1)}, bf16[864,128]{1,0:T(8,128)(2,1)S(1)}, u32[]{:S(2)}, u32[]{:S(2)}) collective-permute-start(bf16[864,128]{1,0:T(8,128)(2,1)} %get-tuple-element.225), channel_id=1, source_target_pairs={{0,2},{1,3},{2,0},{3,1},{4,6},{5,7},{6,4},{7,5},{8,10},{9,11},{10,... | collective-permute-start | bytes 663560 | tf_op jit(solution)/shard_map/ppermute | solution.py:756
  272.2 9.2 %collective-permute-start.13 = (bf16[720,128]{1,0:T(8,128)(2,1)S(1)}, bf16[720,128]{1,0:T(8,128)(2,1)S(1)}, u32[]{:S(2)}, u32[]{:S(2)}) collective-permute-start(bf16[720,128]{1,0:T(8,128)(2,1)S(1)} %add_convert_fusion), channel_id=1, source_target_pairs={{0,4},{1,5},{2,6},{3,7},{4,0},{5,1},{6,2},{7,3},{8,12},{9,13},{10,... | collective-permute-start | bytes 552968 | tf_op jit(solution)/shard_map/ppermute | solution.py:756
  281.4 11.8 %collective-permute-start.16 = (bf16[1440,128]{1,0:T(8,128)(2,1)S(1)}, bf16[1440,128]{1,0:T(8,128)(2,1)S(1)}, u32[]{:S(2)}, u32[]{:S(2)}) collective-permute-start(bf16[1440,128]{1,0:T(8,128)(2,1)S(1)} %pad_maximum_fusion.6), channel_id=1, source_target_pairs={{0,2},{1,3},{2,0},{3,1},{4,6},{5,7},{6,4},{7,5},{8,10},{9,11},{10,... | collective-permute-start | bytes 1105928 | tf_op jit(solution)/shard_map/ppermute | solution.py:756
  281.5 11.7 %collective-permute-start.17 = (bf16[1440,128]{1,0:T(8,128)(2,1)S(1)}, bf16[1440,128]{1,0:T(8,128)(2,1)S(1)}, u32[]{:S(2)}, u32[]{:S(2)}) collective-permute-start(bf16[1440,128]{1,0:T(8,128)(2,1)S(1)} %pad_maximum_fusion.6), channel_id=1, source_target_pairs={{0,1},{1,0},{2,3},{3,2},{4,5},{5,4},{6,7},{7,6},{8,9},{9,8},{10,11... | collective-permute-start | bytes 1105928 | tf_op jit(solution)/shard_map/ppermute | solution.py:756
  282.2 9.0 %collective-permute-start.18 = (bf16[432,128]{1,0:T(8,128)(2,1)S(1)}, bf16[432,128]{1,0:T(8,128)(2,1)S(1)}, u32[]{:S(2)}, u32[]{:S(2)}) collective-permute-start(bf16[432,128]{1,0:T(8,128)(2,1)S(1)} %add_convert_fusion.3), channel_id=1, source_target_pairs={{0,4},{1,5},{2,6},{3,7},{4,0},{5,1},{6,2},{7,3},{8,12},{9,13},{10,... | collective-permute-start | bytes 331784 | tf_op jit(solution)/shard_map/ppermute | solution.py:756
  284.0 7.2 %collective-permute-start.19 = (f32[4,768]{1,0:T(4,128)S(1)}, f32[4,768]{1,0:T(4,128)S(1)}, u32[]{:S(2)}, u32[]{:S(2)}) collective-permute-start(f32[4,768]{1,0:T(4,128)S(1)} %add.78), channel_id=1, source_target_pairs={{0,1},{1,0},{2,3},{3,2},{4,5},{5,4},{6,7},{7,6},{8,9},{9,8},{10,11... | collective-permute-start | bytes 36872 | tf_op jit(solution)/shard_map/ppermute | solution.py:756
  293.3 7.6 %collective-permute-start.20 = (bf16[720,128]{1,0:T(8,128)(2,1)S(1)}, bf16[720,128]{1,0:T(8,128)(2,1)S(1)}, u32[]{:S(2)}, u32[]{:S(2)}) collective-permute-start(bf16[720,128]{1,0:T(8,128)(2,1)S(1)} %slice.34), channel_id=1, source_target_pairs={{0,1},{1,0},{2,3},{3,2},{4,5},{5,4},{6,7},{7,6},{8,9},{9,8},{10,11... | collective-permute-start | bytes 552968 | tf_op jit(solution)/shard_map/ppermute | solution.py:756
  293.9 7.0 %collective-permute-start.21 = (bf16[720,128]{1,0:T(8,128)(2,1)S(1)}, bf16[720,128]{1,0:T(8,128)(2,1)S(1)}, u32[]{:S(2)}, u32[]{:S(2)}) collective-permute-start(bf16[720,128]{1,0:T(8,128)(2,1)S(1)} %slice.35), channel_id=1, source_target_pairs={{0,2},{1,3},{2,0},{3,1},{4,6},{5,7},{6,4},{7,5},{8,10},{9,11},{10,... | collective-permute-start | bytes 552968 | tf_op jit(solution)/shard_map/ppermute | solution.py:756
  301.4 9.2 %collective-permute-start.27 = (bf16[5760,128]{1,0:T(8,128)(2,1)S(1)}, bf16[5760,128]{1,0:T(8,128)(2,1)S(1)}, u32[]{:S(2)}, u32[]{:S(2)}) collective-permute-start(bf16[5760,128]{1,0:T(8,128)(2,1)S(1)} %pad_maximum_fusion), channel_id=1, source_target_pairs={{0,8},{8,0},{16,24},{24,16},{1,9},{9,1},{17,25},{25,17},{2,10},{10... | collective-permute-start | bytes 4423688 | tf_op jit(solution)/shard_map/ppermute | solution.py:756
  302.4 8.3 %collective-permute-start.24 = (bf16[864,128]{1,0:T(8,128)(2,1)}, bf16[864,128]{1,0:T(8,128)(2,1)}, u32[]{:S(2)}, u32[]{:S(2)}) collective-permute-start(bf16[864,128]{1,0:T(8,128)(2,1)} %pad_maximum_fusion.7), channel_id=1, source_target_pairs={{0,2},{1,3},{2,0},{3,1},{4,6},{5,7},{6,4},{7,5},{8,10},{9,11},{10,... | collective-permute-start | bytes 663560 | tf_op jit(solution)/shard_map/ppermute | solution.py:756
  302.7 8.0 %collective-permute-start.25 = (bf16[864,128]{1,0:T(8,128)(2,1)}, bf16[864,128]{1,0:T(8,128)(2,1)S(1)}, u32[]{:S(2)}, u32[]{:S(2)}) collective-permute-start(bf16[864,128]{1,0:T(8,128)(2,1)} %pad_maximum_fusion.7), channel_id=1, source_target_pairs={{0,16},{8,24},{16,0},{24,8},{1,17},{9,25},{17,1},{25,9},{2,18},{10... | collective-permute-start | bytes 663560 | tf_op jit(solution)/shard_map/ppermute | solution.py:756
  310.7 7.2 %collective-permute-start.28 = (bf16[864,128]{1,0:T(8,128)(2,1)}, bf16[864,128]{1,0:T(8,128)(2,1)}, u32[]{:S(2)}, u32[]{:S(2)}) collective-permute-start(bf16[864,128]{1,0:T(8,128)(2,1)} %collective-permute-done.24), channel_id=1, source_target_pairs={{0,16},{8,24},{16,0},{24,8},{1,17},{9,25},{17,1},{25,9},{2,18},{10... | collective-permute-start | bytes 663560 | tf_op jit(solution)/shard_map/ppermute | solution.py:756
  (34 other events, 180.4 us)

commit v6 on v5

--- a/solution.py
+++ b/solution.py
@@ -80,9 +80,17 @@
     queries = q_ref[...] * head_mask(parity, HEAD**-0.5)
     values = jnp.transpose(v_ref[...] * head_mask(parity, 1.0))
     outs = []
+
+    def product(index):
+        finish = (index + 1) * block
+        return contract(k_ref[:finish, :], queries[index * block : finish], 1, 1)
+
+    ready = product(0)
     for index, probs_ref in enumerate(probs_refs):
         first, finish = index * block, (index + 1) * block
-        scores = contract(k_ref[:finish, :], queries[first:finish], 1, 1)
+        scores = ready
+        if index + 1 < len(probs_refs):
+            ready = product(index + 1)
         rows = pl.ds(pl.multiple_of(parity * (length // 2) + index * part, part), part)
         made_ref[rows, :] = contract(normed_ref[rows, :], weights, 1, 0).astype(BF16)
         diagonal = scores[first:] + bias_ref[...]
@@ -153,12 +161,20 @@
     dk_sum[...] = jnp.zeros_like(dk_sum)
     dv_sum[...] = jnp.zeros_like(dv_sum)
     dq_parts = []
+
+    def product(index):
+        finish = (index + 1) * block
+        return contract(v_ref[:finish, :], grads[index * block : finish], 1, 1)
+
+    ready = product(0)
     for index, probs_ref in enumerate(probs_refs):
         first, finish = index * block, (index + 1) * block
         probs = probs_ref[0]
         some = grads[first:finish]
         dv_sum[:finish, :] += contract(probs, some, 1, 0)
-        grad_probs = contract(v_ref[:finish, :], some, 1, 1)
+        grad_probs = ready
+        if index + 1 < len(probs_refs):
+            ready = product(index + 1)
         shares = some.astype(F32) * o_ref[first:finish, :].astype(F32)
         delta = jnp.sum(jnp.transpose(shares), axis=0, keepdims=True)
         grad_scores = (probs.astype(F32) * (grad_probs - delta)).astype(BF16)

time: 327 us -> 322 us (0.985)
  Pallas kernels: 203 us -> 198 us
  waiting for transfers between devices: 55.7 us -> 52.3 us
  starting transfers between devices: 46.2 us -> 49.5 us
    ppermute x30, waiting for transfers between devices: 34.7 us -> 31.3 us  [swap(): return lax.ppermute(value, axis, [(i, i ^ bit) for i in range(size)])]
    ppermute x30, starting transfers between devices: 25.3 us -> 28.6 us  [swap(): return lax.ppermute(value, axis, [(i, i ^ bit) for i in range(size)])]
  transfers between devices with their start and end apart: 34 -> 34, of which waited for: 17 -> 16; matrix products, arithmetic and copies ran while one was open for 3% -> 4% of each run, Pallas kernels for 50% -> 49%
where the time goes in v6:
time: 322 us; the launch traced here: 320 us
  Pallas kernels  198 us (61%)
  waiting for transfers between devices  52.3 us (16%)
  starting transfers between devices  49.5 us (15%)
  local copies, waits for them, and re-layouts  9.74 us (3%)
  other arithmetic  9.32 us (3%)
    pallas_call x2, Pallas kernels, attention_back(): pl.pallas_call(functools.partial(attention_back_kernel, block=block, bloc...  32.4 us
    ppermute x30, waiting for transfers between devices, swap(): return lax.ppermute(value, axis, [(i, i ^ bit) for i in range(size)])  31.3 us
    ppermute x30, starting transfers between devices, swap(): return lax.ppermute(value, axis, [(i, i ^ bit) for i in range(size)])  28.6 us
    pallas_call x1, Pallas kernels, attention(): pl.pallas_call(functools.partial(attention_kernel, block=block), grid=(pa...  27.6 us
    pallas_call x1, Pallas kernels, expert(): pl.pallas_call(expert_kernel, grid=(hidden // tile,), in_specs=[whole, wh...  26.8 us
    pallas_call x8, Pallas kernels, add_split(): pl.pallas_call(add_split_kernel, grid_spec=pltpu.PrefetchScalarGridSpec(n...  23 us
    all_to_all x4, waiting for transfers between devices, exchange(): lax.all_to_all(rows, 'expert', split_axis=0, concat_axis=0, tiled=True)  21.1 us
    all_to_all x4, starting transfers between devices, exchange(): lax.all_to_all(rows, 'expert', split_axis=0, concat_axis=0, tiled=True)  20.9 us
  transfers between devices with their start and end apart: 34, of which 16 were waited for; matrix products, arithmetic and copies ran while one was open for 4% of the time, Pallas kernels for 49%

profile of v6, /device:TPU:0, one launch (start us, length us, event | category | flops | bytes accessed | tf_op | source)
XLA Modules:
  0.0 320.4 jit_solution(13404631772712902947)
XLA Ops:
  0.6 5.4 %route.1 = (bf16[1024,768]{1,0:T(8,128)(2,1)}, s32[1,1024]{1,0:T(1,128)}, s32[1024,128]{1,0:T(8,128)}) custom-call(s32[1,1024]{1,0:T(1,128)} %bitcast.51, bf16[1024,768]{1,0:T(8,128)(2,1)} %cot_ref.3), custom_call_target="tpu_custom_call" | custom-call | flops 1000000 | bytes 100000 | tf_op jit(solution)/shard_map/route/pallas_call | solution.py:464
  6.1 7.5 %all-to-all-start = ((bf16[8,128,768]{2,1,0:T(8,128)(2,1)}), bf16[8,128,768]{2,1,0:T(8,128)(2,1)S(1)}, u32[]{:S(2)}, u32[]{:S(2)}) async-start(bf16[8,128,768]{2,1,0:T(8,128)(2,1)} %bitcast.43), calls=%async_computation | async-start | bytes 3145728 | tf_op jit(solution)/shard_map/all_to_all | solution.py:908
  14.3 27.6 %attention.1 = (bf16[1024,768]{1,0:T(8,128)(2,1)}, bf16[1024,768]{1,0:T(8,128)(2,1)}, bf16[1024,768]{1,0:T(8,128)(2,1)}, bf16[1024,768]{1,0:T(8,128)(2,1)}, bf16...) custom-call(bf16[1024,768]{1,0:T(8,128)(2,1)} %tokens_ref.3, ...), custom_call_target="tpu_custom_call" | custom-call | flops 1000000 | bytes 100000 | tf_op jit(solution)/shard_map/attention/pallas_call | solution.py:127
  41.8 8.9 %branch.1 = (f32[1024,768]{1,0:T(8,128)}, bf16[1024,768]{1,0:T(8,128)(2,1)}) custom-call(bf16[1024,768]{1,0:T(8,128)(2,1)} %get-tuple-element.145.mixed_ref.o_ref, bf16[1024,768]{1,0:T(8,128)(2,1)} %tokens_ref.3, bf16[768,768]{1,0:T(8,128)(2,1)} %weight_ref.3, f32[1,768]{1,0:T(1,128)} %get-tuple-element.287.gain_ref, f32[1,768]{1,0:T(1,128)} %get-tuple-element.286.bias_ref, ...), custom_call_target="tpu_custom_call" | custom-call | flops 1000000 | bytes 100000 | tf_op jit(solution)/shard_map/branch/pallas_call | solution.py:546
  51.9 6.0 %all-to-all-start.1 = ((bf16[8,128,768]{2,1,0:T(8,128)(2,1)}), bf16[8,128,768]{2,1,0:T(8,128)(2,1)S(1)}, u32[]{:S(2)}, u32[]{:S(2)}) async-start(bf16[8,128,768]{2,1,0:T(8,128)(2,1)} %bitcast.44), calls=%async_computation.1 | async-start | bytes 3145728 | tf_op jit(solution)/shard_map/all_to_all | solution.py:908
  58.9 7.8 %settle.1 = (bf16[768,1024]{1,0:T(8,128)(2,1)}, bf16[768,1024]{1,0:T(8,128)(2,1)}, bf16[1024,768]{1,0:T(8,128)(2,1)}, f32[1024,1]{1,0:T(8,128)}, f32[1024,1]{1,0:T(8,128)}) custom-call(bf16[1024,768]{1,0:T(8,128)(2,1)} %tokens_ref.3, f32[1,768]{1,0:T(1,128)} %get-tuple-element.289.gain_ref.first_gain_ref, ...), custom_call_target="tpu_custom_call" | custom-call | flops 1000000 | bytes 100000 | tf_op jit(solution)/shard_map/settle/pallas_call | solution.py:507
  68.0 9.9 %expert_cots.1.cd_ref = bf16[1024,3072]{1,0:T(8,128)(2,1)} custom-call(bf16[1024,768]{1,0:T(8,128)(2,1)} %bitcast.30, bf16[1,3072,768]{2,1,0:T(8,128)(2,1)} %down_ref.3), custom_call_target="tpu_custom_call" | custom-call | flops 1000000 | bytes 100000 | tf_op jit(solution)/shard_map/expert_cots/pallas_call | solution.py:272
  77.9 16.4 %all-to-all-done.1 = bf16[8,128,768]{2,1,0:T(8,128)(2,1)S(1)} async-done(((bf16[8,128,768]{2,1,0:T(8,128)(2,1)}), bf16[8,128,768]{2,1,0:T(8,128)(2,1)S(1)}, u32[]{:S(2)}, u32[]{:S(2)}) %all-to-all-start.1) | async-done | bytes 1572896 | tf_op jit(solution)/shard_map/all_to_all | solution.py:908
  95.4 26.8 %expert.1 = (bf16[1024,768]{1,0:T(8,128)(2,1)}, bf16[1024,768]{1,0:T(8,128)(2,1)}, bf16[1024,768]{1,0:T(8,128)(2,1)}, bf16[1024,3072]{1,0:T(8,128)(2,1)}, bf16[1024,3072]{1,0:T(8,128)(2,1)}) custom-call(bf16[1024,768]{1,0:T(8,128)(2,1)} %bitcast.32, bf16[1024,768]{1,0:T(8,128)(2,1)} %bitcast.31, bf16[1024,3072]{1,0:T(8,128)(2,1)} %expert_cots.1.cd_ref, ...), custom_call_target="tpu_custom_call" | custom-call | flops 1000000 | bytes 100000 | tf_op jit(solution)/shard_map/expert/pallas_call | solution.py:331
  122.2 3.6 %all-to-all-start.2 = ((bf16[8,128,768]{2,1,0:T(8,128)(2,1)}), bf16[8,128,768]{2,1,0:T(8,128)(2,1)S(1)}, u32[]{:S(2)}, u32[]{:S(2)}) async-start(bf16[8,128,768]{2,1,0:T(8,128)(2,1)} %bitcast.42), calls=%async_computation.2 | async-start | bytes 3145728 | tf_op jit(solution)/shard_map/all_to_all | solution.py:908
  125.9 18.8 %expert_weights.1 = (bf16[2,768,768]{2,1,0:T(8,128)(2,1)}, bf16[2,768,768]{2,1,0:T(8,128)(2,1)}, bf16[2,768,768]{2,1,0:T(8,128)(2,1)}, bf16[2,768,768]{2,1,0:T(8,128)(2,1)}) custom-call(s32[1]{0:T(128)} %bitcast.2.core_ref, bf16[1024,768]{1,0:T(8,128)(2,1)} %bitcast.33, bf16[1024,768]{1,0:T(8,128)(2,1)} %get-tuple-element.161.dy_ref, ...), custom_call_target="tpu_custom_call" | custom-call | flops 1000000 | bytes 100000 | tf_op jit(solution)/shard_map/expert_weights/pallas_call | solution.py:409
  145.2 4.4 %collective-permute-done = bf16[2,768,768]{2,1,0:T(8,128)(2,1)} collective-permute-done((bf16[2,768,768]{2,1,0:T(8,128)(2,1)}, bf16[2,768,768]{2,1,0:T(8,128)(2,1)}, u32[]{:S(2)}, u32[]{:S(2)}) %collective-permute-start) | collective-permute-done | bytes 2359328 | tf_op jit(solution)/shard_map/ppermute | solution.py:772
  149.6 4.4 %add_split.8 = (bf16[768,768]{1,0:T(8,128)(2,1)}, bf16[768,768]{1,0:T(8,128)(2,1)}) custom-call(s32[1]{0:T(128)} %bitcast.9.mine_ref, bf16[1536,768]{1,0:T(8,128)(2,1)} %bitcast.40, bf16[1536,768]{1,0:T(8,128)(2,1)} %bitcast.11.right_ref), custom_call_target="tpu_custom_call" | custom-call | flops 1000000 | bytes 100000 | tf_op jit(solution)/shard_map/add_split/pallas_call | solution.py:831
  154.0 4.4 %add_split.9 = (bf16[768,768]{1,0:T(8,128)(2,1)}, bf16[768,768]{1,0:T(8,128)(2,1)}) custom-call(s32[1]{0:T(128)} %bitcast.9.mine_ref, bf16[1536,768]{1,0:T(8,128)(2,1)} %bitcast.39, bf16[1536,768]{1,0:T(8,128)(2,1)} %bitcast.15.right_ref), custom_call_target="tpu_custom_call" | custom-call | flops 1000000 | bytes 100000 | tf_op jit(solution)/shard_map/add_split/pallas_call | solution.py:831
  158.3 4.7 %all-to-all-done.2 = bf16[8,128,768]{2,1,0:T(8,128)(2,1)S(1)} async-done(((bf16[8,128,768]{2,1,0:T(8,128)(2,1)}), bf16[8,128,768]{2,1,0:T(8,128)(2,1)S(1)}, u32[]{:S(2)}, u32[]{:S(2)}) %all-to-all-start.2) | async-done | bytes 1572896 | tf_op jit(solution)/shard_map/all_to_all | solution.py:908
  164.5 3.8 %all-to-all-start.3 = ((bf16[8,128,768]{2,1,0:T(8,128)(2,1)}), bf16[8,128,768]{2,1,0:T(8,128)(2,1)S(1)}, u32[]{:S(2)}, u32[]{:S(2)}) async-start(bf16[8,128,768]{2,1,0:T(8,128)(2,1)} %bitcast.41), calls=%async_computation.3 | async-start | bytes 3145728 | tf_op jit(solution)/shard_map/all_to_all | solution.py:908
  168.3 13.1 %second_back.1 = (bf16[1024,768]{1,0:T(8,128)(2,1)}, bf16[1024,768]{1,0:T(8,128)(2,1)}, f32[2,768]{1,0:T(2,128)}, bf16[15,384,128]{2,1,0:T(8,128)(2,1)}, bf16[15,384,128]{2,1,0:T(8,128)(2,1)}) custom-call(s32[1]{0:T(128)} %bitcast.2.core_ref, s32[1024,128]{1,0:T(8,128)} %get-tuple-element.144.wide_ref, bf16[1024,768]{1,0:T(8,128)(2,1)} %bitcast.35, ...), custom_call_target="tpu_custom_call" | custom-call | flops 1000000 | bytes 100000 | tf_op jit(solution)/shard_map/second_back/pallas_call | solution.py:626
  181.4 16.2 %attention_back.2 = (bf16[3,1024,384]{2,1,0:T(8,128)(2,1)}, bf16[15,384,128]{2,1,0:T(8,128)(2,1)}, bf16[15,384,128]{2,1,0:T(8,128)(2,1)}) custom-call(s32[1]{0:T(128)} %bitcast.2.core_ref, bf16[1024,768]{1,0:T(8,128)(2,1)} %get-tuple-element.141.q_ref, bf16[1024,768]{1,0:T(8,128)(2,1)} %get-tuple-element.142.k_ref, ...), custom_call_target="tpu_custom_call", output_to_operand_aliasing={{1}: (11, {}), {2}: (12, {})} | custom-call | flops 1000000 | bytes 100000 | tf_op jit(solution)/shard_map/attention_back/pallas_call | solution.py:238
  208.6 16.2 %attention_back.3 = (bf16[3,1024,384]{2,1,0:T(8,128)(2,1)}, bf16[9,384,128]{2,1,0:T(8,128)(2,1)}, bf16[9,384,128]{2,1,0:T(8,128)(2,1)}) custom-call(s32[1]{0:T(128)} %bitcast.2.core_ref, bf16[1024,768]{1,0:T(8,128)(2,1)} %get-tuple-element.141.q_ref, bf16[1024,768]{1,0:T(8,128)(2,1)} %get-tuple-element.142.k_ref, ...), custom_call_target="tpu_custom_call" | custom-call | flops 1000000 | bytes 100000 | tf_op jit(solution)/shard_map/attention_back/pallas_call | solution.py:238
  229.6 6.0 %layer_output.1 = bf16[1024,768]{1,0:T(8,128)(2,1)} custom-call(s32[1024,128]{1,0:T(8,128)} %get-tuple-element.144.wide_ref, bf16[1024,768]{1,0:T(8,128)(2,1)} %bitcast.34, f32[1024,768]{1,0:T(8,128)} %get-tuple-element.151.resid_ref, f32[1024,1]{1,0:T(8,128)} %get-tuple-element.205.gate_ref), custom_call_target="tpu_custom_call" | custom-call | flops 1000000 | bytes 100000 | tf_op jit(solution)/shard_map/layer_output/pallas_call | solution.py:708
  246.5 10.7 %first_back.1 = (f32[1024,768]{1,0:T(8,128)}, f32[2,768]{1,0:T(2,128)}) custom-call(bf16[3,1024,384]{2,1,0:T(8,128)(2,1)} %get-tuple-element.214.left_ref, bf16[3,1024,384]{2,1,0:T(8,128)(2,1)} %get-tuple-element.215.right_ref, bf16[1024,768]{1,0:T(8,128)(2,1)} %tokens_ref.3, bf16[1024,768]{1,0:T(8,128)(2,1)} %get-tuple-element.216.resid_ref, ...), custom_call_target="tpu_custom_call" | custom-call | flops 1000000 | bytes 100000 | tf_op jit(solution)/shard_map/first_back/pallas_call | solution.py:683
  282.0 4.1 %collective-permute-done.19 = f32[4,768]{1,0:T(4,128)S(1)} collective-permute-done((f32[4,768]{1,0:T(4,128)S(1)}, f32[4,768]{1,0:T(4,128)S(1)}, u32[]{:S(2)}, u32[]{:S(2)}) %collective-permute-start.19) | collective-permute-done | bytes 12320 | tf_op jit(solution)/shard_map/ppermute | solution.py:772
  300.3 3.5 %collective-permute-done.26 = f32[4,768]{1,0:T(4,128)S(1)} collective-permute-done((f32[4,768]{1,0:T(4,128)S(1)}, f32[4,768]{1,0:T(4,128)S(1)}, u32[]{:S(2)}, u32[]{:S(2)}) %collective-permute-start.26) | collective-permute-done | bytes 12320 | tf_op jit(solution)/shard_map/ppermute | solution.py:772
  306.8 4.6 %assemble.2 = (f32[768,768]{1,0:T(8,128)}, f32[768,768]{1,0:T(8,128)}, f32[768,768]{1,0:T(8,128)}, f32[768,768]{1,0:T(8,128)}) custom-call(s32[1]{0:T(128)} %bitcast.2.core_ref, bf16[15,384,128]{2,1,0:T(8,128)(2,1)} %bitcast.36, bf16[15,384,128]{2,1,0:T(8,128)(2,1)} %bitcast.45), custom_call_target="tpu_custom_call" | custom-call | flops 1000000 | bytes 100000 | tf_op jit(solution)/shard_map/assemble/pallas_call | solution.py:754
  (151 shorter events, 84.6 us)
Async XLA Ops:
  6.1 44.6 %all-to-all-start = ((bf16[8,128,768]{2,1,0:T(8,128)(2,1)}), bf16[8,128,768]{2,1,0:T(8,128)(2,1)S(1)}, u32[]{:S(2)}, u32[]{:S(2)}) async-start(bf16[8,128,768]{2,1,0:T(8,128)(2,1)} %bitcast.43), calls=%async_computation | async-start | bytes 3145728 | tf_op jit(solution)/shard_map/all_to_all | solution.py:908
  51.9 42.4 %all-to-all-start.1 = ((bf16[8,128,768]{2,1,0:T(8,128)(2,1)}), bf16[8,128,768]{2,1,0:T(8,128)(2,1)S(1)}, u32[]{:S(2)}, u32[]{:S(2)}) async-start(bf16[8,128,768]{2,1,0:T(8,128)(2,1)} %bitcast.44), calls=%async_computation.1 | async-start | bytes 3145728 | tf_op jit(solution)/shard_map/all_to_all | solution.py:908
  122.2 40.8 %all-to-all-start.2 = ((bf16[8,128,768]{2,1,0:T(8,128)(2,1)}), bf16[8,128,768]{2,1,0:T(8,128)(2,1)S(1)}, u32[]{:S(2)}, u32[]{:S(2)}) async-start(bf16[8,128,768]{2,1,0:T(8,128)(2,1)} %bitcast.42), calls=%async_computation.2 | async-start | bytes 3145728 | tf_op jit(solution)/shard_map/all_to_all | solution.py:908
  144.7 9.3 %collective-permute-start.1 = (bf16[2,768,768]{2,1,0:T(8,128)(2,1)}, bf16[2,768,768]{2,1,0:T(8,128)(2,1)}, u32[]{:S(2)}, u32[]{:S(2)}) collective-permute-start(bf16[2,768,768]{2,1,0:T(8,128)(2,1)} %get-tuple-element.169), channel_id=1, source_target_pairs={{0,8},{8,0},{16,24},{24,16},{1,9},{9,1},{17,25},{25,17},{2,10},{10... | collective-permute-start | bytes 7077896 | tf_op jit(solution)/shard_map/ppermute | solution.py:772
  163.0 34.6 %collective-permute-start.2 = (bf16[1,768,768]{2,1,0:T(8,128)(2,1)}, bf16[1,768,768]{2,1,0:T(8,128)(2,1)}, u32[]{:S(2)}, u32[]{:S(2)}) collective-permute-start(bf16[1,768,768]{2,1,0:T(8,128)(2,1)} %bitcast.12), channel_id=1, source_target_pairs={{0,16},{8,24},{16,0},{24,8},{1,17},{9,25},{17,1},{25,9},{2,18},{10... | collective-permute-start | bytes 3538952 | tf_op jit(solution)/shard_map/ppermute | solution.py:772
  164.5 60.3 %all-to-all-start.3 = ((bf16[8,128,768]{2,1,0:T(8,128)(2,1)}), bf16[8,128,768]{2,1,0:T(8,128)(2,1)S(1)}, u32[]{:S(2)}, u32[]{:S(2)}) async-start(bf16[8,128,768]{2,1,0:T(8,128)(2,1)} %bitcast.41), calls=%async_computation.3 | async-start | bytes 3145728 | tf_op jit(solution)/shard_map/all_to_all | solution.py:908
  205.6 19.2 %collective-permute-start.4 = (bf16[2880,128]{1,0:T(8,128)(2,1)}, bf16[2880,128]{1,0:T(8,128)(2,1)S(1)}, u32[]{:S(2)}, u32[]{:S(2)}) collective-permute-start(bf16[2880,128]{1,0:T(8,128)(2,1)} %get-tuple-element.192), channel_id=1, source_target_pairs={{0,1},{1,0},{2,3},{3,2},{4,5},{5,4},{6,7},{7,6},{8,9},{9,8},{10,11... | collective-permute-start | bytes 2211848 | tf_op jit(solution)/shard_map/ppermute | solution.py:772
  207.5 28.1 %collective-permute-start.7 = (bf16[1,768,768]{2,1,0:T(8,128)(2,1)}, bf16[1,768,768]{2,1,0:T(8,128)(2,1)S(1)}, u32[]{:S(2)}, u32[]{:S(2)}) collective-permute-start(bf16[1,768,768]{2,1,0:T(8,128)(2,1)} %bitcast.52), channel_id=1, source_target_pairs={{0,16},{8,24},{16,0},{24,8},{1,17},{9,25},{17,1},{25,9},{2,18},{10... | collective-permute-start | bytes 3538952 | tf_op jit(solution)/shard_map/ppermute | solution.py:772
  224.8 13.6 %collective-permute-start.6 = (bf16[3456,128]{1,0:T(8,128)(2,1)}, bf16[3456,128]{1,0:T(8,128)(2,1)}, u32[]{:S(2)}, u32[]{:S(2)}) collective-permute-start(bf16[3456,128]{1,0:T(8,128)(2,1)} %bitcast.53), channel_id=1, source_target_pairs={{0,8},{8,0},{16,24},{24,16},{1,9},{9,1},{17,25},{25,17},{2,10},{10... | collective-permute-start | bytes 2654216 | tf_op jit(solution)/shard_map/ppermute | solution.py:772
  228.1 10.4 %collective-permute-start.5 = (bf16[1440,128]{1,0:T(8,128)(2,1)}, bf16[1440,128]{1,0:T(8,128)(2,1)S(1)}, u32[]{:S(2)}, u32[]{:S(2)}) collective-permute-start(bf16[1440,128]{1,0:T(8,128)(2,1)} %get-tuple-element.202), channel_id=1, source_target_pairs={{0,2},{1,3},{2,0},{3,1},{4,6},{5,7},{6,4},{7,5},{8,10},{9,11},{10,... | collective-permute-start | bytes 1105928 | tf_op jit(solution)/shard_map/ppermute | solution.py:772
  241.2 16.0 %collective-permute-start.9 = (bf16[1728,128]{1,0:T(8,128)(2,1)}, bf16[1728,128]{1,0:T(8,128)(2,1)S(1)}, u32[]{:S(2)}, u32[]{:S(2)}) collective-permute-start(bf16[1728,128]{1,0:T(8,128)(2,1)} %get-tuple-element.213), channel_id=1, source_target_pairs={{0,16},{8,24},{16,0},{24,8},{1,17},{9,25},{17,1},{25,9},{2,18},{10... | collective-permute-start | bytes 1327112 | tf_op jit(solution)/shard_map/ppermute | solution.py:772
  244.1 13.1 %collective-permute-start.8 = (bf16[720,128]{1,0:T(8,128)(2,1)}, bf16[720,128]{1,0:T(8,128)(2,1)S(1)}, u32[]{:S(2)}, u32[]{:S(2)}) collective-permute-start(bf16[720,128]{1,0:T(8,128)(2,1)} %get-tuple-element.210), channel_id=1, source_target_pairs={{0,4},{1,5},{2,6},{3,7},{4,0},{5,1},{6,2},{7,3},{8,12},{9,13},{10,... | collective-permute-start | bytes 552968 | tf_op jit(solution)/shard_map/ppermute | solution.py:772
  260.1 7.1 %collective-permute-start.11 = (bf16[864,128]{1,0:T(8,128)(2,1)}, bf16[864,128]{1,0:T(8,128)(2,1)S(1)}, u32[]{:S(2)}, u32[]{:S(2)}) collective-permute-start(bf16[864,128]{1,0:T(8,128)(2,1)} %get-tuple-element.225), channel_id=1, source_target_pairs={{0,2},{1,3},{2,0},{3,1},{4,6},{5,7},{6,4},{7,5},{8,10},{9,11},{10,... | collective-permute-start | bytes 663560 | tf_op jit(solution)/shard_map/ppermute | solution.py:772
  267.3 9.1 %collective-permute-start.13 = (bf16[720,128]{1,0:T(8,128)(2,1)S(1)}, bf16[720,128]{1,0:T(8,128)(2,1)S(1)}, u32[]{:S(2)}, u32[]{:S(2)}) collective-permute-start(bf16[720,128]{1,0:T(8,128)(2,1)S(1)} %add_convert_fusion), channel_id=1, source_target_pairs={{0,4},{1,5},{2,6},{3,7},{4,0},{5,1},{6,2},{7,3},{8,12},{9,13},{10,... | collective-permute-start | bytes 552968 | tf_op jit(solution)/shard_map/ppermute | solution.py:772
  276.5 11.7 %collective-permute-start.16 = (bf16[1440,128]{1,0:T(8,128)(2,1)S(1)}, bf16[1440,128]{1,0:T(8,128)(2,1)S(1)}, u32[]{:S(2)}, u32[]{:S(2)}) collective-permute-start(bf16[1440,128]{1,0:T(8,128)(2,1)S(1)} %pad_maximum_fusion.6), channel_id=1, source_target_pairs={{0,2},{1,3},{2,0},{3,1},{4,6},{5,7},{6,4},{7,5},{8,10},{9,11},{10,... | collective-permute-start | bytes 1105928 | tf_op jit(solution)/shard_map/ppermute | solution.py:772
  276.5 11.6 %collective-permute-start.17 = (bf16[1440,128]{1,0:T(8,128)(2,1)S(1)}, bf16[1440,128]{1,0:T(8,128)(2,1)S(1)}, u32[]{:S(2)}, u32[]{:S(2)}) collective-permute-start(bf16[1440,128]{1,0:T(8,128)(2,1)S(1)} %pad_maximum_fusion.6), channel_id=1, source_target_pairs={{0,1},{1,0},{2,3},{3,2},{4,5},{5,4},{6,7},{7,6},{8,9},{9,8},{10,11... | collective-permute-start | bytes 1105928 | tf_op jit(solution)/shard_map/ppermute | solution.py:772
  277.9 8.2 %collective-permute-start.18 = (bf16[432,128]{1,0:T(8,128)(2,1)S(1)}, bf16[432,128]{1,0:T(8,128)(2,1)S(1)}, u32[]{:S(2)}, u32[]{:S(2)}) collective-permute-start(bf16[432,128]{1,0:T(8,128)(2,1)S(1)} %add_convert_fusion.3), channel_id=1, source_target_pairs={{0,4},{1,5},{2,6},{3,7},{4,0},{5,1},{6,2},{7,3},{8,12},{9,13},{10,... | collective-permute-start | bytes 331784 | tf_op jit(solution)/shard_map/ppermute | solution.py:772
  279.3 6.8 %collective-permute-start.19 = (f32[4,768]{1,0:T(4,128)S(1)}, f32[4,768]{1,0:T(4,128)S(1)}, u32[]{:S(2)}, u32[]{:S(2)}) collective-permute-start(f32[4,768]{1,0:T(4,128)S(1)} %add.78), channel_id=1, source_target_pairs={{0,1},{1,0},{2,3},{3,2},{4,5},{5,4},{6,7},{7,6},{8,9},{9,8},{10,11... | collective-permute-start | bytes 36872 | tf_op jit(solution)/shard_map/ppermute | solution.py:772
  288.2 7.1 %collective-permute-start.20 = (bf16[720,128]{1,0:T(8,128)(2,1)S(1)}, bf16[720,128]{1,0:T(8,128)(2,1)S(1)}, u32[]{:S(2)}, u32[]{:S(2)}) collective-permute-start(bf16[720,128]{1,0:T(8,128)(2,1)S(1)} %slice.34), channel_id=1, source_target_pairs={{0,1},{1,0},{2,3},{3,2},{4,5},{5,4},{6,7},{7,6},{8,9},{9,8},{10,11... | collective-permute-start | bytes 552968 | tf_op jit(solution)/shard_map/ppermute | solution.py:772
  289.4 5.9 %collective-permute-start.21 = (bf16[720,128]{1,0:T(8,128)(2,1)S(1)}, bf16[720,128]{1,0:T(8,128)(2,1)S(1)}, u32[]{:S(2)}, u32[]{:S(2)}) collective-permute-start(bf16[720,128]{1,0:T(8,128)(2,1)S(1)} %slice.35), channel_id=1, source_target_pairs={{0,2},{1,3},{2,0},{3,1},{4,6},{5,7},{6,4},{7,5},{8,10},{9,11},{10,... | collective-permute-start | bytes 552968 | tf_op jit(solution)/shard_map/ppermute | solution.py:772
  295.8 9.6 %collective-permute-start.27 = (bf16[5760,128]{1,0:T(8,128)(2,1)S(1)}, bf16[5760,128]{1,0:T(8,128)(2,1)S(1)}, u32[]{:S(2)}, u32[]{:S(2)}) collective-permute-start(bf16[5760,128]{1,0:T(8,128)(2,1)S(1)} %pad_maximum_fusion), channel_id=1, source_target_pairs={{0,8},{8,0},{16,24},{24,16},{1,9},{9,1},{17,25},{25,17},{2,10},{10... | collective-permute-start | bytes 4423688 | tf_op jit(solution)/shard_map/ppermute | solution.py:772
  296.8 8.3 %collective-permute-start.24 = (bf16[864,128]{1,0:T(8,128)(2,1)}, bf16[864,128]{1,0:T(8,128)(2,1)}, u32[]{:S(2)}, u32[]{:S(2)}) collective-permute-start(bf16[864,128]{1,0:T(8,128)(2,1)} %pad_maximum_fusion.7), channel_id=1, source_target_pairs={{0,2},{1,3},{2,0},{3,1},{4,6},{5,7},{6,4},{7,5},{8,10},{9,11},{10,... | collective-permute-start | bytes 663560 | tf_op jit(solution)/shard_map/ppermute | solution.py:772
  297.8 7.6 %collective-permute-start.25 = (bf16[864,128]{1,0:T(8,128)(2,1)}, bf16[864,128]{1,0:T(8,128)(2,1)S(1)}, u32[]{:S(2)}, u32[]{:S(2)}) collective-permute-start(bf16[864,128]{1,0:T(8,128)(2,1)} %pad_maximum_fusion.7), channel_id=1, source_target_pairs={{0,16},{8,24},{16,0},{24,8},{1,17},{9,25},{17,1},{25,9},{2,18},{10... | collective-permute-start | bytes 663560 | tf_op jit(solution)/shard_map/ppermute | solution.py:772
  305.4 7.0 %collective-permute-start.28 = (bf16[864,128]{1,0:T(8,128)(2,1)}, bf16[864,128]{1,0:T(8,128)(2,1)}, u32[]{:S(2)}, u32[]{:S(2)}) collective-permute-start(bf16[864,128]{1,0:T(8,128)(2,1)} %collective-permute-done.24), channel_id=1, source_target_pairs={{0,16},{8,24},{16,0},{24,8},{1,17},{9,25},{17,1},{25,9},{2,18},{10... | collective-permute-start | bytes 663560 | tf_op jit(solution)/shard_map/ppermute | solution.py:772
  (34 other events, 181.9 us)
